TPU v7x, 32 devices: a whole 2x2x4 slice. The times are simulated.
32 devices in a mesh: fsdp: 8 (over y, x, core), dp: 4 (over z).
Axes of the slice: x: 2, y: 2, z: 4, core: 2. Of those that a mesh axis runs over, the one named last changes fastest.
Arguments:
- inputs: bfloat16 [2, 32, 512, 1024], P(None, ('fsdp', 'dp')), may hold values from -6 to 6
- block_ids: int32 [2, 32, 512], P(None, ('fsdp', 'dp')), may hold values from 0 to 3, never falling along the last dimension, each value on 1 to 256 neighbouring positions
- routes: int32 [2, 32, 512, 8], P(None, ('fsdp', 'dp')), may hold values from 0 to 31, all different within a row; in each aligned block of 512 rows (0 to 511, 512 to 1023, ..., all dimensions but the last counted through in order) at most 144 rows name the same one
- out_grad: bfloat16 [2, 32, 512, 1024], P(None, ('fsdp', 'dp')), may hold values from -6 to 6
- norm_gain: bfloat16 [1024], P(('fsdp', 'dp')), may hold values from 0.5 to 1.5
- w_query: bfloat16 [1024, 1024], P(('fsdp', 'dp')), may hold values from -0.75 to 0.75
- key_weight: bfloat16 [1024, 512], P(('fsdp', 'dp')), may hold values from -0.75 to 0.75
- value_weight: bfloat16 [1024, 512], P(('fsdp', 'dp')), may hold values from -0.1875 to 0.1875
- w_output: bfloat16 [1024, 1024], P(('fsdp', 'dp')), may hold values from -2 to 2
- moe_gain: bfloat16 [1024], P(('fsdp', 'dp')), may hold values from 0.5 to 1.5
- w_router: bfloat16 [1024, 32], P(('fsdp', 'dp')), may hold values from -0.09375 to 0.09375
- w_gate: bfloat16 [32, 1024, 512], P('fsdp', 'dp'), may hold values from -0.1875 to 0.1875
- w_up: bfloat16 [32, 1024, 512], P('fsdp', 'dp'), may hold values from -0.1875 to 0.1875
- w_down: bfloat16 [32, 512, 1024], P('fsdp', 'dp'), may hold values from -4 to 4
Outputs:
- output: bfloat16 [2, 32, 512, 1024], P(None, ('fsdp', 'dp'))
- input_grad: float32 [2, 32, 512, 1024], P(None, ('fsdp', 'dp'))
- grad_norm_gain: float32 [1024], P(('fsdp', 'dp'))
- grad_w_query: float32 [1024, 1024], P(('fsdp', 'dp'))
- grad_w_key: float32 [1024, 512], P(('fsdp', 'dp'))
- grad_w_value: float32 [1024, 512], P(('fsdp', 'dp'))
- grad_w_output: float32 [1024, 1024], P(('fsdp', 'dp'))
- grad_moe_gain: float32 [1024], P(('fsdp', 'dp'))
- grad_w_router: float32 [1024, 32], P(('fsdp', 'dp'))
- grad_w_gate: float32 [32, 1024, 512], P('fsdp', 'dp')
- grad_w_up: float32 [32, 1024, 512], P('fsdp', 'dp')
- grad_w_down: float32 [32, 512, 1024], P('fsdp', 'dp')
Inputs may be any that keep to these rules, and one draw needn't show every extreme that they name: `block_ids`: along each sequence the ids never fall; a run of equal ids holds 1 to 256 tokens. `routes`: each token names 8 different experts. Among the 512 tokens of one sequence no expert is named more than 144 times, and in every draw some expert is named exactly 144 times in some sequence.
All inputs are finite; a program needn't handle non-finite values.
Results may differ from a plain program's by a relative error of at most 0.017.
Values may be sent and summed in bfloat16 or wider, within the bound.
A program may use at most 320 MiB of HBM per device.

v0:
```python
import jax
import jax.numpy as jnp
from jax import lax
from jax.sharding import PartitionSpec as P

QUERY_HEADS = 16
KEY_VALUE_HEADS = 8
HEAD_SIZE = 64
CAP = 144


EPS = 1e-06
RESIDUAL_SCALE = 0.22
SCORE_SCALE = 0.015625
THETA = 10000.0
NEG_FILL = -1e30


def rope_tables(sequence_length, head_dim):
    half_dim = head_dim // 2
    inverse_freq = THETA ** (-(jnp.arange(half_dim, dtype=jnp.float32) * 2.0) / head_dim)
    angles = jnp.arange(sequence_length, dtype=jnp.float32)[:, None] * inverse_freq[None, :]
    cosine_table = jnp.concatenate([jnp.cos(angles), jnp.cos(angles)], axis=1)
    sine_table = jnp.concatenate([jnp.sin(angles), jnp.sin(angles)], axis=1)
    return (cosine_table[:, None, :], sine_table[:, None, :])


def apply_rotary(stack, cosine_table, sine_table):
    half_dim = stack.shape[-1] // 2
    turned = jnp.concatenate([-stack[..., half_dim:], stack[..., :half_dim]], axis=-1)
    return stack * cosine_table + turned * sine_table


def rotate_back(grad_stack, cosine_table, sine_table):
    half_dim = grad_stack.shape[-1] // 2
    scaled = grad_stack * sine_table
    turned = jnp.concatenate([scaled[..., half_dim:], -scaled[..., :half_dim]], axis=-1)
    return grad_stack * cosine_table + turned


def rms_scale(rows, gain):
    return rows * lax.rsqrt(jnp.mean(rows * rows, axis=-1, keepdims=True) + EPS) * gain


def route_gates(logits, picks):
    chosen = jnp.take_along_axis(logits, picks, axis=1)
    lifted = jnp.exp(chosen - jnp.max(chosen, axis=1, keepdims=True))
    return lifted / jnp.sum(lifted, axis=1, keepdims=True)


def slot_layout(picks, experts, capacity):
    flat = picks.reshape(-1)
    onehot = (flat[:, None] == jnp.arange(experts, dtype=jnp.int32)[None, :]).astype(jnp.int32)
    before = jnp.cumsum(onehot, axis=0) - onehot
    rank = jnp.sum(before * onehot, axis=1)
    slot = flat * capacity + rank
    route_of = (
        jnp.zeros((experts * capacity,), jnp.int32)
        .at[slot]
        .set(jnp.arange(flat.shape[0], dtype=jnp.int32))
    )
    filled = jnp.zeros((experts * capacity,), jnp.int32).at[slot].set(jnp.ones_like(slot))
    return (slot, route_of, filled)


def attend(query_group, key_group, value_group, visible):
    sequence_length = query_group.shape[0]
    split = query_group.reshape(sequence_length, -1, key_group.shape[1])
    scores = SCORE_SCALE * jnp.einsum(
        "sgd,td->gst", split, key_group, preferred_element_type=jnp.float32
    )
    scores = jnp.where(visible[None], scores, NEG_FILL)
    highest = jnp.max(scores, axis=2, keepdims=True)
    lifted = jnp.exp(scores - highest)
    total = jnp.sum(lifted, axis=2, keepdims=True)
    weights_low = (lifted / total).astype(jnp.bfloat16)
    mixed = jnp.einsum("gst,td->sgd", weights_low, value_group, preferred_element_type=jnp.float32)
    return (mixed.reshape(sequence_length, -1), (highest + jnp.log(total))[:, :, 0])


def attend_back(query_group, key_group, value_group, grad_group, log_total, visible):
    sequence_length = query_group.shape[0]
    head_dim = key_group.shape[1]
    split = query_group.reshape(sequence_length, -1, head_dim)
    grad_split = grad_group.reshape(sequence_length, -1, head_dim)
    scores = SCORE_SCALE * jnp.einsum(
        "sgd,td->gst", split, key_group, preferred_element_type=jnp.float32
    )
    scores = jnp.where(visible[None], scores, NEG_FILL)
    weights = jnp.exp(scores - log_total[:, :, None])
    weight_grad = jnp.einsum(
        "sgd,td->gst", grad_split, value_group, preferred_element_type=jnp.float32
    )
    value_gradient = jnp.einsum(
        "gst,sgd->td", weights.astype(jnp.bfloat16), grad_split, preferred_element_type=jnp.float32
    )
    row_dot = jnp.sum(weights * weight_grad, axis=2, keepdims=True)
    score_grad = (weights * (weight_grad - row_dot)).astype(jnp.bfloat16)
    query_grad = SCORE_SCALE * jnp.einsum(
        "gst,td->sgd", score_grad, key_group, preferred_element_type=jnp.float32
    )
    key_grad = SCORE_SCALE * jnp.einsum(
        "gst,sgd->td", score_grad, split, preferred_element_type=jnp.float32
    )
    return (query_grad.reshape(sequence_length, -1), key_grad, value_gradient)


def swish_parts(pre_gate):
    logistic = jax.nn.sigmoid(pre_gate)
    return (logistic, pre_gate * logistic)


def expert_apply(rows_in, gate_w, up_w, down_w, lead):
    pre_gate = jnp.einsum(
        lead + "cd,edf->" + lead + "cf", rows_in, gate_w, preferred_element_type=jnp.float32
    )
    pre_up = jnp.einsum(
        lead + "cd,edf->" + lead + "cf", rows_in, up_w, preferred_element_type=jnp.float32
    )
    logistic, swish = swish_parts(pre_gate)
    activation = (swish * pre_up).astype(jnp.bfloat16)
    produced = jnp.einsum(
        lead + "cf,efd->" + lead + "cd", activation, down_w, preferred_element_type=jnp.float32
    ).astype(jnp.bfloat16)
    return (produced, pre_gate, pre_up)


def expert_revert(slot_grad, pre_gate, pre_up, gate_w, up_w, down_w, lead):
    act_grad = jnp.einsum(
        lead + "cd,efd->" + lead + "cf", slot_grad, down_w, preferred_element_type=jnp.float32
    )
    logistic, swish = swish_parts(pre_gate)
    gate_in = (act_grad * pre_up * logistic * (1.0 + pre_gate * (1.0 - logistic))).astype(
        jnp.bfloat16
    )
    up_in = (act_grad * swish).astype(jnp.bfloat16)
    rows_grad = jnp.einsum(
        lead + "cf,edf->" + lead + "cd", gate_in, gate_w, preferred_element_type=jnp.float32
    )
    rows_grad = rows_grad + jnp.einsum(
        lead + "cf,edf->" + lead + "cd", up_in, up_w, preferred_element_type=jnp.float32
    )
    return (rows_grad.astype(jnp.bfloat16), gate_in, up_in)


def expert_weight_terms(rows_in, gate_in, up_in, pre_gate, pre_up, slot_grad, lead):
    logistic, swish = swish_parts(pre_gate)
    activation = (swish * pre_up).astype(jnp.bfloat16)
    grad_gate = jnp.einsum(
        lead + "cd," + lead + "cf->edf", rows_in, gate_in, preferred_element_type=jnp.float32
    )
    grad_up = jnp.einsum(
        lead + "cd," + lead + "cf->edf", rows_in, up_in, preferred_element_type=jnp.float32
    )
    grad_down = jnp.einsum(
        lead + "cf," + lead + "cd->efd", activation, slot_grad, preferred_element_type=jnp.float32
    )
    return (grad_gate, grad_up, grad_down)


def local(
    inputs,
    block_ids,
    routes,
    out_grad,
    norm_gain,
    w_query,
    key_weight,
    value_weight,
    w_output,
    moe_gain,
    w_router,
    w_gate,
    w_up,
    w_down,
):
    micro = inputs.shape[0]
    sequence_length = inputs.shape[2]
    feature_width = inputs.shape[3]
    top = routes.shape[3]
    experts = w_router.shape[1]
    local_experts = w_gate.shape[0]
    hidden = w_gate.shape[2]
    group_size = QUERY_HEADS // KEY_VALUE_HEADS
    owners = lax.axis_size("fsdp")
    cosine_table, sine_table = rope_tables(sequence_length, HEAD_SIZE)

    def fetch_layer():
        return (
            lax.all_gather(norm_gain, ("fsdp", "dp"), axis=0, tiled=True),
            lax.all_gather(w_query, ("fsdp", "dp"), axis=0, tiled=True),
            lax.all_gather(key_weight, ("fsdp", "dp"), axis=0, tiled=True),
            lax.all_gather(value_weight, ("fsdp", "dp"), axis=0, tiled=True),
            lax.all_gather(w_output, ("fsdp", "dp"), axis=0, tiled=True),
            lax.all_gather(moe_gain, ("fsdp", "dp"), axis=0, tiled=True),
            lax.all_gather(w_router, ("fsdp", "dp"), axis=0, tiled=True),
        )

    def fetch_experts():
        return (
            lax.all_gather(w_gate, "dp", axis=1, tiled=True),
            lax.all_gather(w_up, "dp", axis=1, tiled=True),
            lax.all_gather(w_down, "dp", axis=1, tiled=True),
        )

    total_gain_one = jnp.zeros((feature_width,), jnp.float32)
    total_query = jnp.zeros((feature_width, QUERY_HEADS * HEAD_SIZE), jnp.float32)
    key_weight_total = jnp.zeros((feature_width, KEY_VALUE_HEADS * HEAD_SIZE), jnp.float32)
    value_weight_total = jnp.zeros((feature_width, KEY_VALUE_HEADS * HEAD_SIZE), jnp.float32)
    total_output = jnp.zeros((QUERY_HEADS * HEAD_SIZE, feature_width), jnp.float32)
    total_gain_two = jnp.zeros((feature_width,), jnp.float32)
    total_router = jnp.zeros((feature_width, experts), jnp.float32)
    total_gate = jnp.zeros((local_experts, feature_width, hidden), jnp.float32)
    total_up = jnp.zeros((local_experts, feature_width, hidden), jnp.float32)
    total_down = jnp.zeros((local_experts, hidden, feature_width), jnp.float32)
    expert_ids = jnp.arange(experts, dtype=jnp.int32)
    outputs = []
    input_grads = []
    for index in range(micro):
        layer = fetch_layer()
        expert_w = fetch_experts()
        gain_one, query_w, key_w, value_w, output_w, gain_two, router_w = layer
        gate_w, up_w, down_w = expert_w
        rows = inputs[index, 0].astype(jnp.float32)
        ids = block_ids[index, 0]
        picks = routes[index, 0]
        visible = ids[None, :] <= ids[:, None]
        gain_one_wide = gain_one.astype(jnp.float32)
        gain_two_wide = gain_two.astype(jnp.float32)
        normed = rms_scale(rows, gain_one_wide).astype(jnp.bfloat16)
        query = jnp.dot(normed, query_w, preferred_element_type=jnp.float32)
        key_rows = jnp.dot(normed, key_w, preferred_element_type=jnp.float32)
        value_rows = jnp.dot(normed, value_w, preferred_element_type=jnp.float32).astype(
            jnp.bfloat16
        )
        rotated_queries = apply_rotary(
            query.reshape(sequence_length, QUERY_HEADS, HEAD_SIZE), cosine_table, sine_table
        ).astype(jnp.bfloat16)
        rotated_keys = apply_rotary(
            key_rows.reshape(sequence_length, KEY_VALUE_HEADS, HEAD_SIZE), cosine_table, sine_table
        ).astype(jnp.bfloat16)
        grouped_queries = rotated_queries.reshape(
            sequence_length, KEY_VALUE_HEADS, group_size * HEAD_SIZE
        ).transpose(1, 0, 2)
        key_groups = rotated_keys.transpose(1, 0, 2)
        grouped_values = value_rows.reshape(sequence_length, KEY_VALUE_HEADS, HEAD_SIZE).transpose(
            1, 0, 2
        )

        def attend_group(operands):
            return attend(operands[0], operands[1], operands[2], visible)

        mixed, log_totals = lax.map(attend_group, (grouped_queries, key_groups, grouped_values))
        attended = (
            mixed.transpose(1, 0, 2)
            .reshape(sequence_length, QUERY_HEADS * HEAD_SIZE)
            .astype(jnp.bfloat16)
        )
        branch = jnp.dot(attended, output_w, preferred_element_type=jnp.float32)
        residual = rows + RESIDUAL_SCALE * branch
        moe_in = rms_scale(residual, gain_two_wide).astype(jnp.bfloat16)
        logits = jnp.dot(moe_in, router_w, preferred_element_type=jnp.float32)
        gates = route_gates(logits, picks)
        slot, route_of, filled = slot_layout(picks, experts, CAP)
        dispatch = jnp.where(
            filled[:, None] > 0, moe_in[route_of // top], jnp.zeros((), jnp.bfloat16)
        )
        grad_rows = out_grad[index, 0].astype(jnp.float32)
        moe_grad = RESIDUAL_SCALE * grad_rows
        slot_rows = (
            (gates[:, :, None] * moe_grad[:, None, :])
            .astype(jnp.bfloat16)
            .reshape(sequence_length * top, feature_width)
        )
        slot_grad = jnp.where(filled[:, None] > 0, slot_rows[route_of], jnp.zeros((), jnp.bfloat16))
        arrived = lax.all_to_all(
            dispatch.reshape(owners, local_experts, CAP, feature_width),
            "fsdp",
            split_axis=0,
            concat_axis=0,
            tiled=True,
        )
        produced, pre_gate, pre_up = expert_apply(arrived, gate_w, up_w, down_w, "se")
        expert_out = lax.all_to_all(
            produced, "fsdp", split_axis=0, concat_axis=0, tiled=True
        ).reshape(experts * CAP, feature_width)
        gathered = expert_out[slot].reshape(sequence_length, top, feature_width)
        moe_sum = jnp.sum(gates[:, :, None] * gathered.astype(jnp.float32), axis=1)
        outputs.append((residual + RESIDUAL_SCALE * moe_sum).astype(jnp.bfloat16))
        layer = fetch_layer()
        gain_one, query_w, key_w, value_w, output_w, gain_two, router_w = layer
        gain_one_wide = gain_one.astype(jnp.float32)
        gain_two_wide = gain_two.astype(jnp.float32)
        gate_grad = jnp.sum(moe_grad[:, None, :] * gathered.astype(jnp.float32), axis=2)
        chosen_grad = gates * (gate_grad - jnp.sum(gates * gate_grad, axis=1, keepdims=True))
        logit_grad = jnp.sum(
            jnp.where(picks[:, :, None] == expert_ids[None, None, :], chosen_grad[:, :, None], 0.0),
            axis=1,
        ).astype(jnp.bfloat16)
        expert_w = fetch_experts()
        gate_w, up_w, down_w = expert_w
        arrived_grad = lax.all_to_all(
            slot_grad.reshape(owners, local_experts, CAP, feature_width),
            "fsdp",
            split_axis=0,
            concat_axis=0,
            tiled=True,
        )
        rows_grad, gate_in, up_in = expert_revert(
            arrived_grad, pre_gate, pre_up, gate_w, up_w, down_w, "se"
        )
        grad_gate, grad_up, grad_down = expert_weight_terms(
            arrived, gate_in, up_in, pre_gate, pre_up, arrived_grad, "se"
        )
        total_gate = total_gate + grad_gate
        total_up = total_up + grad_up
        total_down = total_down + grad_down
        returned_grad = lax.all_to_all(
            rows_grad, "fsdp", split_axis=0, concat_axis=0, tiled=True
        ).reshape(experts * CAP, feature_width)
        routed_grad = returned_grad[slot].reshape(sequence_length, top, feature_width)
        moe_in_grad = jnp.einsum(
            "se,de->sd", logit_grad, router_w, preferred_element_type=jnp.float32
        )
        moe_in_grad = moe_in_grad + jnp.sum(routed_grad.astype(jnp.float32), axis=1)
        total_router = total_router + jnp.einsum(
            "sd,se->de", moe_in, logit_grad, preferred_element_type=jnp.float32
        )
        unused_two, norm_two_back = jax.vjp(rms_scale, residual, gain_two_wide)
        residual_norm_grad, gain_two_grad = norm_two_back(moe_in_grad)
        total_gain_two = total_gain_two + gain_two_grad
        residual_grad = grad_rows + residual_norm_grad
        branch_grad = (RESIDUAL_SCALE * residual_grad).astype(jnp.bfloat16)
        total_output = total_output + jnp.einsum(
            "sh,sd->hd", attended, branch_grad, preferred_element_type=jnp.float32
        )
        attended_gradient = jnp.einsum(
            "sd,hd->sh", branch_grad, output_w, preferred_element_type=jnp.float32
        ).astype(jnp.bfloat16)
        gradient_groups = attended_gradient.reshape(
            sequence_length, KEY_VALUE_HEADS, group_size * HEAD_SIZE
        ).transpose(1, 0, 2)

        def attend_group_back(operands):
            return attend_back(
                operands[0], operands[1], operands[2], operands[3], operands[4], visible
            )

        query_grad_rot, key_grad_rot, value_gradient = lax.map(
            attend_group_back,
            (grouped_queries, key_groups, grouped_values, gradient_groups, log_totals),
        )
        query_grad = (
            rotate_back(
                query_grad_rot.transpose(1, 0, 2).reshape(sequence_length, QUERY_HEADS, HEAD_SIZE),
                cosine_table,
                sine_table,
            )
            .reshape(sequence_length, QUERY_HEADS * HEAD_SIZE)
            .astype(jnp.bfloat16)
        )
        key_grad = (
            rotate_back(key_grad_rot.transpose(1, 0, 2), cosine_table, sine_table)
            .reshape(sequence_length, KEY_VALUE_HEADS * HEAD_SIZE)
            .astype(jnp.bfloat16)
        )
        value_gradient = (
            value_gradient.transpose(1, 0, 2)
            .reshape(sequence_length, KEY_VALUE_HEADS * HEAD_SIZE)
            .astype(jnp.bfloat16)
        )
        normed_grad = jnp.einsum(
            "sh,dh->sd", query_grad, query_w, preferred_element_type=jnp.float32
        )
        normed_grad = normed_grad + jnp.einsum(
            "sh,dh->sd", key_grad, key_w, preferred_element_type=jnp.float32
        )
        normed_grad = normed_grad + jnp.einsum(
            "sh,dh->sd", value_gradient, value_w, preferred_element_type=jnp.float32
        )
        total_query = total_query + jnp.einsum(
            "sd,sh->dh", normed, query_grad, preferred_element_type=jnp.float32
        )
        key_weight_total = key_weight_total + jnp.einsum(
            "sd,sh->dh", normed, key_grad, preferred_element_type=jnp.float32
        )
        value_weight_total = value_weight_total + jnp.einsum(
            "sd,sh->dh", normed, value_gradient, preferred_element_type=jnp.float32
        )
        unused_one, norm_one_back = jax.vjp(rms_scale, rows, gain_one_wide)
        rows_norm_grad, gain_one_grad = norm_one_back(normed_grad)
        total_gain_one = total_gain_one + gain_one_grad
        input_grads.append(residual_grad + rows_norm_grad)
    layer_totals = (
        lax.psum_scatter(total_gain_one, ("fsdp", "dp"), scatter_dimension=0, tiled=True),
        lax.psum_scatter(total_query, ("fsdp", "dp"), scatter_dimension=0, tiled=True),
        lax.psum_scatter(key_weight_total, ("fsdp", "dp"), scatter_dimension=0, tiled=True),
        lax.psum_scatter(value_weight_total, ("fsdp", "dp"), scatter_dimension=0, tiled=True),
        lax.psum_scatter(total_output, ("fsdp", "dp"), scatter_dimension=0, tiled=True),
        lax.psum_scatter(total_gain_two, ("fsdp", "dp"), scatter_dimension=0, tiled=True),
        lax.psum_scatter(total_router, ("fsdp", "dp"), scatter_dimension=0, tiled=True),
    )
    expert_totals = (
        lax.psum_scatter(
            total_gate.astype(jnp.bfloat16), "dp", scatter_dimension=1, tiled=True
        ).astype(jnp.float32),
        lax.psum_scatter(
            total_up.astype(jnp.bfloat16), "dp", scatter_dimension=1, tiled=True
        ).astype(jnp.float32),
        lax.psum_scatter(
            total_down.astype(jnp.bfloat16), "dp", scatter_dimension=1, tiled=True
        ).astype(jnp.float32),
    )
    return (
        jnp.stack(outputs)[:, None],
        jnp.stack(input_grads)[:, None],
        layer_totals[0],
        layer_totals[1],
        layer_totals[2],
        layer_totals[3],
        layer_totals[4],
        layer_totals[5],
        layer_totals[6],
        expert_totals[0],
        expert_totals[1],
        expert_totals[2],
    )


def solution(mesh):
    in_specs = (
        P(None, ("fsdp", "dp"), None, None),
        P(None, ("fsdp", "dp"), None),
        P(None, ("fsdp", "dp"), None, None),
        P(None, ("fsdp", "dp"), None, None),
        P(("fsdp", "dp")),
        P(("fsdp", "dp"), None),
        P(("fsdp", "dp"), None),
        P(("fsdp", "dp"), None),
        P(("fsdp", "dp"), None),
        P(("fsdp", "dp")),
        P(("fsdp", "dp"), None),
        P("fsdp", "dp", None),
        P("fsdp", "dp", None),
        P("fsdp", "dp", None),
    )
    out_specs = (
        P(None, ("fsdp", "dp"), None, None),
        P(None, ("fsdp", "dp"), None, None),
        P(("fsdp", "dp")),
        P(("fsdp", "dp"), None),
        P(("fsdp", "dp"), None),
        P(("fsdp", "dp"), None),
        P(("fsdp", "dp"), None),
        P(("fsdp", "dp")),
        P(("fsdp", "dp"), None),
        P("fsdp", "dp", None),
        P("fsdp", "dp", None),
        P("fsdp", "dp", None),
    )
    return jax.shard_map(local, mesh=mesh, in_specs=in_specs, out_specs=out_specs, check_vma=False)
```

profile of v0, /device:TPU:0, one launch (start us, length us, event | category | flops | bytes accessed | tf_op | source)
XLA Modules:
  0.0 2396.0 jit_solution(17857516314177445439)
XLA Ops:
  15.0 42.0 %all-reduce.5 = (bf16[1024]{0:T(1024)(128)(2,1)S(1)}, bf16[1024]{0:T(1024)(128)(2,1)S(1)}) all-reduce(bf16[1024]{0:T(1024)(128)(2,1)S(1)} %dynamic-update-slice, bf16[1024]{0:T(1024)(128)(2,1)S(1)} %dynamic-update-slice.1), channel_id=1, replica_groups=mesh['fsdp'=8,'dp'=4] {'fsdp','dp'}, use_global_device_ids=true, to_apply=%add | all-reduce | flops 2048 | bytes 8192
  61.5 73.3 %all_gather.26 = bf16[1024,32]{1,0:T(8,128)(2,1)} all-gather(bf16[32,32]{1,0:T(8,128)(2,1)S(1)} %copy-done.110), channel_id=1, replica_groups=mesh['fsdp'=8,'dp'=4] {'fsdp','dp'}, dimensions={0}, use_global_device_ids=true | all-gather | bytes 67584 | tf_op jit(solution)/shard_map/all_gather | solution.py:196
  211.0 40.1 %while.56 = (s32[]{:T(128)}, bf16[8,512,128]{1,2,0:T(8,128)(2,1)S(1)}, f32[8,2,512]{2,1,0:T(2,128)S(1)}, bf16[8,512,64]{1,2,0:T(8,128)(2,1)}, bf16[8,512,64]{1,2...) while((s32[]{:T(128)}, bf16[8,512,128]{1,2,0:T(8,128)(2,1)S(1)}, ...), condition=%wide.region_4.5_spmd.clone, body=%wide.region_1.4_spmd.clone.sunk | while | flops 138673152 | bytes 7769185 | solution.py:253
  256.6 33.1 %gather_fusion.8 = f32[4096]{0:T(1024)S(1)} fusion(f32[512,32]{0,1:T(8,128)S(1)} %fusion.271, s32[4096]{0:T(1024)S(1)} %reshape.796), kind=kCustom, calls=%fused_computation.clone | custom fusion | bytes 65536 | tf_op jit(solution)/shard_map/jit(take_along_axis)/gather | solution.py:46
  355.4 104.7 %all-to-all-done = bf16[8,4,144,1024]{3,2,1,0:T(8,128)(2,1)} async-done(((bf16[8,4,144,1024]{3,2,1,0:T(8,128)(2,1)}), bf16[8,4,144,1024]{3,2,1,0:T(8,128)(2,1)}, u32[]{:S(2)}, u32[]{:S(2)}) %all-to-all-start) | async-done | bytes 9437216 | tf_op jit(solution)/shard_map/all_to_all | solution.py:276
  488.1 58.9 %all-gather.20.cloned.1.call-done = bf16[4,512,1024]{2,1,0:T(8,128)(2,1)} async-done(((bf16[4,128,1024]{2,1,0:T(8,128)(2,1)}), bf16[4,512,1024]{2,1,0:T(8,128)(2,1)}) %all-gather.20.cloned.1.call-update) | async-done | bytes 4194320 | tf_op jit(solution)/shard_map/all_gather | solution.py:203
  723.9 34.1 %while.57 = (s32[]{:T(128)}, bf16[8,512,128]{1,2,0:T(8,128)(2,1)S(1)}, f32[8,2,512]{2,1,0:T(2,128)S(1)}, bf16[8,512,64]{1,2,0:T(8,128)(2,1)}, bf16[8,512,64]{1,2...) while((s32[]{:T(128)}, bf16[8,512,128]{1,2,0:T(8,128)(2,1)S(1)}, ...), condition=%wide.region_18.20_spmd.clone, body=%wide.region_15.19_spmd.clone.sunk | while | flops 138673152 | bytes 7769185 | solution.py:253
  762.7 25.9 %gather_fusion.1 = bf16[4096,1024]{1,0:T(8,128)(2,1)} fusion(bf16[4608,1024]{1,0:T(8,128)(2,1)} %bitcast.31, s32[4096]{0:T(1024)S(1)} %broadcast_clamp_fusion.1), kind=kCustom, calls=%fused_computation.3 | custom fusion | bytes 16793600 | tf_op jit(solution)/shard_map/gather | solution.py:287
  798.9 30.2 %all-to-all-done.5 = bf16[8,4,144,1024]{3,2,1,0:T(8,128)(2,1)} async-done(((bf16[8,4,144,1024]{3,2,1,0:T(8,128)(2,1)}), bf16[8,4,144,1024]{3,2,1,0:T(8,128)(2,1)}, u32[]{:S(2)}, u32[]{:S(2)}) %all-to-all-start.5) | async-done | bytes 9437216 | tf_op jit(solution)/shard_map/all_to_all | solution.py:318
  829.1 26.2 %gather_fusion.5 = bf16[4096,1024]{1,0:T(8,128)(2,1)} fusion(bf16[4608,1024]{1,0:T(8,128)(2,1)} %bitcast.70, s32[4096]{0:T(1024)S(1)} %broadcast_clamp_fusion.1), kind=kCustom, calls=%fused_computation.7 | custom fusion | bytes 16793600 | tf_op jit(solution)/shard_map/gather | solution.py:321
  872.9 33.1 %gather_fusion.9 = f32[4096]{0:T(1024)S(1)} fusion(f32[512,32]{0,1:T(8,128)S(1)} %fusion.272, s32[4096]{0:T(1024)S(1)} %reshape.801), kind=kCustom, calls=%fused_computation.1.clone | custom fusion | bytes 65536 | tf_op jit(solution)/shard_map/jit(take_along_axis)/gather | solution.py:46
  963.0 108.7 %all_to_all.40 = bf16[8,4,144,1024]{3,2,1,0:T(8,128)(2,1)} all-to-all(bf16[8,4,144,1024]{3,2,1,0:T(8,128)(2,1)S(1)} %get-tuple-element.498), channel_id=1, replica_groups=mesh['fsdp'=8,'dp'=4] {'fsdp'}, dimensions={0} | all-to-all | bytes 18874368 | tf_op jit(solution)/shard_map/all_to_all | solution.py:276
  1096.3 85.8 %all-to-all-done.6 = bf16[8,4,144,1024]{3,2,1,0:T(8,128)(2,1)} async-done(((bf16[8,4,144,1024]{3,2,1,0:T(8,128)(2,1)}), bf16[8,4,144,1024]{3,2,1,0:T(8,128)(2,1)}, u32[]{:S(2)}, u32[]{:S(2)}) %all-to-all-start.6) | async-done | bytes 9437216 | tf_op jit(solution)/shard_map/all_to_all | solution.py:302
  1310.7 46.7 %all-to-all-done.3 = bf16[8,4,144,1024]{3,2,1,0:T(8,128)(2,1)} async-done(((bf16[8,4,144,1024]{3,2,1,0:T(8,128)(2,1)}), bf16[8,4,144,1024]{3,2,1,0:T(8,128)(2,1)}, u32[]{:S(2)}, u32[]{:S(2)}) %all-to-all-start.3) | async-done | bytes 9437216 | tf_op jit(solution)/shard_map/all_to_all | solution.py:284
  1389.7 25.9 %gather_fusion.3 = bf16[4096,1024]{1,0:T(8,128)(2,1)} fusion(bf16[4608,1024]{1,0:T(8,128)(2,1)} %bitcast.58, s32[4096]{0:T(1024)S(1)} %broadcast_clamp_fusion), kind=kCustom, calls=%fused_computation.5 | custom fusion | bytes 16793600 | tf_op jit(solution)/shard_map/gather | solution.py:287
  1426.0 41.9 %all-to-all-done.7 = bf16[8,4,144,1024]{3,2,1,0:T(8,128)(2,1)} async-done(((bf16[8,4,144,1024]{3,2,1,0:T(8,128)(2,1)}), bf16[8,4,144,1024]{3,2,1,0:T(8,128)(2,1)}, u32[]{:S(2)}, u32[]{:S(2)}) %all-to-all-start.7) | async-done | bytes 9437216 | tf_op jit(solution)/shard_map/all_to_all | solution.py:318
  1467.9 26.2 %gather_fusion.7 = bf16[4096,1024]{1,0:T(8,128)(2,1)} fusion(bf16[4608,1024]{1,0:T(8,128)(2,1)} %bitcast.94, s32[4096]{0:T(1024)S(1)} %broadcast_clamp_fusion), kind=kCustom, calls=%fused_computation.9 | custom fusion | bytes 16793600 | tf_op jit(solution)/shard_map/gather | solution.py:321
  1518.9 65.6 %while.59 = (s32[]{:T(128)}, f32[8,512,128]{1,2,0:T(8,128)S(1)}, f32[8,512,64]{1,2,0:T(8,128)S(1)}, bf16[8,512,64]{1,2,0:T(8,128)(2,1)}, bf16[8,512,64]{1,2,0:T(...) while((s32[]{:T(128)}, f32[8,512,128]{1,2,0:T(8,128)S(1)}, ...), condition=%wide.region_44.46_spmd.clone, body=%wide.region_42.45_spmd.clone.sunk | while | flops 340622336 | bytes 18571388 | solution.py:349
  1595.1 76.3 %while.58 = (s32[]{:T(128)}, f32[8,512,128]{1,2,0:T(8,128)}, f32[8,512,64]{1,2,0:T(8,128)}, bf16[8,512,64]{1,2,0:T(8,128)(2,1)}, bf16[8,512,64]{1,2,0:T(8,128)(2...) while((s32[]{:T(128)}, f32[8,512,128]{1,2,0:T(8,128)}, ...), condition=%wide.region_35.37_spmd.clone, body=%wide.region_33.36_spmd.clone.sunk | while | flops 340622336 | bytes 18572404 | solution.py:349
  1730.0 37.2 %all-reduce.4 = (f32[1024]{0:T(1024)S(1)}, f32[1024]{0:T(1024)S(1)}) all-reduce(f32[1024]{0:T(1024)S(1)} %add.352, f32[1024]{0:T(1024)S(1)} %add.359), channel_id=2, replica_groups=mesh['fsdp'=8,'dp'=4] {'fsdp','dp'}, use_global_device_ids=true, to_apply=%region_48.50.clone | all-reduce | flops 2048 | bytes 16384
  1809.8 138.8 %reduce-scatter.13.cloned.1.call-done = f32[32,512]{1,0:T(8,128)} async-done(((f32[1024,512]{1,0:T(8,128)}), f32[32,512]{1,0:T(8,128)}) %reduce-scatter.13.cloned.1.call-update) | async-done | bytes 65552 | tf_op jit(solution)/shard_map/reduce_scatter | solution.py:398
  1948.6 140.4 %reduce-scatter.11.cloned.1.call-done = f32[32,512]{1,0:T(8,128)} async-done(((f32[1024,512]{1,0:T(8,128)}), f32[32,512]{1,0:T(8,128)}) %reduce-scatter.11.cloned.1.call-update) | async-done | bytes 65552 | tf_op jit(solution)/shard_map/reduce_scatter | solution.py:397
  2089.0 149.4 %reduce-scatter.15.cloned.1.call-done = f32[32,1024]{1,0:T(8,128)} async-done(((f32[1024,1024]{1,0:T(8,128)}), f32[32,1024]{1,0:T(8,128)}) %reduce-scatter.15.cloned.1.call-update) | async-done | bytes 131088 | tf_op jit(solution)/shard_map/reduce_scatter | solution.py:399
  2238.4 150.7 %reduce-scatter.9.cloned.1.call-done = f32[32,1024]{1,0:T(8,128)} async-done(((f32[1024,1024]{1,0:T(8,128)}), f32[32,1024]{1,0:T(8,128)}) %reduce-scatter.9.cloned.1.call-update) | async-done | bytes 131088 | tf_op jit(solution)/shard_map/reduce_scatter | solution.py:396
  (757 shorter events, 999.7 us)
Async XLA Ops:
  7.2 180.8 %all-gather.10.cloned.1.call-start = ((), (), s32[]{:S(2)}) async-start(), calls=%async_computation.17 | async-start | bytes 1081344 | tf_op jit(solution)/shard_map/all_gather | solution.py:192
  7.9 188.0 %all-gather.8.cloned.1.call-start = ((), (), s32[]{:S(2)}) async-start(), calls=%async_computation.16 | async-start | bytes 1081344 | tf_op jit(solution)/shard_map/all_gather | solution.py:193
  8.7 190.1 %all-gather.12.cloned.1.call-start = ((), (), s32[]{:S(2)}) async-start(), calls=%async_computation.18 | async-start | bytes 2162688 | tf_op jit(solution)/shard_map/all_gather | solution.py:191
  9.4 241.8 %all-gather.14.cloned.1.call-start = ((), (), s32[]{:S(2)}) async-start(), calls=%async_computation.19 | async-start | bytes 2162688 | tf_op jit(solution)/shard_map/all_gather | solution.py:194
  10.0 456.0 %all-gather.18.cloned.1.call-start = ((), (), s32[]{:S(2)}) async-start(), calls=%async_computation.21 | async-start | bytes 5242880 | tf_op jit(solution)/shard_map/all_gather | solution.py:202
  59.6 148.3 %copy-start.46 = (f32[512,64]{0,1:T(8,128)}, f32[512,64]{0,1:T(8,128)S(1)}, u32[]{:S(2)}) copy-start(f32[512,64]{0,1:T(8,128)S(1)} %pad_maximum_fusion.2) | copy-start | bytes 393220
  349.8 110.3 %all-to-all-start = ((bf16[8,4,144,1024]{3,2,1,0:T(8,128)(2,1)}), bf16[8,4,144,1024]{3,2,1,0:T(8,128)(2,1)}, u32[]{:S(2)}, u32[]{:S(2)}) async-start(bf16[8,4,144,1024]{3,2,1,0:T(8,128)(2,1)} %get-tuple-element.496), calls=%async_computation | async-start | bytes 18874368 | tf_op jit(solution)/shard_map/all_to_all | solution.py:276
  354.9 122.2 %all-gather.16.cloned.1.call-start = ((), (), s32[]{:S(2)}) async-start(), calls=%async_computation.20 | async-start | bytes 5242880 | tf_op jit(solution)/shard_map/all_gather | solution.py:201
  460.1 110.4 %all-to-all-start.4 = ((bf16[8,4,144,1024]{3,2,1,0:T(8,128)(2,1)}), bf16[8,4,144,1024]{3,2,1,0:T(8,128)(2,1)}, u32[]{:S(2)}, u32[]{:S(2)}) async-start(bf16[8,4,144,1024]{3,2,1,0:T(8,128)(2,1)} %get-tuple-element.495), calls=%async_computation.4 | async-start | bytes 18874368 | tf_op jit(solution)/shard_map/all_to_all | solution.py:302
  465.2 81.7 %all-gather.20.cloned.1.call-start = ((), (), s32[]{:S(2)}) async-start(), calls=%async_computation.22 | async-start | bytes 5242880 | tf_op jit(solution)/shard_map/all_gather | solution.py:203
  607.9 110.6 %all-to-all-start.1 = ((bf16[8,4,144,1024]{3,2,1,0:T(8,128)(2,1)}), bf16[8,4,144,1024]{3,2,1,0:T(8,128)(2,1)}, u32[]{:S(2)}, u32[]{:S(2)}) async-start(bf16[8,4,144,1024]{3,2,1,0:T(8,128)(2,1)} %copy.117), calls=%async_computation.1 | async-start | bytes 18874368 | tf_op jit(solution)/shard_map/all_to_all | solution.py:284
  718.6 110.6 %all-to-all-start.5 = ((bf16[8,4,144,1024]{3,2,1,0:T(8,128)(2,1)}), bf16[8,4,144,1024]{3,2,1,0:T(8,128)(2,1)}, u32[]{:S(2)}, u32[]{:S(2)}) async-start(bf16[8,4,144,1024]{3,2,1,0:T(8,128)(2,1)} %copy.125), calls=%async_computation.5 | async-start | bytes 18874368 | tf_op jit(solution)/shard_map/all_to_all | solution.py:318
  762.7 104.8 %copy-start.93 = (f32[512]{0:T(512)}, f32[512]{0:T(512)S(1)}, u32[]{:S(2)}) copy-start(f32[512]{0:T(512)S(1)} %fusion.245) | copy-start | bytes 6148
  1071.7 110.3 %all-to-all-start.6 = ((bf16[8,4,144,1024]{3,2,1,0:T(8,128)(2,1)}), bf16[8,4,144,1024]{3,2,1,0:T(8,128)(2,1)}, u32[]{:S(2)}, u32[]{:S(2)}) async-start(bf16[8,4,144,1024]{3,2,1,0:T(8,128)(2,1)} %get-tuple-element.497), calls=%async_computation.6 | async-start | bytes 18874368 | tf_op jit(solution)/shard_map/all_to_all | solution.py:302
  1076.8 699.8 %reduce-scatter.23.cloned.1.call-start = ((), (), s32[]{:S(2)}) async-start(), calls=%async_computation.30 | async-start | bytes 5242880 | tf_op jit(solution)/shard_map/reduce_scatter | solution.py:410
  1246.9 110.5 %all-to-all-start.3 = ((bf16[8,4,144,1024]{3,2,1,0:T(8,128)(2,1)}), bf16[8,4,144,1024]{3,2,1,0:T(8,128)(2,1)}, u32[]{:S(2)}, u32[]{:S(2)}) async-start(bf16[8,4,144,1024]{3,2,1,0:T(8,128)(2,1)} %copy.121), calls=%async_computation.3 | async-start | bytes 18874368 | tf_op jit(solution)/shard_map/all_to_all | solution.py:284
  1252.2 527.2 %reduce-scatter.21.cloned.1.call-start = ((), (), s32[]{:S(2)}) async-start(), calls=%async_computation.29 | async-start | bytes 5242880 | tf_op jit(solution)/shard_map/reduce_scatter | solution.py:407
  1357.4 110.5 %all-to-all-start.7 = ((bf16[8,4,144,1024]{3,2,1,0:T(8,128)(2,1)}), bf16[8,4,144,1024]{3,2,1,0:T(8,128)(2,1)}, u32[]{:S(2)}, u32[]{:S(2)}) async-start(bf16[8,4,144,1024]{3,2,1,0:T(8,128)(2,1)} %copy.130), calls=%async_computation.7 | async-start | bytes 18874368 | tf_op jit(solution)/shard_map/all_to_all | solution.py:318
  1362.6 419.6 %reduce-scatter.19.cloned.1.call-start = ((), (), s32[]{:S(2)}) async-start(), calls=%async_computation.28 | async-start | bytes 5242880 | tf_op jit(solution)/shard_map/reduce_scatter | solution.py:404
  1389.6 420.1 %reduce-scatter.17.cloned.1.call-start = ((), (), s32[]{:S(2)}) async-start(), calls=%async_computation.27 | async-start | bytes 540672 | tf_op jit(solution)/shard_map/reduce_scatter | solution.py:401
  1677.3 271.3 %reduce-scatter.13.cloned.1.call-start = ((), (), s32[]{:S(2)}) async-start(), calls=%async_computation.25 | async-start | bytes 2162688 | tf_op jit(solution)/shard_map/reduce_scatter | solution.py:398
  1681.4 407.6 %reduce-scatter.11.cloned.1.call-start = ((), (), s32[]{:S(2)}) async-start(), calls=%async_computation.24 | async-start | bytes 2162688 | tf_op jit(solution)/shard_map/reduce_scatter | solution.py:397
  1690.8 547.6 %reduce-scatter.15.cloned.1.call-start = ((), (), s32[]{:S(2)}) async-start(), calls=%async_computation.26 | async-start | bytes 4325376 | tf_op jit(solution)/shard_map/reduce_scatter | solution.py:399
  1697.5 691.6 %reduce-scatter.9.cloned.1.call-start = ((), (), s32[]{:S(2)}) async-start(), calls=%async_computation.23 | async-start | bytes 4325376 | tf_op jit(solution)/shard_map/reduce_scatter | solution.py:396
  (120 other events, 1656.3 us)
Sparse Core Ops, SparseCore 0:
  11.0 56.5 all-gather.9
  70.5 53.0 all-gather.7
  126.5 55.4 all-gather.11
  184.8 55.2 all-gather.13
  241.5 79.5 all-gather.17
  356.9 79.2 all-gather.15
  467.6 79.3 all-gather.19
  1227.2 73.1 reduce-scatter.22
  1302.7 77.2 reduce-scatter.20
  1389.8 75.3 reduce-scatter.18
  1677.4 132.3 reduce-scatter.16
  1812.5 136.1 reduce-scatter.12
  1951.5 137.4 reduce-scatter.10
  2091.7 146.6 reduce-scatter.14
  2241.1 147.9 reduce-scatter.8
where the time goes:
time: 2410 us; the launch traced here: 2400 us
  waiting for transfers between devices  1020 us (42%)
  local copies, waits for them, and re-layouts  440 us (18%)
  matrix products  433 us (18%)
  blocking collectives  261 us (11%)
  other arithmetic  184 us (8%)
  starting transfers between devices  37.1 us (2%)
    reduce_scatter x1, waiting for transfers between devices, local(): lax.psum_scatter(total_query, ('fsdp', 'dp'), scatter_dimension=0, tiled=...  151 us
    reduce_scatter x1, waiting for transfers between devices, local(): lax.psum_scatter(total_output, ('fsdp', 'dp'), scatter_dimension=0, tiled...  149 us
    reduce_scatter x1, waiting for transfers between devices, local(): lax.psum_scatter(key_weight_total, ('fsdp', 'dp'), scatter_dimension=0, t...  140 us
    reduce_scatter x1, waiting for transfers between devices, local(): lax.psum_scatter(value_weight_total, ('fsdp', 'dp'), scatter_dimension=0,...  139 us
    all_to_all x2, waiting for transfers between devices, local(): lax.all_to_all(slot_grad.reshape(owners, local_experts, CAP, feature_widt...  109 us
    all_to_all x1, blocking collectives, local(): lax.all_to_all(dispatch.reshape(owners, local_experts, CAP, feature_width...  109 us
    all_to_all x1, waiting for transfers between devices, local(): lax.all_to_all(dispatch.reshape(owners, local_experts, CAP, feature_width...  105 us
    unnamed x2, blocking collectives  79.2 us
  transfers between devices with their start and end apart: 22, of which 13 were waited for; matrix products, arithmetic and copies ran while one was open for 35% of the time, Pallas kernels for 0%

commit v1 on v0

v1 whole, which is shorter than its diff:
```python
import functools

import jax
import jax.numpy as jnp
import numpy as np
from jax import lax
from jax.experimental import pallas as pl
from jax.experimental.pallas import tpu as pltpu
from jax.sharding import PartitionSpec as P

QUERY_HEADS = 16
KEY_VALUE_HEADS = 8
HEAD_SIZE = 64
CAP = 144
EPS = 1e-06
RESIDUAL_SCALE = 0.22
SCORE_SCALE = 0.015625
THETA = 10000.0
NEG_FILL = -1e30
LANES = 128

BF = jnp.bfloat16
F32 = jnp.float32
VMEM_LIMIT = 64 * 1024 * 1024 - 128 * 1024


def mm(a, b):
    return jnp.dot(a, b, preferred_element_type=F32)


def mm_nt(a, b):
    return lax.dot_general(a, b, (((1,), (1,)), ((), ())), preferred_element_type=F32)


def mm_tn(a, b):
    return lax.dot_general(a, b, (((0,), (0,)), ((), ())), preferred_element_type=F32)


def rope_tables(sequence_length):
    half = HEAD_SIZE // 2
    inverse = np.float32(THETA) ** (-(np.arange(half, dtype=np.float32) * 2.0) / HEAD_SIZE)
    angles = np.arange(sequence_length, dtype=np.float32)[:, None] * inverse.astype(np.float32)[None, :]
    cosine, sine = np.cos(angles), np.sin(angles)
    copies = LANES // HEAD_SIZE
    cosine = np.tile(np.concatenate([cosine, cosine], 1), (1, copies))
    sine = np.tile(np.concatenate([-sine, sine], 1), (1, copies))
    return cosine.astype(np.float32), sine.astype(np.float32)


def lane_iota(shape):
    return lax.broadcasted_iota(jnp.int32, shape, len(shape) - 1)


def turn(block, cosine, sine):
    half = HEAD_SIZE // 2
    lower = (lane_iota(block.shape) % HEAD_SIZE) < half
    partner = jnp.where(
        lower, pltpu.roll(block, LANES - half, 1), pltpu.roll(block, half, 1)
    )
    return block * cosine + partner * sine


def tile_ds(index, width):
    return pl.ds(pl.multiple_of(index * width, width), width)


def head_pair(block, place):
    lower = lane_iota(block.shape) < HEAD_SIZE
    moved = pltpu.roll(block, HEAD_SIZE, 1)
    zero = jnp.zeros_like(block)
    low, high = (block, moved) if place == 0 else (moved, block)
    return jnp.where(lower, low, zero), jnp.where(lower, zero, high)


def attention_forward_kernel(
    x_ref, w_ref, gain_one_ref, gain_two_ref, id_row_ref, id_col_ref, cos_ref, sin_ref, picks_ref,
    q_ref, k_ref, v_ref, att_ref, lse_ref, res_ref, pay_ref, gate_ref,
    normed_ref, bias_ref,
    *, q_width, kv_width, experts,
):
    rows, width = x_ref.shape
    x = x_ref[...].astype(F32)
    scale = lax.rsqrt(jnp.mean(x * x, axis=1, keepdims=True) + EPS)
    normed_ref[...] = (x * scale * gain_one_ref[...]).astype(BF)
    bias_ref[...] = jnp.where(id_col_ref[...] <= id_row_ref[...], 0.0, NEG_FILL)
    step = 256

    def project(out_ref, start, count, rotate):
        def body(j, carry):
            cols = pl.ds(pl.multiple_of(start + j * step, step), step)
            part = mm(normed_ref[...], w_ref[:, cols])
            if rotate:
                part = jnp.concatenate(
                    [
                        turn(part[:, i * LANES : (i + 1) * LANES], cos_ref[...], sin_ref[...])
                        for i in range(step // LANES)
                    ],
                    axis=1,
                )
            out_ref[:, tile_ds(j, step)] = part.astype(BF)
            return carry

        lax.fori_loop(0, count // step, body, 0)

    project(q_ref, 0, q_width, True)
    project(k_ref, q_width, kv_width, True)
    project(v_ref, q_width + kv_width, kv_width, False)

    def pair_body(j, carry):
        k_block = k_ref[:, tile_ds(j, LANES)].astype(F32)
        v_block = v_ref[:, tile_ds(j, LANES)].astype(F32)
        for place in range(2):
            keys = head_pair(k_block, place)
            vals = head_pair(v_block, place)
            group = 2 * j + place
            q_block = q_ref[:, tile_ds(group, LANES)]
            out = None
            for side in range(2):
                scores = mm_nt(keys[side].astype(BF), q_block) * SCORE_SCALE + bias_ref[...]
                highest = jnp.max(scores, axis=0, keepdims=True)
                lifted = jnp.exp(scores - highest)
                total = jnp.sum(lifted, axis=0, keepdims=True)
                low = (lifted * (1.0 / total)).astype(BF)
                lse_ref[pl.ds(2 * group + side, 1), :] = highest + jnp.log(total)
                part = mm_tn(vals[side].astype(BF), low)
                out = part if out is None else out + part
            att_ref[:, tile_ds(group, LANES)] = out.T.astype(BF)
        return carry

    lax.fori_loop(0, KEY_VALUE_HEADS // 2, pair_body, 0)

    start = q_width + 2 * kv_width

    def out_body(j, total):
        cols = pl.ds(pl.multiple_of(start + j * step, step), step)
        here = tile_ds(j, step)
        value = x_ref[:, here].astype(F32) + RESIDUAL_SCALE * mm(att_ref[...], w_ref[:, cols])
        res_ref[:, here] = value
        return total + jnp.sum(value * value, axis=1, keepdims=True)

    square = lax.fori_loop(0, width // step, out_body, jnp.zeros((rows, 1), F32))
    scale = lax.rsqrt(square * (1.0 / width) + EPS)
    pay_ref[:rows, :] = (res_ref[...] * scale * gain_two_ref[...]).astype(BF)
    logits = mm(pay_ref[:rows, :], w_ref[:, start + width :])
    lanes = lane_iota(logits.shape)
    chosen = lanes < 0
    for k in range(picks_ref.shape[1]):
        chosen = chosen | (picks_ref[:, k : k + 1] == lanes)
    masked = jnp.where(chosen, logits, NEG_FILL)
    lifted = jnp.where(chosen, jnp.exp(masked - jnp.max(masked, axis=1, keepdims=True)), 0.0)
    gates = lifted / jnp.sum(lifted, axis=1, keepdims=True)
    across = gates.T[:experts, :]
    gate_ref[...] = across
    high = across.astype(BF)
    pay_ref[rows:, :rows] = high
    pay_ref[rows:, rows:] = (across - high.astype(F32)).astype(BF)


def attention_forward(x, pack, gain_one, gain_two, ids, picks, tables, q_width, kv_width, experts):
    rows, width = x.shape
    out_shape = (
        jax.ShapeDtypeStruct((rows, q_width), BF),
        jax.ShapeDtypeStruct((rows, kv_width), BF),
        jax.ShapeDtypeStruct((rows, kv_width), BF),
        jax.ShapeDtypeStruct((rows, q_width), BF),
        jax.ShapeDtypeStruct((QUERY_HEADS, rows), F32),
        jax.ShapeDtypeStruct((rows, width), F32),
        jax.ShapeDtypeStruct((rows + experts, width), BF),
        jax.ShapeDtypeStruct((experts, rows), F32),
    )
    flops = 2 * rows * width * (q_width + 2 * kv_width + width) + 8 * QUERY_HEADS * rows * rows * 128
    return pl.pallas_call(
        functools.partial(
            attention_forward_kernel, q_width=q_width, kv_width=kv_width, experts=experts
        ),
        out_shape=out_shape,
        scratch_shapes=[pltpu.VMEM((rows, width), BF), pltpu.VMEM((rows, rows), F32)],
        compiler_params=pltpu.CompilerParams(vmem_limit_bytes=VMEM_LIMIT),
        cost_estimate=pl.CostEstimate(
            flops=flops, transcendentals=QUERY_HEADS * rows * rows, bytes_accessed=16 << 20
        ),
        name="attention_forward",
    )(x, pack, gain_one, gain_two, ids[None, :], ids[:, None], *tables, picks)


def slot_marks(sel_ref, gate_rows, upper_ref, local):
    picked = mm(sel_ref[...], gate_rows)
    rows = picked.shape[1] // 2
    gates = picked[:, :rows] + picked[:, rows:]
    used = gates != 0.0
    rank = mm(used.astype(F32).astype(BF), upper_ref[...])
    slots = jnp.where(used, rank, -1.0)
    places = lax.broadcasted_iota(jnp.int32, (CAP, rows), 0).astype(F32)
    hits = [places == slots[e : e + 1, :] for e in range(local)]
    return gates, hits


def fill_upper(upper_ref):
    rows = upper_ref.shape[0]
    upper = lax.broadcasted_iota(jnp.int32, (rows, rows), 0) < lane_iota((rows, rows))
    upper_ref[...] = jnp.where(upper, 1.0, 0.0).astype(BF)


def dispatch_kernel(sel_ref, pay_ref, grad_ref, *refs, local):
    rows_ref, slot_ref, upper_ref = refs[-3:]

    @pl.when(pl.program_id(0) == 0)
    def _():
        fill_upper(upper_ref)

    rows = grad_ref.shape[1]
    gates, hits = slot_marks(sel_ref, pay_ref[0, rows:, :], upper_ref, local)
    marks = jnp.concatenate([jnp.where(h, 1.0, 0.0).astype(BF) for h in hits], axis=0)
    column = jnp.concatenate(
        [
            jnp.sum(jnp.where(h, gates[e : e + 1, :], 0.0), axis=1, keepdims=True)
            for e, h in enumerate(hits)
        ],
        axis=0,
    )
    moved = mm(marks, pay_ref[0, :rows, :]).astype(BF)
    grads = (column * (RESIDUAL_SCALE * mm(marks, grad_ref[0]))).astype(BF)
    for e in range(local):
        rows_ref[e, 0, 0] = moved[e * CAP : (e + 1) * CAP]
        slot_ref[e, 0, 0] = grads[e * CAP : (e + 1) * CAP]


def dispatch(sel, pays, grads, place, places, local, carried):
    count, rows, width = grads.shape
    shape = jax.ShapeDtypeStruct((local, places, count, CAP, width), BF)
    out_spec = pl.BlockSpec((local, 1, 1, CAP, width), lambda s: (0, place, s, 0, 0))
    in_specs = [
        pl.BlockSpec(sel.shape, lambda s: (0, 0)),
        pl.BlockSpec((1,) + pays.shape[1:], lambda s: (s, 0, 0)),
        pl.BlockSpec((1, rows, width), lambda s: (s, 0, 0)),
    ]
    operands = [sel, pays, grads]
    aliases = {}
    if carried is not None:
        operands += list(carried)
        in_specs += [pl.BlockSpec(memory_space=pl.ANY)] * 2
        aliases = {3: 0, 4: 1}
    return pl.pallas_call(
        functools.partial(dispatch_kernel, local=local),
        out_shape=(shape, shape),
        grid=(count,),
        in_specs=in_specs,
        out_specs=(out_spec, out_spec),
        scratch_shapes=[pltpu.VMEM((rows, rows), BF)],
        input_output_aliases=aliases,
        compiler_params=pltpu.CompilerParams(vmem_limit_bytes=VMEM_LIMIT),
        cost_estimate=pl.CostEstimate(
            flops=4 * count * local * CAP * rows * width, transcendentals=0, bytes_accessed=20 << 20
        ),
        name="dispatch",
    )(*operands)


def expert_kernel(
    x_ref, s_ref, wg_ref, wu_ref, wd_ref,
    pr_ref, dg_ref, dot_ref, grad_ref,
    act_ref, both_ref, acc_in_ref, acc_down_ref,
    *, chunk, tile, last,
):
    rows, width = x_ref.shape[-2:]
    hidden = wg_ref.shape[-1]
    owners = grad_ref.shape[0]
    in_rows, down_rows = width // owners, hidden // owners
    step = pl.program_id(0)

    def chunk_body(c, carry):
        here = tile_ds(c, chunk)
        x = x_ref[0, 0, here, :]
        s = s_ref[0, 0, here, :]
        pre_gate = mm(x, wg_ref[0])
        pre_up = mm(x, wu_ref[0])
        act_grad = mm_nt(s, wd_ref[0])
        logistic = jax.nn.sigmoid(pre_gate)
        swish = pre_gate * logistic
        act = (swish * pre_up).astype(BF)
        gate_in = (
            act_grad * pre_up * logistic * (1.0 + pre_gate * (1.0 - logistic))
        ).astype(BF)
        up_in = (act_grad * swish).astype(BF)
        dot_ref[0, here, :] = jnp.sum(act.astype(F32) * act_grad, axis=1, keepdims=True)
        act_ref[here, :] = act
        both_ref[here, :hidden] = gate_in
        both_ref[here, hidden:] = up_in
        pr_ref[0, here, :] = mm(act, wd_ref[0]).astype(BF)
        dg_ref[0, here, :] = (mm_nt(gate_in, wg_ref[0]) + mm_nt(up_in, wu_ref[0])).astype(BF)
        return carry

    lax.fori_loop(0, rows // chunk, chunk_body, 0)

    def in_body(t, carry):
        here = tile_ds(t, tile)
        part = mm_tn(x_ref[0, 0, :, here], both_ref[...])

        @pl.when(step == 0)
        def _():
            acc_in_ref[here, :] = part

        if last > 1:

            @pl.when((step > 0) & (step < last))
            def _():
                acc_in_ref[here, :] = acc_in_ref[here, :] + part

        @pl.when(step == last)
        def _():
            total = (acc_in_ref[here, :] + part).astype(BF)
            for i in range(tile // in_rows):
                piece = total[i * in_rows : (i + 1) * in_rows]
                owner = t * (tile // in_rows) + i
                grad_ref[owner, :in_rows, :] = piece[:, :hidden]
                grad_ref[owner, in_rows : 2 * in_rows, :] = piece[:, hidden:]

        return carry

    lax.fori_loop(0, width // tile, in_body, 0)

    def down_body(t, carry):
        here = tile_ds(t, tile)
        part = mm_tn(act_ref[:, here], s_ref[0, 0])

        @pl.when(step == 0)
        def _():
            acc_down_ref[here, :] = part

        if last > 1:

            @pl.when((step > 0) & (step < last))
            def _():
                acc_down_ref[here, :] = acc_down_ref[here, :] + part

        @pl.when(step == last)
        def _():
            total = (acc_down_ref[here, :] + part).astype(BF)
            for i in range(tile // down_rows):
                piece = total[i * down_rows : (i + 1) * down_rows]
                owner = t * (tile // down_rows) + i
                for c in range(width // hidden):
                    first = 2 * in_rows + c * down_rows
                    grad_ref[owner, first : first + down_rows, :] = piece[
                        :, c * hidden : (c + 1) * hidden
                    ]

        return carry

    lax.fori_loop(0, hidden // tile, down_body, 0)


def expert(which, owners, rows_in, slot_grad, gate_w, up_w, down_w):
    local, micro, rows, width = rows_in.shape
    hidden = gate_w.shape[2]
    out_shape = (
        jax.ShapeDtypeStruct((micro, rows, width), BF),
        jax.ShapeDtypeStruct((micro, rows, width), BF),
        jax.ShapeDtypeStruct((micro, rows, 1), F32),
        jax.ShapeDtypeStruct((owners, 3 * width // owners, hidden), BF),
    )
    in_spec = pl.BlockSpec((1, 1, rows, width), lambda m: (which, m, 0, 0))
    weight = lambda shape: pl.BlockSpec((1,) + shape, lambda m: (which, 0, 0))
    row_spec = lambda last: pl.BlockSpec((1, rows, last), lambda m: (m, 0, 0))
    return pl.pallas_call(
        functools.partial(expert_kernel, chunk=rows // 3, tile=256, last=micro - 1),
        out_shape=out_shape,
        grid=(micro,),
        in_specs=[in_spec, in_spec, weight((width, hidden)), weight((width, hidden)), weight((hidden, width))],
        out_specs=(
            row_spec(width), row_spec(width), row_spec(1),
            pl.BlockSpec((owners, 3 * width // owners, hidden), lambda m: (0, 0, 0)),
        ),
        scratch_shapes=[
            pltpu.VMEM((rows, hidden), BF),
            pltpu.VMEM((rows, 2 * hidden), BF),
            pltpu.VMEM((width, 2 * hidden), F32),
            pltpu.VMEM((hidden, width), F32),
        ],
        compiler_params=pltpu.CompilerParams(vmem_limit_bytes=VMEM_LIMIT),
        cost_estimate=pl.CostEstimate(
            flops=18 * micro * rows * width * hidden, transcendentals=micro * rows * hidden,
            bytes_accessed=30 << 20,
        ),
        name="expert",
    )(rows_in, slot_grad, gate_w, up_w, down_w)


def combine_kernel(sel_ref, pay_ref, *refs, local, received):
    produced = refs[:local]
    returned = refs[local : 2 * local]
    dots = refs[2 * local : 3 * local]
    rest = refs[3 * local :]
    if received:
        other_ref, rest = rest[0], rest[1:]
    out_refs, upper_ref = rest[:-1], rest[-1]

    @pl.when(pl.program_id(0) == 0)
    def _():
        fill_upper(upper_ref)

    rows = upper_ref.shape[0]
    gates, hits = slot_marks(sel_ref, pay_ref[0], upper_ref, local)
    weighted = jnp.concatenate(
        [jnp.where(h, gates[e : e + 1, :], 0.0).astype(BF) for e, h in enumerate(hits)], axis=0
    )
    plain = jnp.concatenate([jnp.where(h, 1.0, 0.0).astype(BF) for h in hits], axis=0)
    made = jnp.concatenate([r[0, 0] for r in produced], axis=0)
    back = jnp.concatenate([r[0, 0] for r in returned], axis=0)
    out = mm_tn(weighted, made)
    grads = mm_tn(plain, back)
    pad = jnp.zeros((8 - local, rows), F32)
    dot_rows = jnp.concatenate(
        [
            jnp.sum(jnp.where(h, dots[e][0, 0], 0.0), axis=0, keepdims=True)
            for e, h in enumerate(hits)
        ]
        + ([pad] if local < 8 else []),
        axis=0,
    )
    high = dot_rows.astype(BF)
    low = (dot_rows - high.astype(F32)).astype(BF)
    tail = jnp.concatenate([mm_tn(sel_ref[...], high), mm_tn(sel_ref[...], low)], axis=1)
    if received:
        out = out + other_ref[0, :rows, :].astype(F32)
        grads = grads + other_ref[0, rows : 2 * rows, :].astype(F32)
        tail = tail + other_ref[0, 2 * rows :, :].astype(F32)
    def put(ref, at):
        ref[at, :rows, :] = out.astype(BF)
        ref[at, rows : 2 * rows, :] = grads.astype(BF)
        ref[at, 2 * rows :, :] = tail.astype(BF)

    if len(out_refs) == 1:
        put(out_refs[0], 0)
    else:
        for index, ref in enumerate(out_refs):
            pl.when(pl.program_id(0) == index)(functools.partial(put, ref, 0))


def combine(sel, pays, produced, returned, dots, micro, side, other):
    count, total_rows, width = pays.shape
    local = len(produced)
    experts = sel.shape[1]
    rows = total_rows - experts
    pick = lambda last: pl.BlockSpec((1, 1, CAP, last), lambda s: (micro, side * count + s, 0, 0))
    in_specs = [
        pl.BlockSpec(sel.shape, lambda s: (0, 0)),
        pl.BlockSpec((1, experts, width), lambda s: (s, rows // experts, 0)),
    ]
    in_specs += [pick(width)] * (2 * local) + [pick(1)] * local
    operands = [sel, pays, *produced, *returned, *dots]
    out_spec = pl.BlockSpec((1, 2 * rows + experts, width), lambda s: (s, 0, 0))
    out_shape = (jax.ShapeDtypeStruct((count, 2 * rows + experts, width), BF),)
    out_specs = (out_spec,)
    if other is not None:
        operands.append(other)
        in_specs.append(out_spec)
        out_shape = (jax.ShapeDtypeStruct((1, 2 * rows + experts, width), BF),) * count
        out_specs = (pl.BlockSpec((1, 2 * rows + experts, width), lambda s: (0, 0, 0)),) * count
    return pl.pallas_call(
        functools.partial(combine_kernel, local=local, received=other is not None),
        out_shape=out_shape,
        grid=(count,),
        in_specs=in_specs,
        out_specs=out_specs,
        scratch_shapes=[pltpu.VMEM((rows, rows), BF)],
        compiler_params=pltpu.CompilerParams(vmem_limit_bytes=VMEM_LIMIT),
        cost_estimate=pl.CostEstimate(
            flops=4 * count * local * CAP * rows * width, transcendentals=0, bytes_accessed=20 << 20
        ),
        name="combine",
    )(*operands)


def attention_backward_kernel(
    *refs, terms, q_width, kv_width, experts, carried,
):
    (
        x_ref, w_ref, gain_one_ref, gain_two_ref, id_row_ref, id_col_ref, cos_ref, sin_ref,
        grad_ref, q_ref, k_ref, v_ref, att_ref, lse_ref, res_ref, pay_ref, gate_ref,
    ) = refs[:17]
    term_refs = refs[17 : 17 + terms]
    rest = refs[17 + terms :]
    if carried:
        prior_ref, rest = rest[0], rest[1:]
    out_ref, in_grad_ref, pack_ref, bias_ref, wide_ref, att_grad_ref, qkv_grad_ref, branch_ref, normed_ref = rest
    rows, width = x_ref.shape
    step = 256
    start = q_width + 2 * kv_width

    def put(row_slice, cols, value):
        if carried:
            value = value + prior_ref[row_slice, cols].astype(F32)
        pack_ref[row_slice, cols] = value.astype(BF)

    def gathered(low, high):
        total = term_refs[0][low:high, :].astype(F32)
        for ref in term_refs[1:]:
            total = total + ref[low:high, :].astype(F32)
        return total

    residual = res_ref[...]
    out_ref[...] = (residual + RESIDUAL_SCALE * gathered(0, rows)).astype(BF)
    tail = gathered(2 * rows, 2 * rows + experts)
    weighted = tail[:, :rows] + tail[:, rows:]
    chosen = weighted - gate_ref[...] * jnp.sum(weighted, axis=0, keepdims=True)
    chosen = jnp.concatenate([chosen, jnp.zeros((LANES - experts, rows), F32)], axis=0)
    logit_grad = chosen.T.astype(BF)
    moe_grad = gathered(rows, 2 * rows) + mm_nt(logit_grad, w_ref[:, start + width :])
    last = mm_tn(pay_ref[:rows, :], logit_grad)
    scale = lax.rsqrt(jnp.mean(residual * residual, axis=1, keepdims=True) + EPS)
    gain_two_grad = jnp.sum(moe_grad * residual * scale, axis=0, keepdims=True)
    u = moe_grad * gain_two_ref[...]
    inner = jnp.sum(u * residual, axis=1, keepdims=True) * (1.0 / width)
    res_grad = grad_ref[...].astype(F32) + scale * u - residual * (scale * scale * scale * inner)
    in_grad_ref[...] = res_grad
    branch_ref[...] = (RESIDUAL_SCALE * res_grad).astype(BF)
    bias_ref[...] = jnp.where(id_col_ref[...] <= id_row_ref[...], 0.0, NEG_FILL)

    def branch_body(j, carry):
        here = tile_ds(j, step)
        att_grad_ref[:, here] = mm_nt(
            branch_ref[...], w_ref[here, start : start + width]
        ).astype(BF)
        part = mm_tn(att_ref[:, here], branch_ref[...])
        put(here, slice(start, start + width), part)
        return carry

    lax.fori_loop(0, q_width // step, branch_body, 0)

    lower = lane_iota((rows, LANES)) < HEAD_SIZE

    def pair_body(j, carry):
        k_block = k_ref[:, tile_ds(j, LANES)].astype(F32)
        v_block = v_ref[:, tile_ds(j, LANES)].astype(F32)
        k_sums, v_sums = [], []
        for place in range(2):
            keys = [h.astype(BF) for h in head_pair(k_block, place)]
            vals = [h.astype(BF) for h in head_pair(v_block, place)]
            group = 2 * j + place
            here = tile_ds(group, LANES)
            q_block = q_ref[:, here]
            g_block = att_grad_ref[:, here]
            q_out = None
            k_parts, v_parts = [], []
            for side in range(2):
                scores = mm_nt(keys[side], q_block) * SCORE_SCALE + bias_ref[...]
                probs = jnp.exp(scores - lse_ref[pl.ds(2 * group + side, 1), :])
                weight_grad = mm_nt(vals[side], g_block)
                v_parts.append(mm(probs.astype(BF), g_block))
                dots = jnp.sum(probs * weight_grad, axis=0, keepdims=True)
                score_grad = (probs * (weight_grad - dots)).astype(BF)
                k_parts.append(mm(score_grad, q_block))
                part = mm_tn(keys[side], score_grad)
                q_out = part if q_out is None else q_out + part
            q_turned = turn(q_out.T * SCORE_SCALE, cos_ref[...], -sin_ref[...])
            qkv_grad_ref[:, here] = q_turned.astype(BF)
            for parts, sums in ((k_parts, k_sums), (v_parts, v_sums)):
                mixed = jnp.where(lower, parts[0], parts[1])
                sums.append(mixed + pltpu.roll(mixed, HEAD_SIZE, 1))
        k_total = jnp.where(lower, k_sums[0], k_sums[1]) * SCORE_SCALE
        v_total = jnp.where(lower, v_sums[0], v_sums[1])
        k_here = pl.ds(pl.multiple_of(q_width + j * LANES, LANES), LANES)
        v_here = pl.ds(pl.multiple_of(q_width + kv_width + j * LANES, LANES), LANES)
        qkv_grad_ref[:, k_here] = turn(k_total, cos_ref[...], -sin_ref[...]).astype(BF)
        qkv_grad_ref[:, v_here] = v_total.astype(BF)
        return carry

    lax.fori_loop(0, KEY_VALUE_HEADS // 2, pair_body, 0)

    x = x_ref[...].astype(F32)
    scale = lax.rsqrt(jnp.mean(x * x, axis=1, keepdims=True) + EPS)
    normed_ref[...] = (x * scale * gain_one_ref[...]).astype(BF)

    def norm_body(j, carry):
        here = tile_ds(j, step)
        grad = mm_nt(qkv_grad_ref[...], w_ref[here, :start])
        put(here, slice(0, start), mm_tn(normed_ref[:, here], qkv_grad_ref[...]))
        wide_ref[:, here] = grad
        return carry

    lax.fori_loop(0, width // step, norm_body, 0)
    normed_grad = wide_ref[...]
    gain_one_grad = jnp.sum(normed_grad * x * scale, axis=0, keepdims=True)
    u = normed_grad * gain_one_ref[...]
    inner = jnp.sum(u * x, axis=1, keepdims=True) * (1.0 / width)
    in_grad_ref[...] = in_grad_ref[...] + scale * u - x * (scale * scale * scale * inner)
    lanes = lane_iota((width, LANES))
    one = jnp.broadcast_to(gain_one_grad, (LANES, width)).T
    two = jnp.broadcast_to(gain_two_grad, (LANES, width)).T
    last = jnp.where(lanes == experts, one, last)
    last = jnp.where(lanes == experts + 1, two, last)
    put(slice(0, width), slice(start + width, start + width + LANES), last)


def attention_backward(
    x, pack, gain_one, gain_two, ids, tables, grad, saved, terms, prior, q_width, kv_width, experts
):
    rows, width = x.shape
    operands = [x, pack, gain_one, gain_two, ids[None, :], ids[:, None], *tables, grad, *saved, *terms]
    if prior is not None:
        operands.append(prior)
    flops = 4 * rows * width * (q_width + 2 * kv_width + width) + 20 * QUERY_HEADS * rows * rows * 128
    return pl.pallas_call(
        functools.partial(
            attention_backward_kernel, terms=len(terms), q_width=q_width, kv_width=kv_width,
            experts=experts, carried=prior is not None,
        ),
        out_shape=(
            jax.ShapeDtypeStruct((rows, width), BF),
            jax.ShapeDtypeStruct((rows, width), F32),
            jax.ShapeDtypeStruct(pack.shape, BF),
        ),
        scratch_shapes=[
            pltpu.VMEM((rows, rows), F32),
            pltpu.VMEM((rows, width), F32),
            pltpu.VMEM((rows, q_width), BF),
            pltpu.VMEM((rows, q_width + 2 * kv_width), BF),
            pltpu.VMEM((rows, width), BF),
            pltpu.VMEM((rows, width), BF),
        ],
        compiler_params=pltpu.CompilerParams(vmem_limit_bytes=VMEM_LIMIT),
        cost_estimate=pl.CostEstimate(
            flops=flops, transcendentals=QUERY_HEADS * rows * rows, bytes_accessed=40 << 20
        ),
        name="attention_backward",
    )(*operands)


def swap(value, distance, size):
    return lax.ppermute(value, "fsdp", [(i, i ^ distance) for i in range(size)])


def local(
    inputs, block_ids, routes, out_grad, norm_gain, w_query, key_weight, value_weight, w_output,
    moe_gain, w_router, w_gate, w_up, w_down,
):
    micro, _, rows, width = inputs.shape
    experts = w_router.shape[1]
    held = w_gate.shape[0]
    hidden = w_gate.shape[2]
    q_width, kv_width = w_query.shape[1], key_weight.shape[1]
    owners = lax.axis_size("fsdp")
    parts = lax.axis_size("dp")
    chips = owners // 2
    tables = tuple(jnp.asarray(t) for t in rope_tables(rows))
    start = q_width + 2 * kv_width + width

    def gather_peers(value):
        mine = jnp.stack([value] + [swap(value, 2 * r, owners) for r in range(1, chips)])
        return mine, swap(mine, 1, owners)

    pieces = [
        w_query, key_weight, value_weight, w_output, w_router, norm_gain[:, None], moe_gain[:, None]
    ]
    filled = sum(p.shape[1] for p in pieces)
    pieces.append(jnp.zeros((w_query.shape[0], start + LANES - filled), BF))
    pack = lax.all_gather(
        jnp.concatenate(pieces, axis=1), ("fsdp", "dp"), axis=0, tiled=True
    )
    gain_one = pack[:, start + experts].astype(F32)[None, :]
    gain_two = pack[:, start + experts + 1].astype(F32)[None, :]
    gate_w = lax.all_gather(w_gate, "dp", axis=1, tiled=True)
    up_w = lax.all_gather(w_up, "dp", axis=1, tiled=True)
    down_w = lax.all_gather(w_down, "dp", axis=1, tiled=True)
    grads = [gather_peers(out_grad[m, 0]) for m in range(micro)]
    first = lax.axis_index("fsdp") * held
    places = jnp.arange(8)[:, None]
    sel = ((jnp.arange(experts)[None, :] == first + places) & (places < held)).astype(BF)

    saved, pays = [], []
    for m in range(micro):
        x = inputs[m, 0]
        q, k, v, att, lse, res, pay, gates = attention_forward(
            x, pack, gain_one, gain_two, block_ids[m, 0], routes[m, 0], tables, q_width, kv_width, experts
        )
        saved.append((q, k, v, att, lse, res, pay, gates))
        pays.append(gather_peers(pay))
    carried = None
    for m in range(micro):
        for side in range(2):
            carried = dispatch(
                sel, pays[m][side], grads[m][side], m * 2 + side, micro * 2, held, carried
            )
    flat = (held, micro * chips // 4, 8 * CAP, width)
    rows_in, slot_grad = carried[0].reshape(flat), carried[1].reshape(flat)
    produced, returned, dots, weight_sums = [], [], [], []
    for e in range(held):
        pr, dg, dot, weight = expert(e, parts, rows_in, slot_grad, gate_w, up_w, down_w)
        split = (micro, 2 * chips, CAP)
        produced.append(pr.reshape(split + (width,)))
        returned.append(dg.reshape(split + (width,)))
        dots.append(dot.reshape(split + (1,)))
        weight_sums.append(
            lax.psum_scatter(weight, "dp", scatter_dimension=0, tiled=True)[0]
        )
    others = []
    for m in range(micro):
        (sent,) = combine(sel, pays[m][1], produced, returned, dots, m, 1, None)
        others.append(swap(sent, 1, owners))
    outputs, input_grads = [], []
    prior = None
    for m in range(micro):
        kept = combine(sel, pays[m][0], produced, returned, dots, m, 0, others[m])
        terms = [kept[0][0]] + [swap(kept[r][0], 2 * r, owners) for r in range(1, chips)]
        out, in_grad, prior = attention_backward(
            inputs[m, 0], pack, gain_one, gain_two, block_ids[m, 0], tables, out_grad[m, 0], saved[m],
            terms, prior, q_width, kv_width, experts,
        )
        outputs.append(out)
        input_grads.append(in_grad)
    layer = lax.psum_scatter(prior, ("fsdp", "dp"), scatter_dimension=0, tiled=True).astype(F32)
    marks = np.cumsum([0, q_width, kv_width, kv_width, width, experts, 1, 1])
    cut = [layer[:, a:b] for a, b in zip(marks[:-1], marks[1:])]
    in_rows, down_rows = width // parts, hidden // parts
    stacked = jnp.stack(weight_sums).astype(F32)
    grad_down = stacked[:, 2 * in_rows :].reshape(held, width // hidden, down_rows, hidden)
    grad_down = grad_down.transpose(0, 2, 1, 3).reshape(held, down_rows, width)
    return (
        jnp.stack(outputs)[:, None],
        jnp.stack(input_grads)[:, None],
        cut[5][:, 0], cut[0], cut[1], cut[2], cut[3], cut[6][:, 0], cut[4],
        stacked[:, :in_rows], stacked[:, in_rows : 2 * in_rows], grad_down,
    )


def solution(mesh):
    rows = ("fsdp", "dp")
    split = lambda rank: P(None, rows, *([None] * (rank - 2)))
    flat = P(rows, None)
    expert_spec = P("fsdp", "dp", None)
    in_specs = (
        split(4), split(3), split(4), split(4), P(rows), flat, flat, flat, flat, P(rows), flat,
        expert_spec, expert_spec, expert_spec,
    )
    out_specs = (
        split(4), split(4), P(rows), flat, flat, flat, flat, P(rows), flat,
        expert_spec, expert_spec, expert_spec,
    )
    return jax.shard_map(local, mesh=mesh, in_specs=in_specs, out_specs=out_specs, check_vma=False)
```

time: 2410 us -> 925 us (0.38)
  waiting for transfers between devices: 1020 us -> 472 us
  matrix products: 433 us -> 0 us
  local copies, waits for them, and re-layouts: 440 us -> 22.8 us
  Pallas kernels: 0 us -> 362 us
  blocking collectives: 261 us -> 0 us
  other arithmetic: 184 us -> 22.4 us
    reduce_scatter x8 -> x5, waiting for transfers between devices: 604 us -> 148 us  [the longest x1 148 us: local(): lax.psum_scatter(prior, ('fsdp', 'dp'), scatter_dimension=0, tiled=True)]
    dot_general x160 -> x0, matrix products: 433 us -> none  [the longest x2 37.2 us: expert_revert(): jnp.einsum(lead + 'cd,efd->' + lead + 'cf', slot_grad, down_w, preferred_...]
    pallas_call x0 -> x16, Pallas kernels: none -> 362 us  [the longest x4 140 us: expert(): pl.pallas_call(functools.partial(expert_kernel, chunk=rows // 3, tile=256...]
    all_to_all x7 -> x0, waiting for transfers between devices: 356 us -> none  [the longest x2 109 us: local(): lax.all_to_all(slot_grad.reshape(owners, local_experts, CAP, feature_widt...]
    gather x14 -> x0, local copies, waits for them, and re-layouts: 253 us -> none  [the longest x6 67.7 us: route_gates(): chosen = jnp.take_along_axis(logits, picks, axis=1)]
    ppermute x0 -> x24, waiting for transfers between devices: none -> 226 us  [swap(): return lax.ppermute(value, 'fsdp', [(i, i ^ distance) for i in range(size)])]
    all_to_all x1 -> x0, blocking collectives: 109 us -> none  [local(): lax.all_to_all(dispatch.reshape(owners, local_experts, CAP, feature_width...]
    unnamed x2 -> x0, blocking collectives: 79.2 us -> none
  transfers between devices with their start and end apart: 22 -> 33, of which waited for: 13 -> 15; matrix products, arithmetic and copies ran while one was open for 35% -> 4% of each run, Pallas kernels for 0% -> 36%
where the time goes in v1:
time: 925 us; the launch traced here: 922 us
  waiting for transfers between devices  472 us (51%)
  Pallas kernels  362 us (39%)
  starting transfers between devices  27.5 us (3%)
  local copies, waits for them, and re-layouts  22.8 us (2%)
  other arithmetic  22.4 us (2%)
  between operations  14.2 us (2%)
    ppermute x24, waiting for transfers between devices, swap(): return lax.ppermute(value, 'fsdp', [(i, i ^ distance) for i in range(size)])  226 us
    reduce_scatter x1, waiting for transfers between devices, local(): lax.psum_scatter(prior, ('fsdp', 'dp'), scatter_dimension=0, tiled=True)  148 us
    pallas_call x4, Pallas kernels, expert(): pl.pallas_call(functools.partial(expert_kernel, chunk=rows // 3, tile=256...  140 us
    pallas_call x2, Pallas kernels, attention_backward(): pl.pallas_call(functools.partial(attention_backward_kernel, terms=len(ter...  78.3 us
    all_gather x1, waiting for transfers between devices, local(): lax.all_gather(jnp.concatenate(pieces, axis=1), ('fsdp', 'dp'), axis=0, t...  68.6 us
    pallas_call x4, Pallas kernels, combine(): pl.pallas_call(functools.partial(combine_kernel, local=local, received=ot...  56.7 us
    pallas_call x2, Pallas kernels, attention_forward(): pl.pallas_call(functools.partial(attention_forward_kernel, q_width=q_widt...  43.8 us
    pallas_call x4, Pallas kernels, dispatch(): pl.pallas_call(functools.partial(dispatch_kernel, local=local), out_shape...  43.5 us
  transfers between devices with their start and end apart: 33, of which 15 were waited for; matrix products, arithmetic and copies ran while one was open for 4% of the time, Pallas kernels for 36%

profile of v1, /device:TPU:0, one launch (start us, length us, event | category | flops | bytes accessed | tf_op | source)
XLA Modules:
  0.0 921.8 jit_solution(7778607630003156903)
XLA Ops:
  26.0 68.6 %all-gather.5.cloned.1.call-done.w_ref.refs_1_ = bf16[1024,3200]{1,0:T(8,128)(2,1)} async-done(((bf16[32,3200]{1,0:T(8,128)(2,1)}), bf16[1024,3200]{1,0:T(8,128)(2,1)}) %all-gather.5.cloned.1.call-update) | async-done | bytes 6553616 | tf_op jit(solution)/shard_map/all_gather | solution.py:658
  96.6 22.0 %attention_forward.2 = (bf16[512,1024]{1,0:T(8,128)(2,1)}, bf16[512,512]{1,0:T(8,128)(2,1)}, bf16[512,512]{1,0:T(8,128)(2,1)}, bf16[512,1024]{1,0:T(8,128)(2,1)}...) custom-call(bf16[512,1024]{1,0:T(8,128)(2,1)} %get-tuple-element.155.x_ref.refs_0_, ...), custom_call_target="tpu_custom_call" | custom-call | flops 7516192768 | bytes 16777216 | tf_op jit(solution)/shard_map/attention_forward/pallas_call | solution.py:172
  120.9 21.8 %attention_forward.3 = (bf16[512,1024]{1,0:T(8,128)(2,1)}, bf16[512,512]{1,0:T(8,128)(2,1)}, bf16[512,512]{1,0:T(8,128)(2,1)}, bf16[512,1024]{1,0:T(8,128)(2,1)}...) custom-call(bf16[512,1024]{1,0:T(8,128)(2,1)} %get-tuple-element.156.x_ref.refs_0_, ...), custom_call_target="tpu_custom_call" | custom-call | flops 7516192768 | bytes 16777216 | tf_op jit(solution)/shard_map/attention_forward/pallas_call | solution.py:172
  149.1 21.4 %collective-permute-done = bf16[544,1024]{1,0:T(8,128)(2,1)} collective-permute-done((bf16[544,1024]{1,0:T(8,128)(2,1)}, bf16[544,1024]{1,0:T(8,128)(2,1)}, u32[]{:S(2)}, u32[]{:S(2)}) %collective-permute-start) | collective-permute-done | bytes 1114144 | tf_op jit(solution)/shard_map/ppermute | solution.py:631
  173.2 21.1 %collective-permute-done.3 = bf16[544,1024]{1,0:T(8,128)(2,1)S(1)} collective-permute-done((bf16[544,1024]{1,0:T(8,128)(2,1)}, bf16[544,1024]{1,0:T(8,128)(2,1)S(1)}, u32[]{:S(2)}, u32[]{:S(2)}) %collective-permute-start.3) | collective-permute-done | bytes 1114144 | tf_op jit(solution)/shard_map/ppermute | solution.py:631
  200.9 17.3 %collective-permute-done.4 = bf16[544,1024]{1,0:T(8,128)(2,1)S(1)} collective-permute-done((bf16[544,1024]{1,0:T(8,128)(2,1)}, bf16[544,1024]{1,0:T(8,128)(2,1)S(1)}, u32[]{:S(2)}, u32[]{:S(2)}) %collective-permute-start.4) | collective-permute-done | bytes 1114144 | tf_op jit(solution)/shard_map/ppermute | solution.py:631
  224.7 16.0 %collective-permute-done.7 = bf16[512,1024]{1,0:T(8,128)(2,1)S(1)} collective-permute-done((bf16[512,1024]{1,0:T(8,128)(2,1)}, bf16[512,1024]{1,0:T(8,128)(2,1)S(1)}, u32[]{:S(2)}, u32[]{:S(2)}) %collective-permute-start.7) | collective-permute-done | bytes 1048608 | tf_op jit(solution)/shard_map/ppermute | solution.py:631
  241.2 21.8 %collective-permute-done.9 = bf16[512,1024]{1,0:T(8,128)(2,1)S(1)} collective-permute-done((bf16[512,1024]{1,0:T(8,128)(2,1)}, bf16[512,1024]{1,0:T(8,128)(2,1)S(1)}, u32[]{:S(2)}, u32[]{:S(2)}) %collective-permute-start.9) | collective-permute-done | bytes 1048608 | tf_op jit(solution)/shard_map/ppermute | solution.py:631
  266.0 10.9 %dispatch.4 = (bf16[4,4,4,144,1024]{4,3,2,1,0:T(8,128)(2,1)}, bf16[4,4,4,144,1024]{4,3,2,1,0:T(8,128)(2,1)}) custom-call(bf16[8,32]{1,0:T(8,128)(2,1)} %fusion.1.sel_ref, bf16[4,544,1024]{2,1,0:T(8,128)(2,1)} %pad_maximum_fusion.pay_ref, bf16[4,512,1024]{2,1,0:T(8,128)(2,1)} %pad_maximum_fusion.3.grad_ref), custom_call_target="tpu_custom_call" | custom-call | flops 4831838208 | bytes 20971520 | tf_op jit(solution)/shard_map/dispatch/pallas_call | solution.py:243
  309.6 27.7 %all-gather.9.cloned.1.call-done.wu_ref = bf16[4,1024,512]{2,1,0:T(8,128)(2,1)} async-done(((bf16[4,256,512]{2,1,0:T(8,128)(2,1)}), bf16[4,1024,512]{2,1,0:T(8,128)(2,1)}) %all-gather.9.cloned.1.call-update) | async-done | bytes 4194320 | tf_op jit(solution)/shard_map/all_gather | solution.py:664
  337.3 34.9 %expert.7 = (bf16[2,1152,1024]{2,1,0:T(8,128)(2,1)}, bf16[2,1152,1024]{2,1,0:T(8,128)(2,1)}, f32[2,1152,1]{2,1,0:T(8,128)}, bf16[4,768,512]{2,1,0:T(8,128)(2,1)}) custom-call(bf16[4,2,1152,1024]{3,2,1,0:T(8,128)(2,1)} %bitcast.79, bf16[4,2,1152,1024]{3,2,1,0:T(8,128)(2,1)} %bitcast.83, bf16[4,1024,512]{2,1,0:T(8,128)(2,1)} %all-gather.7.cloned.1.call-done.wg_ref, ...), custom_call_target="tpu_custom_call" | custom-call | flops 21743271936 | bytes 31457280 | tf_op jit(solution)/shard_map/expert/pallas_call | solution.py:365
  372.3 35.0 %expert.6 = (bf16[2,1152,1024]{2,1,0:T(8,128)(2,1)}, bf16[2,1152,1024]{2,1,0:T(8,128)(2,1)}, f32[2,1152,1]{2,1,0:T(8,128)}, bf16[4,768,512]{2,1,0:T(8,128)(2,1)}) custom-call(bf16[4,2,1152,1024]{3,2,1,0:T(8,128)(2,1)} %bitcast.80, bf16[4,2,1152,1024]{3,2,1,0:T(8,128)(2,1)} %bitcast.84, bf16[4,1024,512]{2,1,0:T(8,128)(2,1)} %all-gather.7.cloned.1.call-done.wg_ref, ...), custom_call_target="tpu_custom_call" | custom-call | flops 21743271936 | bytes 31457280 | tf_op jit(solution)/shard_map/expert/pallas_call | solution.py:365
  407.4 35.2 %expert.5 = (bf16[2,1152,1024]{2,1,0:T(8,128)(2,1)}, bf16[2,1152,1024]{2,1,0:T(8,128)(2,1)}, f32[2,1152,1]{2,1,0:T(8,128)}, bf16[4,768,512]{2,1,0:T(8,128)(2,1)}) custom-call(bf16[4,2,1152,1024]{3,2,1,0:T(8,128)(2,1)} %bitcast.81, bf16[4,2,1152,1024]{3,2,1,0:T(8,128)(2,1)} %bitcast.85, bf16[4,1024,512]{2,1,0:T(8,128)(2,1)} %all-gather.7.cloned.1.call-done.wg_ref, ...), custom_call_target="tpu_custom_call" | custom-call | flops 21743271936 | bytes 31457280 | tf_op jit(solution)/shard_map/expert/pallas_call | solution.py:365
  442.6 35.1 %expert.4 = (bf16[2,1152,1024]{2,1,0:T(8,128)(2,1)}, bf16[2,1152,1024]{2,1,0:T(8,128)(2,1)}, f32[2,1152,1]{2,1,0:T(8,128)}, bf16[4,768,512]{2,1,0:T(8,128)(2,1)}) custom-call(bf16[4,2,1152,1024]{3,2,1,0:T(8,128)(2,1)} %bitcast.82, bf16[4,2,1152,1024]{3,2,1,0:T(8,128)(2,1)} %bitcast.86, bf16[4,1024,512]{2,1,0:T(8,128)(2,1)} %all-gather.7.cloned.1.call-done.wg_ref, ...), custom_call_target="tpu_custom_call" | custom-call | flops 21743271936 | bytes 31457280 | tf_op jit(solution)/shard_map/expert/pallas_call | solution.py:365
  477.6 12.2 %combine.4 = bf16[4,1056,1024]{2,1,0:T(8,128)(2,1)} custom-call(bf16[8,32]{1,0:T(8,128)(2,1)} %fusion.1.sel_ref, bf16[4,544,1024]{2,1,0:T(8,128)(2,1)} %collective-permute-done.11.pay_ref, bf16[2,8,144,1024]{3,2,1,0:T(8,128)(2,1)} %bitcast.111, bf16[2,8,144,1024]{3,2,1,0:T(8,128)(2,1)} %bitcast.103, bf16[2,8,144,1024]{3,2,1,0:T(8,128)(2,1)} %bitcast.95, ...), custom_call_target="tpu_custom_call" | custom-call | flops 4831838208 | bytes 20971520 | tf_op jit(solution)/shard_map/combine/pallas_call | solution.py:460
  490.0 12.2 %combine.6 = bf16[4,1056,1024]{2,1,0:T(8,128)(2,1)} custom-call(bf16[8,32]{1,0:T(8,128)(2,1)} %fusion.1.sel_ref, bf16[4,544,1024]{2,1,0:T(8,128)(2,1)} %collective-permute-done.6.pay_ref, bf16[2,8,144,1024]{3,2,1,0:T(8,128)(2,1)} %bitcast.112, bf16[2,8,144,1024]{3,2,1,0:T(8,128)(2,1)} %bitcast.104, bf16[2,8,144,1024]{3,2,1,0:T(8,128)(2,1)} %bitcast.96, ...), custom_call_target="tpu_custom_call" | custom-call | flops 4831838208 | bytes 20971520 | tf_op jit(solution)/shard_map/combine/pallas_call | solution.py:460
  503.8 16.2 %combine.5 = (bf16[1,1056,1024]{2,1,0:T(8,128)(2,1)}, bf16[1,1056,1024]{2,1,0:T(8,128)(2,1)}, bf16[1,1056,1024]{2,1,0:T(8,128)(2,1)}, bf16[1,1056,1024]{2,1,0:T(8,128)(2,1)}) custom-call(bf16[8,32]{1,0:T(8,128)(2,1)} %fusion.1.sel_ref, bf16[4,544,1024]{2,1,0:T(8,128)(2,1)} %pad_maximum_fusion.pay_ref, bf16[2,8,144,1024]{3,2,1,0:T(8,128)(2,1)} %bitcast.113, ...), custom_call_target="tpu_custom_call" | custom-call | flops 4831838208 | bytes 20971520 | tf_op jit(solution)/shard_map/combine/pallas_call | solution.py:460
  523.6 16.0 %combine.7 = (bf16[1,1056,1024]{2,1,0:T(8,128)(2,1)}, bf16[1,1056,1024]{2,1,0:T(8,128)(2,1)}, bf16[1,1056,1024]{2,1,0:T(8,128)(2,1)}, bf16[1,1056,1024]{2,1,0:T(8,128)(2,1)}) custom-call(bf16[8,32]{1,0:T(8,128)(2,1)} %fusion.1.sel_ref, bf16[4,544,1024]{2,1,0:T(8,128)(2,1)} %pad_maximum_fusion.1.pay_ref, bf16[2,8,144,1024]{3,2,1,0:T(8,128)(2,1)} %bitcast.114, ...), custom_call_target="tpu_custom_call" | custom-call | flops 4831838208 | bytes 20971520 | tf_op jit(solution)/shard_map/combine/pallas_call | solution.py:460
  542.7 27.6 %collective-permute-done.17.refs_18_ = bf16[1056,1024]{1,0:T(8,128)(2,1)} collective-permute-done((bf16[1056,1024]{1,0:T(8,128)(2,1)}, bf16[1056,1024]{1,0:T(8,128)(2,1)}, u32[]{:S(2)}, u32[]{:S(2)}) %collective-permute-start.17) | collective-permute-done | bytes 2162720 | tf_op jit(solution)/shard_map/ppermute | solution.py:631
  572.7 45.4 %collective-permute-done.18.refs_19_ = bf16[1056,1024]{1,0:T(8,128)(2,1)} collective-permute-done((bf16[1056,1024]{1,0:T(8,128)(2,1)}, bf16[1056,1024]{1,0:T(8,128)(2,1)}, u32[]{:S(2)}, u32[]{:S(2)}) %collective-permute-start.18) | collective-permute-done | bytes 2162720 | tf_op jit(solution)/shard_map/ppermute | solution.py:631
  618.1 38.3 %attention_backward.2 = (bf16[512,1024]{1,0:T(8,128)(2,1)}, f32[512,1024]{1,0:T(8,128)}, bf16[1024,3200]{1,0:T(8,128)(2,1)}) custom-call(bf16[512,1024]{1,0:T(8,128)(2,1)} %get-tuple-element.155.x_ref.refs_0_, bf16[1024,3200]{1,0:T(8,128)(2,1)} %all-gather.5.cloned.1.call-done.w_ref.refs_1_, f32[1,1024]{1,0:T(1,128)} %bitcast.157, f32[1,1024]{1,0:T(1,128)} %bitcast.153, ...), custom_call_target="tpu_custom_call" | custom-call | flops 17179869184 | bytes 41943040 | tf_op jit(solution)/shard_map/attention_backward/pallas_call | solution.py:604
  663.0 46.7 %collective-permute-done.22.refs_19_ = bf16[1056,1024]{1,0:T(8,128)(2,1)} collective-permute-done((bf16[1056,1024]{1,0:T(8,128)(2,1)}, bf16[1056,1024]{1,0:T(8,128)(2,1)}, u32[]{:S(2)}, u32[]{:S(2)}) %collective-permute-start.22) | collective-permute-done | bytes 2162720 | tf_op jit(solution)/shard_map/ppermute | solution.py:631
  709.7 39.9 %attention_backward.3 = (bf16[512,1024]{1,0:T(8,128)(2,1)}, f32[512,1024]{1,0:T(8,128)}, bf16[1024,3200]{1,0:T(8,128)(2,1)}) custom-call(bf16[512,1024]{1,0:T(8,128)(2,1)} %get-tuple-element.156.x_ref.refs_0_, bf16[1024,3200]{1,0:T(8,128)(2,1)} %all-gather.5.cloned.1.call-done.w_ref.refs_1_, f32[1,1024]{1,0:T(1,128)} %bitcast.158, f32[1,1024]{1,0:T(1,128)} %bitcast.154, ...), custom_call_target="tpu_custom_call" | custom-call | flops 17179869184 | bytes 41943040 | tf_op jit(solution)/shard_map/attention_backward/pallas_call | solution.py:604
  760.9 148.2 %reduce-scatter.6.cloned.1.call-done = bf16[32,3200]{1,0:T(8,128)(2,1)} async-done(((bf16[1024,3200]{1,0:T(8,128)(2,1)}), bf16[32,3200]{1,0:T(8,128)(2,1)}) %reduce-scatter.6.cloned.1.call-update) | async-done | bytes 204816 | tf_op jit(solution)/shard_map/reduce_scatter | solution.py:712
  (117 shorter events, 115.9 us)
Async XLA Ops:
  7.2 87.4 %all-gather.5.cloned.1.call-start = ((), (), s32[]{:S(2)}) async-start(), calls=%async_computation.5 | async-start | bytes 6758400 | tf_op jit(solution)/shard_map/all_gather | solution.py:658
  10.6 299.0 %all-gather.11.cloned.1.call-start = ((), (), s32[]{:S(2)}) async-start(), calls=%async_computation.8 | async-start | bytes 5242880 | tf_op jit(solution)/shard_map/all_gather | solution.py:665
  11.3 298.2 %all-gather.7.cloned.1.call-start = ((), (), s32[]{:S(2)}) async-start(), calls=%async_computation.6 | async-start | bytes 5242880 | tf_op jit(solution)/shard_map/all_gather | solution.py:663
  12.1 325.2 %all-gather.9.cloned.1.call-start = ((), (), s32[]{:S(2)}) async-start(), calls=%async_computation.7 | async-start | bytes 5242880 | tf_op jit(solution)/shard_map/all_gather | solution.py:664
  14.4 128.3 %collective-permute-start.12 = (bf16[512,1024]{1,0:T(8,128)(2,1)}, bf16[512,1024]{1,0:T(8,128)(2,1)}, u32[]{:S(2)}, u32[]{:S(2)}) collective-permute-start(bf16[512,1024]{1,0:T(8,128)(2,1)} %get-tuple-element.154.refs_8_), channel_id=1, source_target_pairs={{0,8},{4,12},{8,0},{12,4},{16,24},{20,28},{24,16},{28,20},{1,9},{5... | collective-permute-start | bytes 3145736 | tf_op jit(solution)/shard_map/ppermute | solution.py:631
  17.4 126.6 %collective-permute-start.13 = (bf16[512,1024]{1,0:T(8,128)(2,1)}, bf16[512,1024]{1,0:T(8,128)(2,1)}, u32[]{:S(2)}, u32[]{:S(2)}) collective-permute-start(bf16[512,1024]{1,0:T(8,128)(2,1)} %get-tuple-element.154.refs_8_), channel_id=1, source_target_pairs={{0,16},{4,20},{8,24},{12,28},{16,0},{20,4},{24,8},{28,12},{1,17},{... | collective-permute-start | bytes 3145736 | tf_op jit(solution)/shard_map/ppermute | solution.py:631
  18.9 126.6 %collective-permute-start.14 = (bf16[512,1024]{1,0:T(8,128)(2,1)}, bf16[512,1024]{1,0:T(8,128)(2,1)}, u32[]{:S(2)}, u32[]{:S(2)}) collective-permute-start(bf16[512,1024]{1,0:T(8,128)(2,1)} %get-tuple-element.154.refs_8_), channel_id=1, source_target_pairs={{0,24},{4,28},{8,16},{12,20},{16,8},{20,12},{24,0},{28,4},{1,25},{... | collective-permute-start | bytes 3145736 | tf_op jit(solution)/shard_map/ppermute | solution.py:631
  145.5 72.6 %collective-permute-start.4 = (bf16[544,1024]{1,0:T(8,128)(2,1)}, bf16[544,1024]{1,0:T(8,128)(2,1)S(1)}, u32[]{:S(2)}, u32[]{:S(2)}) collective-permute-start(bf16[544,1024]{1,0:T(8,128)(2,1)} %get-tuple-element.74.refs_15_), channel_id=1, source_target_pairs={{0,16},{4,20},{8,24},{12,28},{16,0},{20,4},{24,8},{28,12},{1,17},{... | collective-permute-start | bytes 3342344 | tf_op jit(solution)/shard_map/ppermute | solution.py:631
  147.3 74.6 %collective-permute-start.5 = (bf16[544,1024]{1,0:T(8,128)(2,1)}, bf16[544,1024]{1,0:T(8,128)(2,1)S(1)}, u32[]{:S(2)}, u32[]{:S(2)}) collective-permute-start(bf16[544,1024]{1,0:T(8,128)(2,1)} %get-tuple-element.74.refs_15_), channel_id=1, source_target_pairs={{0,24},{4,28},{8,16},{12,20},{16,8},{20,12},{24,0},{28,4},{1,25},{... | collective-permute-start | bytes 3342344 | tf_op jit(solution)/shard_map/ppermute | solution.py:631
  149.1 600.7 %reduce-scatter.14.cloned.1.call-start = ((), (), s32[]{:S(2)}) async-start(), calls=%async_computation.13 | async-start | bytes 3932160 | tf_op jit(solution)/shard_map/reduce_scatter | solution.py:695
  170.5 70.2 %collective-permute-start.7 = (bf16[512,1024]{1,0:T(8,128)(2,1)}, bf16[512,1024]{1,0:T(8,128)(2,1)S(1)}, u32[]{:S(2)}, u32[]{:S(2)}) collective-permute-start(bf16[512,1024]{1,0:T(8,128)(2,1)} %get-tuple-element.152.refs_8_), channel_id=1, source_target_pairs={{0,8},{4,12},{8,0},{12,4},{16,24},{20,28},{24,16},{28,20},{1,9},{5... | collective-permute-start | bytes 3145736 | tf_op jit(solution)/shard_map/ppermute | solution.py:631
  172.0 69.2 %collective-permute-start.8 = (bf16[512,1024]{1,0:T(8,128)(2,1)}, bf16[512,1024]{1,0:T(8,128)(2,1)S(1)}, u32[]{:S(2)}, u32[]{:S(2)}) collective-permute-start(bf16[512,1024]{1,0:T(8,128)(2,1)} %get-tuple-element.152.refs_8_), channel_id=1, source_target_pairs={{0,16},{4,20},{8,24},{12,28},{16,0},{20,4},{24,8},{28,12},{1,17},{... | collective-permute-start | bytes 3145736 | tf_op jit(solution)/shard_map/ppermute | solution.py:631
  194.3 68.8 %collective-permute-start.9 = (bf16[512,1024]{1,0:T(8,128)(2,1)}, bf16[512,1024]{1,0:T(8,128)(2,1)S(1)}, u32[]{:S(2)}, u32[]{:S(2)}) collective-permute-start(bf16[512,1024]{1,0:T(8,128)(2,1)} %get-tuple-element.152.refs_8_), channel_id=1, source_target_pairs={{0,24},{4,28},{8,16},{12,20},{16,8},{20,12},{24,0},{28,4},{1,25},{... | collective-permute-start | bytes 3145736 | tf_op jit(solution)/shard_map/ppermute | solution.py:631
  218.1 58.8 %collective-permute-start.11 = (bf16[4,544,1024]{2,1,0:T(8,128)(2,1)}, bf16[4,544,1024]{2,1,0:T(8,128)(2,1)}, u32[]{:S(2)}, u32[]{:S(2)}) collective-permute-start(bf16[4,544,1024]{2,1,0:T(8,128)(2,1)} %pad_maximum_fusion.pay_ref), channel_id=1, source_target_pairs={{0,4},{4,0},{8,12},{12,8},{16,20},{20,16},{24,28},{28,24},{1,5},{5... | collective-permute-start | bytes 13369352 | tf_op jit(solution)/shard_map/ppermute | solution.py:631
  240.7 58.0 %collective-permute-start.6 = (bf16[4,544,1024]{2,1,0:T(8,128)(2,1)}, bf16[4,544,1024]{2,1,0:T(8,128)(2,1)}, u32[]{:S(2)}, u32[]{:S(2)}) collective-permute-start(bf16[4,544,1024]{2,1,0:T(8,128)(2,1)} %pad_maximum_fusion.1.pay_ref), channel_id=1, source_target_pairs={{0,4},{4,0},{8,12},{12,8},{16,20},{20,16},{24,28},{28,24},{1,5},{5... | collective-permute-start | bytes 13369352 | tf_op jit(solution)/shard_map/ppermute | solution.py:631
  372.2 377.5 %reduce-scatter.12.cloned.1.call-start = ((), (), s32[]{:S(2)}) async-start(), calls=%async_computation.12 | async-start | bytes 3932160 | tf_op jit(solution)/shard_map/reduce_scatter | solution.py:695
  407.3 342.5 %reduce-scatter.10.cloned.1.call-start = ((), (), s32[]{:S(2)}) async-start(), calls=%async_computation.11 | async-start | bytes 3932160 | tf_op jit(solution)/shard_map/reduce_scatter | solution.py:695
  502.8 247.0 %reduce-scatter.8.cloned.1.call-start = ((), (), s32[]{:S(2)}) async-start(), calls=%async_computation.10 | async-start | bytes 3932160 | tf_op jit(solution)/shard_map/reduce_scatter | solution.py:695
  503.5 405.6 %reduce-scatter.6.cloned.1.call-start = ((), (), s32[]{:S(2)}) async-start(), calls=%async_computation.9 | async-start | bytes 6758400 | tf_op jit(solution)/shard_map/reduce_scatter | solution.py:712
  521.6 96.6 %collective-permute-start.18 = (bf16[1056,1024]{1,0:T(8,128)(2,1)}, bf16[1056,1024]{1,0:T(8,128)(2,1)}, u32[]{:S(2)}, u32[]{:S(2)}) collective-permute-start(bf16[1056,1024]{1,0:T(8,128)(2,1)} %bitcast.167), channel_id=1, source_target_pairs={{0,16},{4,20},{8,24},{12,28},{16,0},{20,4},{24,8},{28,12},{1,17},{... | collective-permute-start | bytes 6488072 | tf_op jit(solution)/shard_map/ppermute | solution.py:631
  523.1 95.1 %collective-permute-start.19 = (bf16[1056,1024]{1,0:T(8,128)(2,1)}, bf16[1056,1024]{1,0:T(8,128)(2,1)}, u32[]{:S(2)}, u32[]{:S(2)}) collective-permute-start(bf16[1056,1024]{1,0:T(8,128)(2,1)} %bitcast.166), channel_id=1, source_target_pairs={{0,24},{4,28},{8,16},{12,20},{16,8},{20,12},{24,0},{28,4},{1,25},{... | collective-permute-start | bytes 6488072 | tf_op jit(solution)/shard_map/ppermute | solution.py:631
  539.6 123.4 %collective-permute-start.21 = (bf16[1056,1024]{1,0:T(8,128)(2,1)}, bf16[1056,1024]{1,0:T(8,128)(2,1)}, u32[]{:S(2)}, u32[]{:S(2)}) collective-permute-start(bf16[1056,1024]{1,0:T(8,128)(2,1)} %bitcast.165), channel_id=1, source_target_pairs={{0,8},{4,12},{8,0},{12,4},{16,24},{20,28},{24,16},{28,20},{1,9},{5... | collective-permute-start | bytes 6488072 | tf_op jit(solution)/shard_map/ppermute | solution.py:631
  541.2 168.6 %collective-permute-start.22 = (bf16[1056,1024]{1,0:T(8,128)(2,1)}, bf16[1056,1024]{1,0:T(8,128)(2,1)}, u32[]{:S(2)}, u32[]{:S(2)}) collective-permute-start(bf16[1056,1024]{1,0:T(8,128)(2,1)} %bitcast.164), channel_id=1, source_target_pairs={{0,16},{4,20},{8,24},{12,28},{16,0},{20,4},{24,8},{28,12},{1,17},{... | collective-permute-start | bytes 6488072 | tf_op jit(solution)/shard_map/ppermute | solution.py:631
  570.3 139.4 %collective-permute-start.23 = (bf16[1056,1024]{1,0:T(8,128)(2,1)}, bf16[1056,1024]{1,0:T(8,128)(2,1)}, u32[]{:S(2)}, u32[]{:S(2)}) collective-permute-start(bf16[1056,1024]{1,0:T(8,128)(2,1)} %bitcast.163), channel_id=1, source_target_pairs={{0,24},{4,28},{8,16},{12,20},{16,8},{20,12},{24,0},{28,4},{1,25},{... | collective-permute-start | bytes 6488072 | tf_op jit(solution)/shard_map/ppermute | solution.py:631
  (19 other events, 433.8 us)
Sparse Core Ops, SparseCore 0:
  11.4 83.1 all-gather.4
  96.1 79.6 all-gather.10
  177.4 79.2 all-gather.6
  258.0 79.2 all-gather.8
  372.3 58.8 reduce-scatter.13
  433.4 60.3 reduce-scatter.11
  502.9 58.9 reduce-scatter.9
  564.8 60.2 reduce-scatter.7
  749.8 159.2 reduce-scatter.5

commit v2 on v1

--- a/solution.py
+++ b/solution.py
@@ -256,25 +256,38 @@
     )(*operands)
 
 
-def expert_kernel(
-    x_ref, s_ref, wg_ref, wu_ref, wd_ref,
-    pr_ref, dg_ref, dot_ref, grad_ref,
-    act_ref, both_ref, acc_in_ref, acc_down_ref,
-    *, chunk, tile, last,
-):
+def expert_kernel(x_ref, s_ref, w_ref, *refs, chunk, tile, last, carried):
+    if carried:
+        prior_ref, refs = refs[0], refs[1:]
+    (
+        pr_ref, dg_ref, dot_ref, grad_ref,
+        gate_ref, up_ref, down_ref, act_ref, both_ref, acc_in_ref, acc_down_ref,
+    ) = refs
     rows, width = x_ref.shape[-2:]
-    hidden = wg_ref.shape[-1]
+    hidden = gate_ref.shape[-1]
     owners = grad_ref.shape[0]
     in_rows, down_rows = width // owners, hidden // owners
-    step = pl.program_id(0)
+    step = pl.program_id(1)
+    pieces = width // hidden
+
+    @pl.when(step == 0)
+    def _():
+        for o in range(owners):
+            gate_ref[o * in_rows : (o + 1) * in_rows, :] = w_ref[o, 0, :in_rows, :]
+            up_ref[o * in_rows : (o + 1) * in_rows, :] = w_ref[o, 0, in_rows : 2 * in_rows, :]
+            for c in range(pieces):
+                first = 2 * in_rows + c * down_rows
+                down_ref[o * down_rows : (o + 1) * down_rows, c * hidden : (c + 1) * hidden] = w_ref[
+                    o, 0, first : first + down_rows, :
+                ]
 
     def chunk_body(c, carry):
         here = tile_ds(c, chunk)
-        x = x_ref[0, 0, here, :]
-        s = s_ref[0, 0, here, :]
-        pre_gate = mm(x, wg_ref[0])
-        pre_up = mm(x, wu_ref[0])
-        act_grad = mm_nt(s, wd_ref[0])
+        x = x_ref[0, here, :]
+        s = s_ref[0, here, :]
+        pre_gate = mm(x, gate_ref[...])
+        pre_up = mm(x, up_ref[...])
+        act_grad = mm_nt(s, down_ref[...])
         logistic = jax.nn.sigmoid(pre_gate)
         swish = pre_gate * logistic
         act = (swish * pre_up).astype(BF)
@@ -286,114 +299,121 @@
         act_ref[here, :] = act
         both_ref[here, :hidden] = gate_in
         both_ref[here, hidden:] = up_in
-        pr_ref[0, here, :] = mm(act, wd_ref[0]).astype(BF)
-        dg_ref[0, here, :] = (mm_nt(gate_in, wg_ref[0]) + mm_nt(up_in, wu_ref[0])).astype(BF)
+        pr_ref[0, here, :] = mm(act, down_ref[...]).astype(BF)
+        dg_ref[0, here, :] = (mm_nt(gate_in, gate_ref[...]) + mm_nt(up_in, up_ref[...])).astype(BF)
         return carry
 
     lax.fori_loop(0, rows // chunk, chunk_body, 0)
+
+    def put(owner, first, value):
+        count = value.shape[0]
+        if carried:
+            value = value + prior_ref[owner, 0, first : first + count, :].astype(F32)
+        grad_ref[owner, 0, first : first + count, :] = value.astype(BF)
+
+    def accumulate(acc_ref, here, part, emit):
+        if last == 0:
+            emit(part)
+            return
+
+        @pl.when(step == 0)
+        def _():
+            acc_ref[here, :] = part
+
+        if last > 1:
+
+            @pl.when((step > 0) & (step < last))
+            def _():
+                acc_ref[here, :] = acc_ref[here, :] + part
+
+        @pl.when(step == last)
+        def _():
+            emit(acc_ref[here, :] + part)
 
     def in_body(t, carry):
         here = tile_ds(t, tile)
-        part = mm_tn(x_ref[0, 0, :, here], both_ref[...])
-
-        @pl.when(step == 0)
-        def _():
-            acc_in_ref[here, :] = part
-
-        if last > 1:
-
-            @pl.when((step > 0) & (step < last))
-            def _():
-                acc_in_ref[here, :] = acc_in_ref[here, :] + part
-
-        @pl.when(step == last)
-        def _():
-            total = (acc_in_ref[here, :] + part).astype(BF)
+
+        def emit(total):
             for i in range(tile // in_rows):
                 piece = total[i * in_rows : (i + 1) * in_rows]
                 owner = t * (tile // in_rows) + i
-                grad_ref[owner, :in_rows, :] = piece[:, :hidden]
-                grad_ref[owner, in_rows : 2 * in_rows, :] = piece[:, hidden:]
-
+                put(owner, 0, piece[:, :hidden])
+                put(owner, in_rows, piece[:, hidden:])
+
+        accumulate(acc_in_ref, here, mm_tn(x_ref[0, :, here], both_ref[...]), emit)
         return carry
 
     lax.fori_loop(0, width // tile, in_body, 0)
 
     def down_body(t, carry):
         here = tile_ds(t, tile)
-        part = mm_tn(act_ref[:, here], s_ref[0, 0])
-
-        @pl.when(step == 0)
-        def _():
-            acc_down_ref[here, :] = part
-
-        if last > 1:
-
-            @pl.when((step > 0) & (step < last))
-            def _():
-                acc_down_ref[here, :] = acc_down_ref[here, :] + part
-
-        @pl.when(step == last)
-        def _():
-            total = (acc_down_ref[here, :] + part).astype(BF)
+
+        def emit(total):
             for i in range(tile // down_rows):
                 piece = total[i * down_rows : (i + 1) * down_rows]
                 owner = t * (tile // down_rows) + i
-                for c in range(width // hidden):
-                    first = 2 * in_rows + c * down_rows
-                    grad_ref[owner, first : first + down_rows, :] = piece[
-                        :, c * hidden : (c + 1) * hidden
-                    ]
-
+                for c in range(pieces):
+                    put(owner, 2 * in_rows + c * down_rows, piece[:, c * hidden : (c + 1) * hidden])
+
+        accumulate(acc_down_ref, here, mm_tn(act_ref[:, here], s_ref[0]), emit)
         return carry
 
     lax.fori_loop(0, hidden // tile, down_body, 0)
 
 
-def expert(which, owners, rows_in, slot_grad, gate_w, up_w, down_w):
-    local, micro, rows, width = rows_in.shape
-    hidden = gate_w.shape[2]
+def experts_step(first, weights, rows_in, slot_grad, prior):
+    owners, count, packed, hidden = weights.shape
+    _, total, width = rows_in.shape
+    rows = 8 * CAP
+    steps = total // rows
     out_shape = (
-        jax.ShapeDtypeStruct((micro, rows, width), BF),
-        jax.ShapeDtypeStruct((micro, rows, width), BF),
-        jax.ShapeDtypeStruct((micro, rows, 1), F32),
-        jax.ShapeDtypeStruct((owners, 3 * width // owners, hidden), BF),
-    )
-    in_spec = pl.BlockSpec((1, 1, rows, width), lambda m: (which, m, 0, 0))
-    weight = lambda shape: pl.BlockSpec((1,) + shape, lambda m: (which, 0, 0))
-    row_spec = lambda last: pl.BlockSpec((1, rows, last), lambda m: (m, 0, 0))
+        jax.ShapeDtypeStruct((count, total, width), BF),
+        jax.ShapeDtypeStruct((count, total, width), BF),
+        jax.ShapeDtypeStruct((count, total, 1), F32),
+        jax.ShapeDtypeStruct(weights.shape, BF),
+    )
+    in_spec = pl.BlockSpec((1, rows, width), lambda e, t: (first + e, t, 0))
+    pack_spec = pl.BlockSpec((owners, 1, packed, hidden), lambda e, t: (0, e, 0, 0))
+    row_spec = lambda last: pl.BlockSpec((1, rows, last), lambda e, t: (e, t, 0))
+    operands = [rows_in, slot_grad, weights]
+    in_specs = [in_spec, in_spec, pack_spec]
+    if prior is not None:
+        operands.append(prior)
+        in_specs.append(pack_spec)
+    kept = 0 if steps == 1 else 1
     return pl.pallas_call(
-        functools.partial(expert_kernel, chunk=rows // 3, tile=256, last=micro - 1),
+        functools.partial(
+            expert_kernel, chunk=rows // 3, tile=256, last=steps - 1, carried=prior is not None
+        ),
         out_shape=out_shape,
-        grid=(micro,),
-        in_specs=[in_spec, in_spec, weight((width, hidden)), weight((width, hidden)), weight((hidden, width))],
-        out_specs=(
-            row_spec(width), row_spec(width), row_spec(1),
-            pl.BlockSpec((owners, 3 * width // owners, hidden), lambda m: (0, 0, 0)),
-        ),
+        grid=(count, steps),
+        in_specs=in_specs,
+        out_specs=(row_spec(width), row_spec(width), row_spec(1), pack_spec),
         scratch_shapes=[
+            pltpu.VMEM((width, hidden), BF),
+            pltpu.VMEM((width, hidden), BF),
+            pltpu.VMEM((hidden, width), BF),
             pltpu.VMEM((rows, hidden), BF),
             pltpu.VMEM((rows, 2 * hidden), BF),
-            pltpu.VMEM((width, 2 * hidden), F32),
-            pltpu.VMEM((hidden, width), F32),
+            pltpu.VMEM((width, 2 * hidden) if kept else (8, LANES), F32),
+            pltpu.VMEM((hidden, width) if kept else (8, LANES), F32),
         ],
         compiler_params=pltpu.CompilerParams(vmem_limit_bytes=VMEM_LIMIT),
         cost_estimate=pl.CostEstimate(
-            flops=18 * micro * rows * width * hidden, transcendentals=micro * rows * hidden,
+            flops=18 * count * total * width * hidden, transcendentals=count * total * hidden,
             bytes_accessed=30 << 20,
         ),
-        name="expert",
-    )(rows_in, slot_grad, gate_w, up_w, down_w)
-
-
-def combine_kernel(sel_ref, pay_ref, *refs, local, received):
-    produced = refs[:local]
-    returned = refs[local : 2 * local]
-    dots = refs[2 * local : 3 * local]
-    rest = refs[3 * local :]
+        name="experts",
+    )(*operands)
+
+
+def combine_kernel(sel_ref, pay_ref, *refs, groups, local, received):
+    produced, returned, dots = (refs[i * groups : (i + 1) * groups] for i in range(3))
+    rest = refs[3 * groups :]
     if received:
         other_ref, rest = rest[0], rest[1:]
     out_refs, upper_ref = rest[:-1], rest[-1]
+    each = local // groups
 
     @pl.when(pl.program_id(0) == 0)
     def _():
@@ -405,14 +425,14 @@
         [jnp.where(h, gates[e : e + 1, :], 0.0).astype(BF) for e, h in enumerate(hits)], axis=0
     )
     plain = jnp.concatenate([jnp.where(h, 1.0, 0.0).astype(BF) for h in hits], axis=0)
-    made = jnp.concatenate([r[0, 0] for r in produced], axis=0)
-    back = jnp.concatenate([r[0, 0] for r in returned], axis=0)
+    made = jnp.concatenate([r[e, 0] for r in produced for e in range(each)], axis=0)
+    back = jnp.concatenate([r[e, 0] for r in returned for e in range(each)], axis=0)
     out = mm_tn(weighted, made)
     grads = mm_tn(plain, back)
     pad = jnp.zeros((8 - local, rows), F32)
     dot_rows = jnp.concatenate(
         [
-            jnp.sum(jnp.where(h, dots[e][0, 0], 0.0), axis=0, keepdims=True)
+            jnp.sum(jnp.where(h, dots[e // each][e % each, 0], 0.0), axis=0, keepdims=True)
             for e, h in enumerate(hits)
         ]
         + ([pad] if local < 8 else []),
@@ -421,44 +441,48 @@
     high = dot_rows.astype(BF)
     low = (dot_rows - high.astype(F32)).astype(BF)
     tail = jnp.concatenate([mm_tn(sel_ref[...], high), mm_tn(sel_ref[...], low)], axis=1)
+    half = tail.shape[0] // 2
+    first = jnp.concatenate([out, tail[:half]], axis=0)
+    second = jnp.concatenate([tail[half:], grads], axis=0)
     if received:
-        out = out + other_ref[0, :rows, :].astype(F32)
-        grads = grads + other_ref[0, rows : 2 * rows, :].astype(F32)
-        tail = tail + other_ref[0, 2 * rows :, :].astype(F32)
-    def put(ref, at):
-        ref[at, :rows, :] = out.astype(BF)
-        ref[at, rows : 2 * rows, :] = grads.astype(BF)
-        ref[at, 2 * rows :, :] = tail.astype(BF)
-
-    if len(out_refs) == 1:
-        put(out_refs[0], 0)
+        first = first + other_ref[0, : rows + half, :].astype(F32)
+        second = second + other_ref[0, rows + half :, :].astype(F32)
+
+        def put(index):
+            out_refs[2 * index][...] = first.astype(BF)
+            out_refs[2 * index + 1][...] = second.astype(BF)
+
+        for index in range(len(out_refs) // 2):
+            pl.when(pl.program_id(0) == index)(functools.partial(put, index))
     else:
-        for index, ref in enumerate(out_refs):
-            pl.when(pl.program_id(0) == index)(functools.partial(put, ref, 0))
-
-
-def combine(sel, pays, produced, returned, dots, micro, side, other):
+        out_refs[0][0, : rows + half, :] = first.astype(BF)
+        out_refs[0][0, rows + half :, :] = second.astype(BF)
+
+
+def combine(sel, pays, produced, returned, dots, side, other):
     count, total_rows, width = pays.shape
-    local = len(produced)
+    groups, each = len(produced), produced[0].shape[0]
+    local = groups * each
     experts = sel.shape[1]
     rows = total_rows - experts
-    pick = lambda last: pl.BlockSpec((1, 1, CAP, last), lambda s: (micro, side * count + s, 0, 0))
+    pick = lambda last: pl.BlockSpec((each, 1, CAP, last), lambda s: (0, side * count + s, 0, 0))
     in_specs = [
         pl.BlockSpec(sel.shape, lambda s: (0, 0)),
         pl.BlockSpec((1, experts, width), lambda s: (s, rows // experts, 0)),
     ]
-    in_specs += [pick(width)] * (2 * local) + [pick(1)] * local
+    in_specs += [pick(width)] * (2 * groups) + [pick(1)] * groups
     operands = [sel, pays, *produced, *returned, *dots]
-    out_spec = pl.BlockSpec((1, 2 * rows + experts, width), lambda s: (s, 0, 0))
-    out_shape = (jax.ShapeDtypeStruct((count, 2 * rows + experts, width), BF),)
+    total = 2 * rows + experts
+    out_spec = pl.BlockSpec((1, total, width), lambda s: (s, 0, 0))
+    out_shape = (jax.ShapeDtypeStruct((count, total, width), BF),)
     out_specs = (out_spec,)
     if other is not None:
         operands.append(other)
         in_specs.append(out_spec)
-        out_shape = (jax.ShapeDtypeStruct((1, 2 * rows + experts, width), BF),) * count
-        out_specs = (pl.BlockSpec((1, 2 * rows + experts, width), lambda s: (0, 0, 0)),) * count
+        out_shape = (jax.ShapeDtypeStruct((total // 2, width), BF),) * (2 * count)
+        out_specs = (pl.BlockSpec((total // 2, width), lambda s: (0, 0)),) * (2 * count)
     return pl.pallas_call(
-        functools.partial(combine_kernel, local=local, received=other is not None),
+        functools.partial(combine_kernel, groups=groups, local=local, received=other is not None),
         out_shape=out_shape,
         grid=(count,),
         in_specs=in_specs,
@@ -479,8 +503,8 @@
         x_ref, w_ref, gain_one_ref, gain_two_ref, id_row_ref, id_col_ref, cos_ref, sin_ref,
         grad_ref, q_ref, k_ref, v_ref, att_ref, lse_ref, res_ref, pay_ref, gate_ref,
     ) = refs[:17]
-    term_refs = refs[17 : 17 + terms]
-    rest = refs[17 + terms :]
+    term_refs = refs[17 : 17 + 2 * terms]
+    rest = refs[17 + 2 * terms :]
     if carried:
         prior_ref, rest = rest[0], rest[1:]
     out_ref, in_grad_ref, pack_ref, bias_ref, wide_ref, att_grad_ref, qkv_grad_ref, branch_ref, normed_ref = rest
@@ -493,20 +517,21 @@
             value = value + prior_ref[row_slice, cols].astype(F32)
         pack_ref[row_slice, cols] = value.astype(BF)
 
-    def gathered(low, high):
-        total = term_refs[0][low:high, :].astype(F32)
-        for ref in term_refs[1:]:
+    def gathered(which, low, high):
+        total = term_refs[which][low:high, :].astype(F32)
+        for ref in term_refs[2 + which :: 2]:
             total = total + ref[low:high, :].astype(F32)
         return total
 
+    half = experts // 2
     residual = res_ref[...]
-    out_ref[...] = (residual + RESIDUAL_SCALE * gathered(0, rows)).astype(BF)
-    tail = gathered(2 * rows, 2 * rows + experts)
+    out_ref[...] = (residual + RESIDUAL_SCALE * gathered(0, 0, rows)).astype(BF)
+    tail = jnp.concatenate([gathered(0, rows, rows + half), gathered(1, 0, half)], axis=0)
     weighted = tail[:, :rows] + tail[:, rows:]
     chosen = weighted - gate_ref[...] * jnp.sum(weighted, axis=0, keepdims=True)
     chosen = jnp.concatenate([chosen, jnp.zeros((LANES - experts, rows), F32)], axis=0)
     logit_grad = chosen.T.astype(BF)
-    moe_grad = gathered(rows, 2 * rows) + mm_nt(logit_grad, w_ref[:, start + width :])
+    moe_grad = gathered(1, half, half + rows) + mm_nt(logit_grad, w_ref[:, start + width :])
     last = mm_tn(pay_ref[:rows, :], logit_grad)
     scale = lax.rsqrt(jnp.mean(residual * residual, axis=1, keepdims=True) + EPS)
     gain_two_grad = jnp.sum(moe_grad * residual * scale, axis=0, keepdims=True)
@@ -603,7 +628,7 @@
     flops = 4 * rows * width * (q_width + 2 * kv_width + width) + 20 * QUERY_HEADS * rows * rows * 128
     return pl.pallas_call(
         functools.partial(
-            attention_backward_kernel, terms=len(terms), q_width=q_width, kv_width=kv_width,
+            attention_backward_kernel, terms=len(terms) // 2, q_width=q_width, kv_width=kv_width,
             experts=experts, carried=prior is not None,
         ),
         out_shape=(
@@ -627,8 +652,237 @@
     )(*operands)
 
 
+def peer_chip(chip, distance):
+    total = 0
+    for bit in (1, 2, 4):
+        total = total + bit * ((chip // bit + (distance // bit) % 2) % 2)
+    return total
+
+
+def where_am_i():
+    f, d = lax.axis_index("fsdp"), lax.axis_index("dp")
+    return f // 2, f % 2, d
+
+
+def meet(peers):
+    barrier = pltpu.get_barrier_semaphore()
+    for peer in peers:
+        pl.semaphore_signal(
+            barrier, inc=1, device_id=peer, device_id_type=pl.DeviceIdType.MESH
+        )
+    pl.semaphore_wait(barrier, len(peers))
+
+
+def push(src, dst, send, receive, peer):
+    copy = pltpu.make_async_remote_copy(
+        src_ref=src, dst_ref=dst, send_sem=send, recv_sem=receive, device_id=peer,
+        device_id_type=pl.DeviceIdType.MESH,
+    )
+    copy.start()
+    return copy
+
+
+def gather_layer_kernel(
+    w_ref, out_ref, own_sem, z_send, z_receive, x_send, x_receive, s_send, s_receive, *, chips, depth
+):
+    chip, core, d = where_am_i()
+    rows = w_ref.shape[0]
+    others = [peer_chip(chip, r) for r in range(1, chips)]
+    f, sibling = chip * 2 + core, chip * 2 + 1 - core
+
+    def block(owner, layer):
+        first = pl.multiple_of((owner * depth + layer) * rows, rows)
+        return out_ref.at[pl.ds(first, rows), :]
+
+    peers = [(f, (d + i) % depth) for i in range(1, depth)]
+    peers += [(c * 2 + core, d) for c in others] + [(sibling, d)]
+    meet(peers)
+    own = pltpu.make_async_copy(w_ref, block(f, d), own_sem)
+    own.start()
+    z_copies = [
+        push(w_ref, block(f, d), z_send.at[i - 1], z_receive.at[i - 1], (f, (d + i) % depth))
+        for i in range(1, depth)
+    ]
+    x_copies, s_copies = [], []
+    layers = [(d + depth - i) % depth for i in range(depth)]
+    for i, layer in enumerate(layers):
+        if i:
+            z_copies[i - 1].wait_recv()
+        src = block(f, layer) if i else w_ref
+        for r, c in enumerate(others):
+            x_copies.append(
+                push(src, block(f, layer), x_send.at[i, r], x_receive.at[i, r], (c * 2 + core, d))
+            )
+        s_copies.append(
+            push(src, block(f, layer), s_send.at[i, 0], s_receive.at[i, 0], (sibling, d))
+        )
+    for i, layer in enumerate(layers):
+        for r, c in enumerate(others):
+            x_copies[i * (chips - 1) + r].wait_recv()
+            there = block(c * 2 + core, layer)
+            s_copies.append(
+                push(there, there, s_send.at[i, r + 1], s_receive.at[i, r + 1], (sibling, d))
+            )
+    own.wait()
+    for copy in z_copies + x_copies:
+        copy.wait_send()
+    for copy in s_copies:
+        copy.wait()
+
+
+def gather_layer(pack, chips, depth):
+    dma = pltpu.SemaphoreType.DMA
+    rows, width = pack.shape
+    return pl.pallas_call(
+        functools.partial(gather_layer_kernel, chips=chips, depth=depth),
+        out_shape=jax.ShapeDtypeStruct((rows * 2 * chips * depth, width), pack.dtype),
+        in_specs=[pl.BlockSpec(memory_space=pl.ANY)],
+        out_specs=pl.BlockSpec(memory_space=pl.ANY),
+        scratch_shapes=[
+            dma(()), dma((depth - 1,)), dma((depth - 1,)), dma((depth, chips - 1)),
+            dma((depth, chips - 1)), dma((depth, chips)), dma((depth, chips)),
+        ],
+        compiler_params=pltpu.CompilerParams(collective_id=1, has_side_effects=True),
+        name="gather_layer",
+    )(pack)
+
+
+def reduce_layer_kernel(
+    pack_ref, out_ref, s_buf, s_sum, x_buf, x_sum, z_buf,
+    s_send, s_receive, x_send, x_receive, z_send, z_receive,
+    *, chips, depth, parts,
+):
+    chip, core, d = where_am_i()
+    total, width = pack_ref.shape
+    rows = total // (2 * chips * depth)
+    span = rows * depth
+    step = width // parts
+    distances = list(range(1, chips))
+    others = [peer_chip(chip, r) for r in distances]
+    f, sibling = chip * 2 + core, chip * 2 + 1 - core
+    peers = [(f, (d + i) % depth) for i in range(1, depth)]
+    peers += [(c * 2 + core, d) for c in others] + [(sibling, d)]
+    meet(peers)
+
+    def band(p):
+        return slice(p * step, (p + 1) * step)
+
+    def mine(c, k):
+        return pl.ds(pl.multiple_of((c * 2 + k) * span, span), span)
+
+    order = [(r, c) for r, c in zip(distances, others)][::-1] + [(0, chip)]
+    s_copies = {}
+    for p in range(parts):
+        for r, c in order:
+            s_copies[p, r] = push(
+                pack_ref.at[mine(c, 1 - core), band(p)], s_buf.at[r, :, band(p)],
+                s_send.at[p, r], s_receive.at[p, r], (sibling, d),
+            )
+    x_copies, z_copies = {}, {}
+
+    def sum_chip(p):
+        for r, c in order:
+            s_copies[p, r].wait_recv()
+            value = pack_ref[mine(c, core), band(p)].astype(F32) + s_buf[r, :, band(p)].astype(F32)
+            s_sum[r, :, band(p)] = value.astype(s_sum.dtype)
+
+    def send_chip(p):
+        for r, c in order[:-1]:
+            x_copies[p, r] = push(
+                s_sum.at[r, :, band(p)], x_buf.at[r - 1, :, band(p)], x_send.at[p, r - 1],
+                x_receive.at[p, r - 1], (c * 2 + core, d),
+            )
+
+    def sum_plane(p):
+        value = s_sum[0, :, band(p)].astype(F32)
+        for r in distances:
+            x_copies[p, r].wait_recv()
+            value = value + x_buf[r - 1, :, band(p)].astype(F32)
+        x_sum[:, :, band(p)] = value.reshape(depth, rows, step).astype(x_sum.dtype)
+
+    def send_plane(p):
+        for i in range(1, depth):
+            to = (d + i) % depth
+            z_copies[p, i] = push(
+                x_sum.at[to, :, band(p)], z_buf.at[i - 1, :, band(p)], z_send.at[p, i - 1],
+                z_receive.at[p, i - 1], (f, to),
+            )
+
+    def finish(p):
+        value = x_sum[d, :, band(p)].astype(F32)
+        for i in range(1, depth):
+            z_copies[p, i].wait_recv()
+            value = value + z_buf[i - 1, :, band(p)].astype(F32)
+        out_ref[:, band(p)] = value
+
+    for p in range(parts + 1):
+        if p < parts:
+            sum_chip(p)
+        if p > 0:
+            send_chip(p - 1)
+    for p in range(parts + 1):
+        if p < parts:
+            sum_plane(p)
+        if p > 0:
+            send_plane(p - 1)
+    for p in range(parts):
+        finish(p)
+    for copy in [*s_copies.values(), *x_copies.values(), *z_copies.values()]:
+        copy.wait_send()
+
+
+def reduce_layer(pack, chips, depth, parts):
+    dma = pltpu.SemaphoreType.DMA
+    total, width = pack.shape
+    rows = total // (2 * chips * depth)
+    kind = BF if rows % 16 == 0 else F32
+    return pl.pallas_call(
+        functools.partial(reduce_layer_kernel, chips=chips, depth=depth, parts=parts),
+        out_shape=jax.ShapeDtypeStruct((rows, width), F32),
+        in_specs=[pl.BlockSpec(memory_space=pltpu.VMEM)],
+        out_specs=pl.BlockSpec(memory_space=pltpu.VMEM),
+        scratch_shapes=[
+            pltpu.VMEM((chips, rows * depth, width), BF),
+            pltpu.VMEM((chips, rows * depth, width), BF),
+            pltpu.VMEM((chips - 1, rows * depth, width), BF),
+            pltpu.VMEM((depth, rows, width), kind),
+            pltpu.VMEM((depth - 1, rows, width), kind),
+            dma((parts, chips)), dma((parts, chips)), dma((parts, chips - 1)), dma((parts, chips - 1)),
+            dma((parts, depth - 1)), dma((parts, depth - 1)),
+        ],
+        compiler_params=pltpu.CompilerParams(
+            collective_id=2, has_side_effects=True, vmem_limit_bytes=VMEM_LIMIT
+        ),
+        name="reduce_layer",
+    )(pack)
+
+
 def swap(value, distance, size):
     return lax.ppermute(value, "fsdp", [(i, i ^ distance) for i in range(size)])
+
+
+def gather_chips(value, size):
+    chips = size // 2
+    if chips != 4:
+        return jnp.stack([value] + [swap(value, 2 * r, size) for r in range(1, chips)])
+    half = value.shape[0] // 2
+    one, two = swap(value, 2, size), swap(value, 4, size)
+    three = jnp.concatenate([swap(one[:half], 4, size), swap(two[half:], 2, size)])
+    return jnp.stack([value, one, two, three])
+
+
+def scatter_chips(kept, size):
+    chips = size // 2
+    if chips != 4:
+        return [kept[0], kept[1]] + [swap(kept[2 * r + h], 2 * r, size) for r in range(1, chips) for h in range(2)]
+    add = lambda a, b: (a.astype(F32) + b.astype(F32)).astype(BF)
+    by_one = swap(kept[6], 2, size)
+    by_two = swap(kept[7], 4, size)
+    one_first = swap(kept[2], 2, size)
+    two_second = swap(kept[5], 4, size)
+    one_second = swap(add(kept[3], by_two), 2, size)
+    two_first = swap(add(kept[4], by_one), 4, size)
+    return [kept[0], kept[1], one_first, one_second, two_first, two_second]
 
 
 def local(
@@ -637,84 +891,87 @@
 ):
     micro, _, rows, width = inputs.shape
     experts = w_router.shape[1]
-    held = w_gate.shape[0]
-    hidden = w_gate.shape[2]
+    held, in_rows, hidden = w_gate.shape
+    down_rows = w_down.shape[1]
     q_width, kv_width = w_query.shape[1], key_weight.shape[1]
     owners = lax.axis_size("fsdp")
-    parts = lax.axis_size("dp")
+    depth = lax.axis_size("dp")
     chips = owners // 2
     tables = tuple(jnp.asarray(t) for t in rope_tables(rows))
     start = q_width + 2 * kv_width + width
-
-    def gather_peers(value):
-        mine = jnp.stack([value] + [swap(value, 2 * r, owners) for r in range(1, chips)])
-        return mine, swap(mine, 1, owners)
-
+    group = max(1, held // 2)
+    cuts = width // hidden
+
+    split_down = w_down.reshape(held, down_rows, cuts, hidden).transpose(0, 2, 1, 3)
+    packed = jnp.concatenate(
+        [w_gate, w_up, split_down.reshape(held, cuts * down_rows, hidden)], axis=1
+    )
+    weights = [
+        lax.all_gather(packed[g : g + group], "dp", axis=0, tiled=False)
+        for g in range(0, held, group)
+    ]
     pieces = [
         w_query, key_weight, value_weight, w_output, w_router, norm_gain[:, None], moe_gain[:, None]
     ]
     filled = sum(p.shape[1] for p in pieces)
     pieces.append(jnp.zeros((w_query.shape[0], start + LANES - filled), BF))
-    pack = lax.all_gather(
-        jnp.concatenate(pieces, axis=1), ("fsdp", "dp"), axis=0, tiled=True
-    )
+    pack = gather_layer(jnp.concatenate(pieces, axis=1), chips, depth)
     gain_one = pack[:, start + experts].astype(F32)[None, :]
     gain_two = pack[:, start + experts + 1].astype(F32)[None, :]
-    gate_w = lax.all_gather(w_gate, "dp", axis=1, tiled=True)
-    up_w = lax.all_gather(w_up, "dp", axis=1, tiled=True)
-    down_w = lax.all_gather(w_down, "dp", axis=1, tiled=True)
-    grads = [gather_peers(out_grad[m, 0]) for m in range(micro)]
     first = lax.axis_index("fsdp") * held
     places = jnp.arange(8)[:, None]
     sel = ((jnp.arange(experts)[None, :] == first + places) & (places < held)).astype(BF)
-
-    saved, pays = [], []
+    later, _ = lax.optimization_barrier((out_grad, pack))
+
+    saved, pays, grads = [], [], []
     for m in range(micro):
         x = inputs[m, 0]
         q, k, v, att, lse, res, pay, gates = attention_forward(
             x, pack, gain_one, gain_two, block_ids[m, 0], routes[m, 0], tables, q_width, kv_width, experts
         )
         saved.append((q, k, v, att, lse, res, pay, gates))
-        pays.append(gather_peers(pay))
-    carried = None
+        mine = gather_chips(later[m, 0], owners)
+        grads.append((mine, swap(mine, 1, owners)))
+        mine = gather_chips(pay, owners)
+        pays.append((mine, swap(mine, 1, owners)))
+    moved = []
     for m in range(micro):
+        carried = None
         for side in range(2):
-            carried = dispatch(
-                sel, pays[m][side], grads[m][side], m * 2 + side, micro * 2, held, carried
-            )
-    flat = (held, micro * chips // 4, 8 * CAP, width)
-    rows_in, slot_grad = carried[0].reshape(flat), carried[1].reshape(flat)
-    produced, returned, dots, weight_sums = [], [], [], []
-    for e in range(held):
-        pr, dg, dot, weight = expert(e, parts, rows_in, slot_grad, gate_w, up_w, down_w)
-        split = (micro, 2 * chips, CAP)
-        produced.append(pr.reshape(split + (width,)))
-        returned.append(dg.reshape(split + (width,)))
-        dots.append(dot.reshape(split + (1,)))
-        weight_sums.append(
-            lax.psum_scatter(weight, "dp", scatter_dimension=0, tiled=True)[0]
-        )
-    others = []
+            carried = dispatch(sel, pays[m][side], grads[m][side], side, 2, held, carried)
+        moved.append([c.reshape(held, 2 * chips * CAP, width) for c in carried])
+    order = [(m, g) for m in range(micro) for g in range(len(weights))]
+    done = {}
+    for m, g in order:
+        prior = done[m - 1, g][3] if m else None
+        done[m, g] = experts_step(g * group, weights[g], *moved[m], prior)
+    sums = [
+        lax.psum_scatter(done[micro - 1, g][3], "dp", scatter_dimension=0, tiled=True)[0]
+        for g in range(len(weights))
+    ]
+    terms = []
     for m in range(micro):
-        (sent,) = combine(sel, pays[m][1], produced, returned, dots, m, 1, None)
-        others.append(swap(sent, 1, owners))
+        parts = [
+            [done[m, g][i].reshape(group, 2 * chips, CAP, -1) for g in range(len(weights))]
+            for i in range(3)
+        ]
+        (sent,) = combine(sel, pays[m][1], *parts, 1, None)
+        kept = combine(sel, pays[m][0], *parts, 0, swap(sent, 1, owners))
+        terms.append(scatter_chips(kept, owners))
     outputs, input_grads = [], []
     prior = None
     for m in range(micro):
-        kept = combine(sel, pays[m][0], produced, returned, dots, m, 0, others[m])
-        terms = [kept[0][0]] + [swap(kept[r][0], 2 * r, owners) for r in range(1, chips)]
         out, in_grad, prior = attention_backward(
             inputs[m, 0], pack, gain_one, gain_two, block_ids[m, 0], tables, out_grad[m, 0], saved[m],
-            terms, prior, q_width, kv_width, experts,
+            terms[m], prior, q_width, kv_width, experts,
         )
         outputs.append(out)
         input_grads.append(in_grad)
-    layer = lax.psum_scatter(prior, ("fsdp", "dp"), scatter_dimension=0, tiled=True).astype(F32)
+    layer = reduce_layer(prior, chips, depth, 5)
     marks = np.cumsum([0, q_width, kv_width, kv_width, width, experts, 1, 1])
     cut = [layer[:, a:b] for a, b in zip(marks[:-1], marks[1:])]
-    in_rows, down_rows = width // parts, hidden // parts
-    stacked = jnp.stack(weight_sums).astype(F32)
-    grad_down = stacked[:, 2 * in_rows :].reshape(held, width // hidden, down_rows, hidden)
+    stacked = jnp.concatenate(sums, axis=0).astype(F32)
+    grad_down = stacked[:, 2 * in_rows :].reshape(held, cuts, down_rows, hidden)
     grad_down = grad_down.transpose(0, 2, 1, 3).reshape(held, down_rows, width)
     return (
         jnp.stack(outputs)[:, None],

time: 925 us -> 721 us (0.78)
  waiting for transfers between devices: 472 us -> 138 us
  Pallas kernels: 362 us -> 471 us
  local copies, waits for them, and re-layouts: 22.8 us -> 33.7 us
  other arithmetic: 22.4 us -> 33 us
    reduce_scatter x5 -> x2, waiting for transfers between devices: 148 us -> 0.01 us  [local(): lax.psum_scatter(done[micro - 1, g][3], 'dp', scatter_dimension=0, tiled=...]
    pallas_call x8 -> x10, Pallas kernels: 197 us -> 308 us  [the longest x4 141 us: experts_step(): pl.pallas_call(functools.partial(expert_kernel, chunk=rows // 3, tile=256...]
    all_gather x4 -> x2, waiting for transfers between devices: 96.3 us -> 0.02 us  [local(): lax.all_gather(packed[g:g + group], 'dp', axis=0, tiled=False)]
    ppermute x24 -> x34, waiting for transfers between devices: 226 us -> 138 us  [swap(): return lax.ppermute(value, 'fsdp', [(i, i ^ distance) for i in range(size)])]
    slice x1 -> x10, local copies, waits for them, and re-layouts: 2.72 us -> 13.3 us  [the longest x4 4.87 us: gather_chips(): one[:half]]
    ppermute x24 -> x34, starting transfers between devices: 27.1 us -> 25.6 us  [swap(): return lax.ppermute(value, 'fsdp', [(i, i ^ distance) for i in range(size)])]
  transfers between devices with their start and end apart: 33 -> 38, of which waited for: 15 -> 13; matrix products, arithmetic and copies ran while one was open for 4% -> 8% of each run, Pallas kernels for 36% -> 66%
where the time goes in v2:
time: 721 us; the launch traced here: 717 us
  Pallas kernels  471 us (65%)
  waiting for transfers between devices  138 us (19%)
  local copies, waits for them, and re-layouts  33.7 us (5%)
  other arithmetic  33 us (5%)
  starting transfers between devices  25.8 us (4%)
  between operations  14.4 us (2%)
    pallas_call x4, Pallas kernels, experts_step(): pl.pallas_call(functools.partial(expert_kernel, chunk=rows // 3, tile=256...  141 us
    ppermute x34, waiting for transfers between devices, swap(): return lax.ppermute(value, 'fsdp', [(i, i ^ distance) for i in range(size)])  138 us
    pallas_call x2, Pallas kernels, attention_backward(): pl.pallas_call(functools.partial(attention_backward_kernel, terms=len(ter...  76.5 us
    pallas_call x1, Pallas kernels, reduce_layer(): pl.pallas_call(functools.partial(reduce_layer_kernel, chips=chips, depth=...  60.5 us
    pallas_call x4, Pallas kernels, combine(): pl.pallas_call(functools.partial(combine_kernel, groups=groups, local=loc...  56.4 us
    pallas_call x1, Pallas kernels, gather_layer(): pl.pallas_call(functools.partial(gather_layer_kernel, chips=chips, depth=...  50 us
    pallas_call x2, Pallas kernels, attention_forward(): pl.pallas_call(functools.partial(attention_forward_kernel, q_width=q_widt...  43.8 us
    pallas_call x4, Pallas kernels, dispatch(): pl.pallas_call(functools.partial(dispatch_kernel, local=local), out_shape...  43.3 us
  transfers between devices with their start and end apart: 38, of which 13 were waited for; matrix products, arithmetic and copies ran while one was open for 8% of the time, Pallas kernels for 66%

profile of v2, /device:TPU:0, one launch (start us, length us, event | category | flops | bytes accessed | tf_op | source)
XLA Modules:
  0.0 716.6 jit_solution(8600329502785834461)
XLA Ops:
  12.3 50.0 %gather_layer.1.w_ref.refs_1_ = bf16[1024,3200]{1,0:T(8,128)(2,1)} custom-call(bf16[32,3200]{1,0:T(8,128)(2,1)} %concatenate.21.w_ref), custom_call_target="tpu_custom_call" | custom-call | tf_op jit(solution)/shard_map/gather_layer/pallas_call | solution.py:736
  76.1 22.0 %attention_forward.2 = (bf16[512,1024]{1,0:T(8,128)(2,1)}, bf16[512,512]{1,0:T(8,128)(2,1)}, bf16[512,512]{1,0:T(8,128)(2,1)}, bf16[512,1024]{1,0:T(8,128)(2,1)}...) custom-call(bf16[512,1024]{1,0:T(8,128)(2,1)} %get-tuple-element.189.x_ref.refs_0_, ...), custom_call_target="tpu_custom_call" | custom-call | flops 7516192768 | bytes 16777216 | tf_op jit(solution)/shard_map/attention_forward/pallas_call | solution.py:172
  100.7 21.9 %attention_forward.3 = (bf16[512,1024]{1,0:T(8,128)(2,1)}, bf16[512,512]{1,0:T(8,128)(2,1)}, bf16[512,512]{1,0:T(8,128)(2,1)}, bf16[512,1024]{1,0:T(8,128)(2,1)}...) custom-call(bf16[512,1024]{1,0:T(8,128)(2,1)} %get-tuple-element.190.x_ref.refs_0_, ...), custom_call_target="tpu_custom_call" | custom-call | flops 7516192768 | bytes 16777216 | tf_op jit(solution)/shard_map/attention_forward/pallas_call | solution.py:172
  150.3 10.8 %collective-permute-done.17 = bf16[544,1024]{1,0:T(8,128)(2,1)S(1)} collective-permute-done((bf16[544,1024]{1,0:T(8,128)(2,1)}, bf16[544,1024]{1,0:T(8,128)(2,1)S(1)}, u32[]{:S(2)}, u32[]{:S(2)}) %collective-permute-start.17) | collective-permute-done | bytes 1114144 | tf_op jit(solution)/shard_map/ppermute | solution.py:861
  163.3 10.9 %collective-permute-done.18 = bf16[544,1024]{1,0:T(8,128)(2,1)S(1)} collective-permute-done((bf16[544,1024]{1,0:T(8,128)(2,1)}, bf16[544,1024]{1,0:T(8,128)(2,1)S(1)}, u32[]{:S(2)}, u32[]{:S(2)}) %collective-permute-start.18) | collective-permute-done | bytes 1114144 | tf_op jit(solution)/shard_map/ppermute | solution.py:861
  174.2 11.3 %collective-permute-done.7 = bf16[256,1024]{1,0:T(8,128)(2,1)} collective-permute-done((bf16[256,1024]{1,0:T(8,128)(2,1)}, bf16[256,1024]{1,0:T(8,128)(2,1)}, u32[]{:S(2)}, u32[]{:S(2)}) %collective-permute-start.7) | collective-permute-done | bytes 524320 | tf_op jit(solution)/shard_map/ppermute | solution.py:861
  225.6 10.8 %dispatch.4 = (bf16[4,2,4,144,1024]{4,3,2,1,0:T(8,128)(2,1)}, bf16[4,2,4,144,1024]{4,3,2,1,0:T(8,128)(2,1)}) custom-call(bf16[8,32]{1,0:T(8,128)(2,1)} %fusion.1.sel_ref, bf16[4,544,1024]{2,1,0:T(8,128)(2,1)} %pad_maximum_fusion.pay_ref, bf16[4,512,1024]{2,1,0:T(8,128)(2,1)} %pad_maximum_fusion.2.grad_ref), custom_call_target="tpu_custom_call" | custom-call | flops 4831838208 | bytes 20971520 | tf_op jit(solution)/shard_map/dispatch/pallas_call | solution.py:243
  236.4 10.9 %dispatch.6 = (bf16[4,2,4,144,1024]{4,3,2,1,0:T(8,128)(2,1)}, bf16[4,2,4,144,1024]{4,3,2,1,0:T(8,128)(2,1)}) custom-call(bf16[8,32]{1,0:T(8,128)(2,1)} %fusion.1.sel_ref, bf16[4,544,1024]{2,1,0:T(8,128)(2,1)} %pad_maximum_fusion.1.pay_ref, bf16[4,512,1024]{2,1,0:T(8,128)(2,1)} %pad_maximum_fusion.3.grad_ref), custom_call_target="tpu_custom_call" | custom-call | flops 4831838208 | bytes 20971520 | tf_op jit(solution)/shard_map/dispatch/pallas_call | solution.py:243
  247.3 10.9 %dispatch.5 = (bf16[4,2,4,144,1024]{4,3,2,1,0:T(8,128)(2,1)}, bf16[4,2,4,144,1024]{4,3,2,1,0:T(8,128)(2,1)}) custom-call(bf16[8,32]{1,0:T(8,128)(2,1)} %fusion.1.sel_ref, bf16[4,544,1024]{2,1,0:T(8,128)(2,1)} %collective-permute-done.4.pay_ref, bf16[4,512,1024]{2,1,0:T(8,128)(2,1)} %collective-permute-done.9.grad_ref, ...), custom_call_target="tpu_custom_call", output_to_operand_aliasing={{0}: (3, {}), {1}: (4, {})} | custom-call | flops 4831838208 | bytes 20971520 | tf_op jit(solution)/shard_map/dispatch/pallas_call | solution.py:243
  258.2 10.8 %dispatch.7 = (bf16[4,2,4,144,1024]{4,3,2,1,0:T(8,128)(2,1)}, bf16[4,2,4,144,1024]{4,3,2,1,0:T(8,128)(2,1)}) custom-call(bf16[8,32]{1,0:T(8,128)(2,1)} %fusion.1.sel_ref, bf16[4,544,1024]{2,1,0:T(8,128)(2,1)} %collective-permute-done.21.pay_ref, ...), custom_call_target="tpu_custom_call", output_to_operand_aliasing={{0}: (3, {}), {1}: (4, {})} | custom-call | flops 4831838208 | bytes 20971520 | tf_op jit(solution)/shard_map/dispatch/pallas_call | solution.py:243
  269.0 34.8 %experts.5 = (bf16[2,1152,1024]{2,1,0:T(8,128)(2,1)}, bf16[2,1152,1024]{2,1,0:T(8,128)(2,1)}, f32[2,1152,1]{2,1,0:T(8,128)}, bf16[4,2,768,512]{3,2,1,0:T(8,128)(2,1)}) custom-call(bf16[4,1152,1024]{2,1,0:T(8,128)(2,1)} %bitcast.112, bf16[4,1152,1024]{2,1,0:T(8,128)(2,1)} %bitcast.114, bf16[4,2,768,512]{3,2,1,0:T(8,128)(2,1)} %bitcast.151), custom_call_target="tpu_custom_call" | custom-call | flops 21743271936 | bytes 31457280 | tf_op jit(solution)/shard_map/experts/pallas_call | solution.py:384
  303.8 35.8 %experts.7 = (bf16[2,1152,1024]{2,1,0:T(8,128)(2,1)}, bf16[2,1152,1024]{2,1,0:T(8,128)(2,1)}, f32[2,1152,1]{2,1,0:T(8,128)}, bf16[4,2,768,512]{3,2,1,0:T(8,128)(2,1)}) custom-call(bf16[4,1152,1024]{2,1,0:T(8,128)(2,1)} %bitcast.108, bf16[4,1152,1024]{2,1,0:T(8,128)(2,1)} %bitcast.110, bf16[4,2,768,512]{3,2,1,0:T(8,128)(2,1)} %bitcast.152, ...), custom_call_target="tpu_custom_call" | custom-call | flops 21743271936 | bytes 31457280 | tf_op jit(solution)/shard_map/experts/pallas_call | solution.py:384
  339.7 34.8 %experts.4 = (bf16[2,1152,1024]{2,1,0:T(8,128)(2,1)}, bf16[2,1152,1024]{2,1,0:T(8,128)(2,1)}, f32[2,1152,1]{2,1,0:T(8,128)}, bf16[4,2,768,512]{3,2,1,0:T(8,128)(2,1)}) custom-call(bf16[4,1152,1024]{2,1,0:T(8,128)(2,1)} %bitcast.113, bf16[4,1152,1024]{2,1,0:T(8,128)(2,1)} %bitcast.115, bf16[4,2,768,512]{3,2,1,0:T(8,128)(2,1)} %bitcast.153), custom_call_target="tpu_custom_call" | custom-call | flops 21743271936 | bytes 31457280 | tf_op jit(solution)/shard_map/experts/pallas_call | solution.py:384
  374.5 12.3 %combine.4 = bf16[4,1056,1024]{2,1,0:T(8,128)(2,1)} custom-call(bf16[8,32]{1,0:T(8,128)(2,1)} %fusion.1.sel_ref, bf16[4,544,1024]{2,1,0:T(8,128)(2,1)} %collective-permute-done.4.pay_ref, bf16[2,8,144,1024]{3,2,1,0:T(8,128)(2,1)} %bitcast.104, bf16[2,8,144,1024]{3,2,1,0:T(8,128)(2,1)} %bitcast.96, bf16[2,8,144,1024]{3,2,1,0:T(8,128)(2,1)} %bitcast.106, ...), custom_call_target="tpu_custom_call" | custom-call | flops 4831838208 | bytes 20971520 | tf_op jit(solution)/shard_map/combine/pallas_call | solution.py:484
  386.8 35.6 %experts.6 = (bf16[2,1152,1024]{2,1,0:T(8,128)(2,1)}, bf16[2,1152,1024]{2,1,0:T(8,128)(2,1)}, f32[2,1152,1]{2,1,0:T(8,128)}, bf16[4,2,768,512]{3,2,1,0:T(8,128)(2,1)}) custom-call(bf16[4,1152,1024]{2,1,0:T(8,128)(2,1)} %bitcast.109, bf16[4,1152,1024]{2,1,0:T(8,128)(2,1)} %bitcast.111, bf16[4,2,768,512]{3,2,1,0:T(8,128)(2,1)} %bitcast.154, ...), custom_call_target="tpu_custom_call" | custom-call | flops 21743271936 | bytes 31457280 | tf_op jit(solution)/shard_map/experts/pallas_call | solution.py:384
  422.4 12.4 %combine.6 = bf16[4,1056,1024]{2,1,0:T(8,128)(2,1)} custom-call(bf16[8,32]{1,0:T(8,128)(2,1)} %fusion.1.sel_ref, bf16[4,544,1024]{2,1,0:T(8,128)(2,1)} %collective-permute-done.21.pay_ref, bf16[2,8,144,1024]{3,2,1,0:T(8,128)(2,1)} %bitcast.100, bf16[2,8,144,1024]{3,2,1,0:T(8,128)(2,1)} %bitcast.92, bf16[2,8,144,1024]{3,2,1,0:T(8,128)(2,1)} %bitcast.102, ...), custom_call_target="tpu_custom_call" | custom-call | flops 4831838208 | bytes 20971520 | tf_op jit(solution)/shard_map/combine/pallas_call | solution.py:484
  435.2 16.0 %combine.5 = (bf16[528,1024]{1,0:T(8,128)(2,1)}, bf16[528,1024]{1,0:T(8,128)(2,1)}, bf16[528,1024]{1,0:T(8,128)(2,1)}, bf16[528,1024]{1,0:T(8,128)(2,1)}, bf16[5...) custom-call(bf16[8,32]{1,0:T(8,128)(2,1)} %fusion.1.sel_ref, ...), custom_call_target="tpu_custom_call" | custom-call | flops 4831838208 | bytes 20971520 | tf_op jit(solution)/shard_map/combine/pallas_call | solution.py:484
  452.7 15.8 %combine.7 = (bf16[528,1024]{1,0:T(8,128)(2,1)}, bf16[528,1024]{1,0:T(8,128)(2,1)}, bf16[528,1024]{1,0:T(8,128)(2,1)}, bf16[528,1024]{1,0:T(8,128)(2,1)}, bf16[5...) custom-call(bf16[8,32]{1,0:T(8,128)(2,1)} %fusion.1.sel_ref, ...), custom_call_target="tpu_custom_call" | custom-call | flops 4831838208 | bytes 20971520 | tf_op jit(solution)/shard_map/combine/pallas_call | solution.py:484
  484.0 17.3 %collective-permute-done.31 = bf16[528,1024]{1,0:T(8,128)(2,1)S(1)} collective-permute-done((bf16[528,1024]{1,0:T(8,128)(2,1)}, bf16[528,1024]{1,0:T(8,128)(2,1)S(1)}, u32[]{:S(2)}, u32[]{:S(2)}) %collective-permute-start.31) | collective-permute-done | bytes 1081376 | tf_op jit(solution)/shard_map/ppermute | solution.py:861
  505.6 20.1 %collective-permute-done.29 = bf16[528,1024]{1,0:T(8,128)(2,1)S(1)} collective-permute-done((bf16[528,1024]{1,0:T(8,128)(2,1)}, bf16[528,1024]{1,0:T(8,128)(2,1)S(1)}, u32[]{:S(2)}, u32[]{:S(2)}) %collective-permute-start.29) | collective-permute-done | bytes 1081376 | tf_op jit(solution)/shard_map/ppermute | solution.py:861
  530.0 18.9 %collective-permute-done.15.refs_21_ = bf16[528,1024]{1,0:T(8,128)(2,1)S(1)} collective-permute-done((bf16[528,1024]{1,0:T(8,128)(2,1)S(1)}, bf16[528,1024]{1,0:T(8,128)(2,1)S(1)}, u32[]{:S(2)}, u32[]{:S(2)}) %collective-permute-start.15) | collective-permute-done | bytes 1081376 | tf_op jit(solution)/shard_map/ppermute | solution.py:861
  550.7 37.4 %attention_backward.2 = (bf16[512,1024]{1,0:T(8,128)(2,1)}, f32[512,1024]{1,0:T(8,128)}, bf16[1024,3200]{1,0:T(8,128)(2,1)}) custom-call(bf16[512,1024]{1,0:T(8,128)(2,1)} %get-tuple-element.189.x_ref.refs_0_, bf16[1024,3200]{1,0:T(8,128)(2,1)} %gather_layer.1.w_ref.refs_1_, f32[1,1024]{1,0:T(1,128)} %bitcast.147, f32[1,1024]{1,0:T(1,128)} %bitcast.143, ...), custom_call_target="tpu_custom_call" | custom-call | flops 17179869184 | bytes 41943040 | tf_op jit(solution)/shard_map/attention_backward/pallas_call | solution.py:629
  594.1 39.1 %attention_backward.3 = (bf16[512,1024]{1,0:T(8,128)(2,1)}, f32[512,1024]{1,0:T(8,128)}, bf16[1024,3200]{1,0:T(8,128)(2,1)}) custom-call(bf16[512,1024]{1,0:T(8,128)(2,1)} %get-tuple-element.190.x_ref.refs_0_, bf16[1024,3200]{1,0:T(8,128)(2,1)} %gather_layer.1.w_ref.refs_1_, f32[1,1024]{1,0:T(1,128)} %bitcast.148, f32[1,1024]{1,0:T(1,128)} %bitcast.144, ...), custom_call_target="tpu_custom_call" | custom-call | flops 17179869184 | bytes 41943040 | tf_op jit(solution)/shard_map/attention_backward/pallas_call | solution.py:629
  633.2 60.5 %reduce_layer.1 = f32[32,3200]{1,0:T(8,128)} custom-call(bf16[1024,3200]{1,0:T(8,128)(2,1)} %get-tuple-element.135.pack_ref), custom_call_target="tpu_custom_call" | custom-call | tf_op jit(solution)/shard_map/reduce_layer/pallas_call | solution.py:839
  (177 shorter events, 141.4 us)
Async XLA Ops:
  7.2 261.8 %all-gather.7.cloned.1.call-start = ((), (), s32[]{:S(2)}) async-start(), calls=%async_computation.5 | async-start | bytes 7864320 | tf_op jit(solution)/shard_map/all_gather | solution.py:910
  11.2 328.4 %all-gather.5.cloned.1.call-start = ((), (), s32[]{:S(2)}) async-start(), calls=%async_computation.4 | async-start | bytes 7864320 | tf_op jit(solution)/shard_map/all_gather | solution.py:910
  64.7 57.9 %collective-permute-start.5 = (bf16[512,1024]{1,0:T(8,128)(2,1)}, bf16[512,1024]{1,0:T(8,128)(2,1)}, u32[]{:S(2)}, u32[]{:S(2)}) collective-permute-start(bf16[512,1024]{1,0:T(8,128)(2,1)} %get-tuple-element.186), channel_id=1, source_target_pairs={{0,8},{4,12},{8,0},{12,4},{16,24},{20,28},{24,16},{28,20},{1,9},{5... | collective-permute-start | bytes 3145736 | tf_op jit(solution)/shard_map/ppermute | solution.py:861
  65.6 57.1 %collective-permute-start.6 = (bf16[512,1024]{1,0:T(8,128)(2,1)}, bf16[512,1024]{1,0:T(8,128)(2,1)}, u32[]{:S(2)}, u32[]{:S(2)}) collective-permute-start(bf16[512,1024]{1,0:T(8,128)(2,1)} %get-tuple-element.186), channel_id=1, source_target_pairs={{0,16},{4,20},{8,24},{12,28},{16,0},{20,4},{24,8},{28,12},{1,17},{... | collective-permute-start | bytes 3145736 | tf_op jit(solution)/shard_map/ppermute | solution.py:861
  65.6 58.3 %collective-permute-start.22 = (bf16[512,1024]{1,0:T(8,128)(2,1)}, bf16[512,1024]{1,0:T(8,128)(2,1)}, u32[]{:S(2)}, u32[]{:S(2)}) collective-permute-start(bf16[512,1024]{1,0:T(8,128)(2,1)} %get-tuple-element.187), channel_id=1, source_target_pairs={{0,8},{4,12},{8,0},{12,4},{16,24},{20,28},{24,16},{28,20},{1,9},{5... | collective-permute-start | bytes 3145736 | tf_op jit(solution)/shard_map/ppermute | solution.py:861
  66.7 62.9 %collective-permute-start.23 = (bf16[512,1024]{1,0:T(8,128)(2,1)}, bf16[512,1024]{1,0:T(8,128)(2,1)}, u32[]{:S(2)}, u32[]{:S(2)}) collective-permute-start(bf16[512,1024]{1,0:T(8,128)(2,1)} %get-tuple-element.187), channel_id=1, source_target_pairs={{0,16},{4,20},{8,24},{12,28},{16,0},{20,4},{24,8},{28,12},{1,17},{... | collective-permute-start | bytes 3145736 | tf_op jit(solution)/shard_map/ppermute | solution.py:861
  98.1 39.3 %collective-permute-start = (bf16[544,1024]{1,0:T(8,128)(2,1)}, bf16[544,1024]{1,0:T(8,128)(2,1)}, u32[]{:S(2)}, u32[]{:S(2)}) collective-permute-start(bf16[544,1024]{1,0:T(8,128)(2,1)} %get-tuple-element.81.refs_15_), channel_id=1, source_target_pairs={{0,8},{4,12},{8,0},{12,4},{16,24},{20,28},{24,16},{28,20},{1,9},{5... | collective-permute-start | bytes 3342344 | tf_op jit(solution)/shard_map/ppermute | solution.py:861
  123.8 50.3 %collective-permute-start.18 = (bf16[544,1024]{1,0:T(8,128)(2,1)}, bf16[544,1024]{1,0:T(8,128)(2,1)S(1)}, u32[]{:S(2)}, u32[]{:S(2)}) collective-permute-start(bf16[544,1024]{1,0:T(8,128)(2,1)} %get-tuple-element.109.refs_15_), channel_id=1, source_target_pairs={{0,16},{4,20},{8,24},{12,28},{16,0},{20,4},{24,8},{28,12},{1,17},{... | collective-permute-start | bytes 3342344 | tf_op jit(solution)/shard_map/ppermute | solution.py:861
  129.5 55.9 %collective-permute-start.7 = (bf16[256,1024]{1,0:T(8,128)(2,1)}, bf16[256,1024]{1,0:T(8,128)(2,1)}, u32[]{:S(2)}, u32[]{:S(2)}) collective-permute-start(bf16[256,1024]{1,0:T(8,128)(2,1)} %slice.134), channel_id=1, source_target_pairs={{0,16},{4,20},{8,24},{12,28},{16,0},{20,4},{24,8},{28,12},{1,17},{... | collective-permute-start | bytes 1572872 | tf_op jit(solution)/shard_map/ppermute | solution.py:861
  137.4 49.3 %collective-permute-start.8 = (bf16[256,1024]{1,0:T(8,128)(2,1)}, bf16[256,1024]{1,0:T(8,128)(2,1)}, u32[]{:S(2)}, u32[]{:S(2)}) collective-permute-start(bf16[256,1024]{1,0:T(8,128)(2,1)} %slice.135), channel_id=1, source_target_pairs={{0,8},{4,12},{8,0},{12,4},{16,24},{20,28},{24,16},{28,20},{1,9},{5... | collective-permute-start | bytes 1572872 | tf_op jit(solution)/shard_map/ppermute | solution.py:861
  150.3 46.5 %collective-permute-start.24 = (bf16[256,1024]{1,0:T(8,128)(2,1)}, bf16[256,1024]{1,0:T(8,128)(2,1)}, u32[]{:S(2)}, u32[]{:S(2)}) collective-permute-start(bf16[256,1024]{1,0:T(8,128)(2,1)} %slice.140), channel_id=1, source_target_pairs={{0,16},{4,20},{8,24},{12,28},{16,0},{20,4},{24,8},{28,12},{1,17},{... | collective-permute-start | bytes 1572872 | tf_op jit(solution)/shard_map/ppermute | solution.py:861
  162.0 541.4 %reduce-scatter.5.cloned.1.call-start = ((), (), s32[]{:S(2)}) async-start(), calls=%async_computation.3 | async-start | bytes 7864320 | tf_op jit(solution)/shard_map/reduce_scatter | solution.py:949
  197.9 49.5 %collective-permute-start.9 = (bf16[4,512,1024]{2,1,0:T(8,128)(2,1)}, bf16[4,512,1024]{2,1,0:T(8,128)(2,1)}, u32[]{:S(2)}, u32[]{:S(2)}) collective-permute-start(bf16[4,512,1024]{2,1,0:T(8,128)(2,1)} %pad_maximum_fusion.2.grad_ref), channel_id=1, source_target_pairs={{0,4},{4,0},{8,12},{12,8},{16,20},{20,16},{24,28},{28,24},{1,5},{5... | collective-permute-start | bytes 12582920 | tf_op jit(solution)/shard_map/ppermute | solution.py:861
  339.6 363.8 %reduce-scatter.3.cloned.1.call-start = ((), (), s32[]{:S(2)}) async-start(), calls=%async_computation.2 | async-start | bytes 7864320 | tf_op jit(solution)/shard_map/reduce_scatter | solution.py:949
  386.7 48.4 %collective-permute-start.10 = (bf16[4,1056,1024]{2,1,0:T(8,128)(2,1)}, bf16[4,1056,1024]{2,1,0:T(8,128)(2,1)}, u32[]{:S(2)}, u32[]{:S(2)}) collective-permute-start(bf16[4,1056,1024]{2,1,0:T(8,128)(2,1)} %combine.4), channel_id=1, source_target_pairs={{0,4},{4,0},{8,12},{12,8},{16,20},{20,16},{24,28},{28,24},{1,5},{5... | collective-permute-start | bytes 25952264 | tf_op jit(solution)/shard_map/ppermute | solution.py:861
  469.7 58.3 %collective-permute-start.11 = (bf16[528,1024]{1,0:T(8,128)(2,1)}, bf16[528,1024]{1,0:T(8,128)(2,1)S(1)}, u32[]{:S(2)}, u32[]{:S(2)}) collective-permute-start(bf16[528,1024]{1,0:T(8,128)(2,1)} %get-tuple-element.96), channel_id=1, source_target_pairs={{0,8},{4,12},{8,0},{12,4},{16,24},{20,28},{24,16},{28,20},{1,9},{5... | collective-permute-start | bytes 3244040 | tf_op jit(solution)/shard_map/ppermute | solution.py:861
  470.6 57.7 %collective-permute-start.16 = (bf16[528,1024]{1,0:T(8,128)(2,1)}, bf16[528,1024]{1,0:T(8,128)(2,1)S(1)}, u32[]{:S(2)}, u32[]{:S(2)}) collective-permute-start(bf16[528,1024]{1,0:T(8,128)(2,1)} %get-tuple-element.101), channel_id=1, source_target_pairs={{0,16},{4,20},{8,24},{12,28},{16,0},{20,4},{24,8},{28,12},{1,17},{... | collective-permute-start | bytes 3244040 | tf_op jit(solution)/shard_map/ppermute | solution.py:861
  478.3 47.5 %collective-permute-start.29 = (bf16[528,1024]{1,0:T(8,128)(2,1)}, bf16[528,1024]{1,0:T(8,128)(2,1)S(1)}, u32[]{:S(2)}, u32[]{:S(2)}) collective-permute-start(bf16[528,1024]{1,0:T(8,128)(2,1)} %get-tuple-element.127), channel_id=1, source_target_pairs={{0,16},{4,20},{8,24},{12,28},{16,0},{20,4},{24,8},{28,12},{1,17},{... | collective-permute-start | bytes 3244040 | tf_op jit(solution)/shard_map/ppermute | solution.py:861
  480.7 68.2 %collective-permute-start.15 = (bf16[528,1024]{1,0:T(8,128)(2,1)S(1)}, bf16[528,1024]{1,0:T(8,128)(2,1)S(1)}, u32[]{:S(2)}, u32[]{:S(2)}) collective-permute-start(bf16[528,1024]{1,0:T(8,128)(2,1)S(1)} %add_convert_fusion.2), channel_id=1, source_target_pairs={{0,16},{4,20},{8,24},{12,28},{16,0},{20,4},{24,8},{28,12},{1,17},{... | collective-permute-start | bytes 3244040 | tf_op jit(solution)/shard_map/ppermute | solution.py:861
  501.3 48.4 %collective-permute-start.13 = (bf16[528,1024]{1,0:T(8,128)(2,1)S(1)}, bf16[528,1024]{1,0:T(8,128)(2,1)S(1)}, u32[]{:S(2)}, u32[]{:S(2)}) collective-permute-start(bf16[528,1024]{1,0:T(8,128)(2,1)S(1)} %add_convert_fusion.3), channel_id=1, source_target_pairs={{0,8},{4,12},{8,0},{12,4},{16,24},{20,28},{24,16},{28,20},{1,9},{5... | collective-permute-start | bytes 3244040 | tf_op jit(solution)/shard_map/ppermute | solution.py:861
  525.7 62.4 %collective-permute-start.28 = (bf16[528,1024]{1,0:T(8,128)(2,1)}, bf16[528,1024]{1,0:T(8,128)(2,1)}, u32[]{:S(2)}, u32[]{:S(2)}) collective-permute-start(bf16[528,1024]{1,0:T(8,128)(2,1)} %get-tuple-element.125), channel_id=1, source_target_pairs={{0,8},{4,12},{8,0},{12,4},{16,24},{20,28},{24,16},{28,20},{1,9},{5... | collective-permute-start | bytes 3244040 | tf_op jit(solution)/shard_map/ppermute | solution.py:861
  527.9 60.2 %collective-permute-start.33 = (bf16[528,1024]{1,0:T(8,128)(2,1)}, bf16[528,1024]{1,0:T(8,128)(2,1)}, u32[]{:S(2)}, u32[]{:S(2)}) collective-permute-start(bf16[528,1024]{1,0:T(8,128)(2,1)} %get-tuple-element.130), channel_id=1, source_target_pairs={{0,16},{4,20},{8,24},{12,28},{16,0},{20,4},{24,8},{28,12},{1,17},{... | collective-permute-start | bytes 3244040 | tf_op jit(solution)/shard_map/ppermute | solution.py:861
  528.4 65.7 %collective-permute-start.32 = (bf16[528,1024]{1,0:T(8,128)(2,1)}, bf16[528,1024]{1,0:T(8,128)(2,1)}, u32[]{:S(2)}, u32[]{:S(2)}) collective-permute-start(bf16[528,1024]{1,0:T(8,128)(2,1)} %add_convert_fusion), channel_id=1, source_target_pairs={{0,16},{4,20},{8,24},{12,28},{16,0},{20,4},{24,8},{28,12},{1,17},{... | collective-permute-start | bytes 3244040 | tf_op jit(solution)/shard_map/ppermute | solution.py:861
  548.9 45.2 %collective-permute-start.30 = (bf16[528,1024]{1,0:T(8,128)(2,1)}, bf16[528,1024]{1,0:T(8,128)(2,1)}, u32[]{:S(2)}, u32[]{:S(2)}) collective-permute-start(bf16[528,1024]{1,0:T(8,128)(2,1)} %add_convert_fusion.1), channel_id=1, source_target_pairs={{0,8},{4,12},{8,0},{12,4},{16,24},{20,28},{24,16},{28,20},{1,9},{5... | collective-permute-start | bytes 3244040 | tf_op jit(solution)/shard_map/ppermute | solution.py:861
  (41 other events, 691.8 us)
Sparse Core Ops, SparseCore 0:
  11.4 127.4 all-gather.6
  162.2 120.8 all-gather.4
  339.7 116.1 reduce-scatter.4
  458.0 111.2 reduce-scatter.2

commit v3 on v2

--- a/solution.py
+++ b/solution.py
@@ -58,6 +58,13 @@
         lower, pltpu.roll(block, LANES - half, 1), pltpu.roll(block, half, 1)
     )
     return block * cosine + partner * sine
+
+
+def hint(flops, transcendentals, bytes_accessed, share=16):
+    return pl.CostEstimate(
+        flops=flops // share, transcendentals=transcendentals // share,
+        bytes_accessed=bytes_accessed // share,
+    )
 
 
 def tile_ds(index, width):
@@ -176,7 +183,7 @@
         out_shape=out_shape,
         scratch_shapes=[pltpu.VMEM((rows, width), BF), pltpu.VMEM((rows, rows), F32)],
         compiler_params=pltpu.CompilerParams(vmem_limit_bytes=VMEM_LIMIT),
-        cost_estimate=pl.CostEstimate(
+        cost_estimate=hint(
             flops=flops, transcendentals=QUERY_HEADS * rows * rows, bytes_accessed=16 << 20
         ),
         name="attention_forward",
@@ -249,7 +256,7 @@
         scratch_shapes=[pltpu.VMEM((rows, rows), BF)],
         input_output_aliases=aliases,
         compiler_params=pltpu.CompilerParams(vmem_limit_bytes=VMEM_LIMIT),
-        cost_estimate=pl.CostEstimate(
+        cost_estimate=hint(
             flops=4 * count * local * CAP * rows * width, transcendentals=0, bytes_accessed=20 << 20
         ),
         name="dispatch",
@@ -399,9 +406,9 @@
             pltpu.VMEM((hidden, width) if kept else (8, LANES), F32),
         ],
         compiler_params=pltpu.CompilerParams(vmem_limit_bytes=VMEM_LIMIT),
-        cost_estimate=pl.CostEstimate(
+        cost_estimate=hint(
             flops=18 * count * total * width * hidden, transcendentals=count * total * hidden,
-            bytes_accessed=30 << 20,
+            bytes_accessed=30 << 20, share=16 if prior is None else 1,
         ),
         name="experts",
     )(*operands)
@@ -489,8 +496,8 @@
         out_specs=out_specs,
         scratch_shapes=[pltpu.VMEM((rows, rows), BF)],
         compiler_params=pltpu.CompilerParams(vmem_limit_bytes=VMEM_LIMIT),
-        cost_estimate=pl.CostEstimate(
-            flops=4 * count * local * CAP * rows * width, transcendentals=0, bytes_accessed=20 << 20
+        cost_estimate=hint(
+            flops=4 * count * local * CAP * rows * width, transcendentals=0, bytes_accessed=20 << 20, share=1
         ),
         name="combine",
     )(*operands)
@@ -645,8 +652,8 @@
             pltpu.VMEM((rows, width), BF),
         ],
         compiler_params=pltpu.CompilerParams(vmem_limit_bytes=VMEM_LIMIT),
-        cost_estimate=pl.CostEstimate(
-            flops=flops, transcendentals=QUERY_HEADS * rows * rows, bytes_accessed=40 << 20
+        cost_estimate=hint(
+            flops=flops, transcendentals=QUERY_HEADS * rows * rows, bytes_accessed=40 << 20, share=1
         ),
         name="attention_backward",
     )(*operands)
@@ -853,6 +860,7 @@
         compiler_params=pltpu.CompilerParams(
             collective_id=2, has_side_effects=True, vmem_limit_bytes=VMEM_LIMIT
         ),
+        cost_estimate=pl.CostEstimate(flops=0, transcendentals=0, bytes_accessed=1 << 30),
         name="reduce_layer",
     )(pack)
 
@@ -861,28 +869,57 @@
     return lax.ppermute(value, "fsdp", [(i, i ^ distance) for i in range(size)])
 
 
-def gather_chips(value, size):
+def after(value, *earlier):
+    return lax.optimization_barrier((value, *earlier))[0] if earlier else value
+
+
+def send_near(value, size):
+    return swap(value, 2, size), swap(value, 4, size)
+
+
+def gather_chips(value, near, size):
+    chips = size // 2
+    if near is None:
+        return [value] + [swap(value, 2 * r, size) for r in range(1, chips)]
+    half = value.shape[0] // 2
+    one, two = near
+    return [value, one, two, swap(one[:half], 4, size), swap(two[half:], 2, size)]
+
+
+def both_cores(pieces, size, *earlier):
+    if earlier:
+        pieces = [pieces[0]] + [after(p, *earlier) for p in pieces[1:]]
+    chips = size // 2
+    mine = jnp.stack(pieces[: chips - 1] + [jnp.concatenate(pieces[chips - 1 :])])
+    return mine, swap(mine, 1, size)
+
+
+def scatter_near(kept, size, *earlier):
     chips = size // 2
     if chips != 4:
-        return jnp.stack([value] + [swap(value, 2 * r, size) for r in range(1, chips)])
-    half = value.shape[0] // 2
-    one, two = swap(value, 2, size), swap(value, 4, size)
-    three = jnp.concatenate([swap(one[:half], 4, size), swap(two[half:], 2, size)])
-    return jnp.stack([value, one, two, three])
-
-
-def scatter_chips(kept, size):
-    chips = size // 2
-    if chips != 4:
-        return [kept[0], kept[1]] + [swap(kept[2 * r + h], 2 * r, size) for r in range(1, chips) for h in range(2)]
+        return [swap(kept[2 * r + h], 2 * r, size) for r in range(1, chips) for h in range(2)]
+    return [swap(after(kept[6], *earlier), 2, size), swap(after(kept[7], *earlier), 4, size)]
+
+
+def scatter_far(kept, near, size, *earlier):
+    if size != 8:
+        return (), ()
     add = lambda a, b: (a.astype(F32) + b.astype(F32)).astype(BF)
-    by_one = swap(kept[6], 2, size)
-    by_two = swap(kept[7], 4, size)
-    one_first = swap(kept[2], 2, size)
-    two_second = swap(kept[5], 4, size)
-    one_second = swap(add(kept[3], by_two), 2, size)
-    two_first = swap(add(kept[4], by_one), 4, size)
-    return [kept[0], kept[1], one_first, one_second, two_first, two_second]
+    by_one, by_two = after(near[0], *earlier), after(near[1], *earlier)
+    one_sum, two_sum = add(kept[3], by_two), add(kept[4], by_one)
+    return (one_sum, two_sum), (swap(one_sum, 2, size), swap(two_sum, 4, size))
+
+
+def scatter_rest(kept, size, *earlier):
+    if size != 8:
+        return ()
+    return swap(after(kept[2], *earlier), 2, size), swap(after(kept[5], *earlier), 4, size)
+
+
+def scattered(kept, near, far, rest):
+    if not far:
+        return [kept[0], kept[1]] + near
+    return [kept[0], kept[1], rest[0], far[0], far[1], rest[1]]
 
 
 def local(
@@ -921,52 +958,99 @@
     first = lax.axis_index("fsdp") * held
     places = jnp.arange(8)[:, None]
     sel = ((jnp.arange(experts)[None, :] == first + places) & (places < held)).astype(BF)
-    later, _ = lax.optimization_barrier((out_grad, pack))
-
-    saved, pays, grads = [], [], []
-    for m in range(micro):
-        x = inputs[m, 0]
-        q, k, v, att, lse, res, pay, gates = attention_forward(
+    square = chips == 4
+
+    def forward(m, x):
+        return attention_forward(
             x, pack, gain_one, gain_two, block_ids[m, 0], routes[m, 0], tables, q_width, kv_width, experts
         )
-        saved.append((q, k, v, att, lse, res, pay, gates))
-        mine = gather_chips(later[m, 0], owners)
-        grads.append((mine, swap(mine, 1, owners)))
-        mine = gather_chips(pay, owners)
-        pays.append((mine, swap(mine, 1, owners)))
-    moved = []
-    for m in range(micro):
+
+    def dispatched(m, pay, grad):
         carried = None
         for side in range(2):
-            carried = dispatch(sel, pays[m][side], grads[m][side], side, 2, held, carried)
-        moved.append([c.reshape(held, 2 * chips * CAP, width) for c in carried])
-    order = [(m, g) for m in range(micro) for g in range(len(weights))]
-    done = {}
-    for m, g in order:
+            carried = dispatch(sel, pay[side], grad[side], side, 2, held, carried)
+        return [c.reshape(held, 2 * chips * CAP, width) for c in carried]
+
+    saved, arrived, pays, moved, done, terms = [], [], [], [], {}, []
+    ready = ()
+    for m in range(micro):
+        grad = after(out_grad[m, 0], *ready)
+        grad_near = send_near(grad, owners) if square else None
+        if m == 0:
+            saved.append(forward(0, after(inputs[0, 0], *(grad_near if square else ()))))
+            for n in range(1, micro):
+                saved.append(forward(n, after(inputs[n, 0], saved[n - 1][4])))
+        pay = saved[m][6]
+        pay_near = None
+        if square and m == 0:
+            one, two = send_near(pay, owners)
+            ready = (one,)
+            pay_near = after(one, saved[-1][4]), after(two, saved[-1][4])
+        elif m:
+            pay = after(pay, *arrived[m - 1][0][1:])
+            ready = (pay,)
+        arrived.append((gather_chips(pay, pay_near, owners), gather_chips(grad, grad_near, owners), grad_near))
+
+    def expert_part(m, g, *earlier):
         prior = done[m - 1, g][3] if m else None
-        done[m, g] = experts_step(g * group, weights[g], *moved[m], prior)
-    sums = [
-        lax.psum_scatter(done[micro - 1, g][3], "dp", scatter_dimension=0, tiled=True)[0]
-        for g in range(len(weights))
-    ]
-    terms = []
-    for m in range(micro):
+        rows_in, slot_grad = moved[m]
+        if earlier:
+            rows_in = after(rows_in, *earlier)
+        done[m, g] = experts_step(g * group, weights[g], rows_in, slot_grad, prior)
+
+    def returned(m, earlier):
         parts = [
             [done[m, g][i].reshape(group, 2 * chips, CAP, -1) for g in range(len(weights))]
             for i in range(3)
         ]
-        (sent,) = combine(sel, pays[m][1], *parts, 1, None)
-        kept = combine(sel, pays[m][0], *parts, 0, swap(sent, 1, owners))
-        terms.append(scatter_chips(kept, owners))
+        (sent,) = combine(sel, after(pays[m][1], *earlier), *parts, 1, None)
+        return combine(sel, pays[m][0], *parts, 0, swap(sent, 1, owners))
+
     outputs, input_grads = [], []
-    prior = None
-    for m in range(micro):
+
+    def backward(m, found, prior):
         out, in_grad, prior = attention_backward(
             inputs[m, 0], pack, gain_one, gain_two, block_ids[m, 0], tables, out_grad[m, 0], saved[m],
-            terms[m], prior, q_width, kv_width, experts,
+            found, prior, q_width, kv_width, experts,
         )
         outputs.append(out)
         input_grads.append(in_grad)
+        return prior
+
+    added, far, rest = (), (), ()
+    for m in range(micro):
+        held_back = (done[m - 1, 0][2],) if m else ()
+        pay_held = arrived[m + 1][2] if m == 0 and micro > 1 and square else held_back
+        pays.append(both_cores(arrived[m][0], owners, *pay_held))
+        moved.append(dispatched(m, pays[m], both_cores(arrived[m][1], owners, *held_back)))
+        hold = arrived[m + 1][2] if m + 1 < micro and square else ()
+        if m == 0:
+            expert_part(0, 0, *hold)
+        else:
+            for g in range(1, len(weights)):
+                expert_part(m - 1, g, moved[m][0])
+            kept = returned(m - 1, far)
+            near = scatter_near(kept, owners, *rest)
+            expert_part(m, 0, kept[-1])
+            added, far = scatter_far(kept, near, owners, done[m, 0][2])
+            rest = scatter_rest(kept, owners, *far)
+            terms.append(scattered(kept, near, far, rest))
+    for g in range(1, len(weights)):
+        expert_part(micro - 1, g, *added)
+    kept = returned(micro - 1, far)
+    near = scatter_near(kept, owners, *rest)
+    last_rest = scatter_rest(kept, owners, *rest)
+    prior, held_back = None, ()
+    for m in range(micro - 1):
+        prior = backward(m, [after(terms[m][0], kept[-1])] + terms[m][1:], prior)
+        held_back = (prior,)
+    last_far = scatter_far(kept, near, owners, *held_back)[1]
+    terms.append(scattered(kept, near, last_far, last_rest))
+    prior = backward(micro - 1, terms[-1], prior)
+    sums = []
+    for g in range(len(weights)):
+        summed = after(done[micro - 1, g][3], *(far if g else added))
+        sums.append(lax.psum_scatter(summed, "dp", scatter_dimension=0, tiled=True)[0])
     layer = reduce_layer(prior, chips, depth, 5)
     marks = np.cumsum([0, q_width, kv_width, kv_width, width, experts, 1, 1])
     cut = [layer[:, a:b] for a, b in zip(marks[:-1], marks[1:])]

time: 721 us -> 704 us (0.976)
  waiting for transfers between devices: 138 us -> 107 us
  starting transfers between devices: 25.8 us -> 35.5 us
    ppermute x34 -> x33, waiting for transfers between devices: 138 us -> 88.7 us  [swap(): return lax.ppermute(value, 'fsdp', [(i, i ^ distance) for i in range(size)])]
    all_gather x2, waiting for transfers between devices: 0.02 us -> 17.8 us  [local(): lax.all_gather(packed[g:g + group], 'dp', axis=0, tiled=False)]
    pallas_call x1, Pallas kernels: 50 us -> 59.6 us  [gather_layer(): pl.pallas_call(functools.partial(gather_layer_kernel, chips=chips, depth=...]
    ppermute x34 -> x33, starting transfers between devices: 25.6 us -> 34.9 us  [swap(): return lax.ppermute(value, 'fsdp', [(i, i ^ distance) for i in range(size)])]
    pallas_call x1, Pallas kernels: 60.5 us -> 51.6 us  [reduce_layer(): pl.pallas_call(functools.partial(reduce_layer_kernel, chips=chips, depth=...]
    another operation x8 -> x7, other arithmetic: 15.8 us -> 17.1 us  [both_cores(): mine = jnp.stack(pieces[:chips - 1] + [jnp.concatenate(pieces[chips - 1:])])]
  transfers between devices with their start and end apart: 38 -> 37, of which waited for: 13 -> 10; matrix products, arithmetic and copies ran while one was open for 8% -> 7% of each run, Pallas kernels for 66% -> 59%
where the time goes in v3:
time: 704 us; the launch traced here: 699 us
  Pallas kernels  473 us (67%)
  waiting for transfers between devices  107 us (15%)
  other arithmetic  37.1 us (5%)
  starting transfers between devices  35.5 us (5%)
  local copies, waits for them, and re-layouts  32 us (5%)
  between operations  14.4 us (2%)
    pallas_call x4, Pallas kernels, experts_step(): pl.pallas_call(functools.partial(expert_kernel, chunk=rows // 3, tile=256...  142 us
    ppermute x33, waiting for transfers between devices, swap(): return lax.ppermute(value, 'fsdp', [(i, i ^ distance) for i in range(size)])  88.7 us
    pallas_call x2, Pallas kernels, attention_backward(): pl.pallas_call(functools.partial(attention_backward_kernel, terms=len(ter...  76.6 us
    pallas_call x1, Pallas kernels, gather_layer(): pl.pallas_call(functools.partial(gather_layer_kernel, chips=chips, depth=...  59.6 us
    pallas_call x4, Pallas kernels, combine(): pl.pallas_call(functools.partial(combine_kernel, groups=groups, local=loc...  56.2 us
    pallas_call x1, Pallas kernels, reduce_layer(): pl.pallas_call(functools.partial(reduce_layer_kernel, chips=chips, depth=...  51.6 us
    pallas_call x2, Pallas kernels, attention_forward(): pl.pallas_call(functools.partial(attention_forward_kernel, q_width=q_widt...  43.7 us
    pallas_call x4, Pallas kernels, dispatch(): pl.pallas_call(functools.partial(dispatch_kernel, local=local), out_shape...  43.5 us
  transfers between devices with their start and end apart: 37, of which 10 were waited for; matrix products, arithmetic and copies ran while one was open for 7% of the time, Pallas kernels for 59%

profile of v3, /device:TPU:0, one launch (start us, length us, event | category | flops | bytes accessed | tf_op | source)
XLA Modules:
  0.0 699.1 jit_solution(728720166199921142)
XLA Ops:
  19.2 59.6 %gather_layer.1.w_ref.refs_1_ = bf16[1024,3200]{1,0:T(8,128)(2,1)} custom-call(bf16[32,3200]{1,0:T(8,128)(2,1)} %concatenate.18.w_ref), custom_call_target="tpu_custom_call" | custom-call | tf_op jit(solution)/shard_map/gather_layer/pallas_call | solution.py:743
  84.6 22.0 %attention_forward.2 = (bf16[512,1024]{1,0:T(8,128)(2,1)}, bf16[512,512]{1,0:T(8,128)(2,1)}, bf16[512,512]{1,0:T(8,128)(2,1)}, bf16[512,1024]{1,0:T(8,128)(2,1)}...) custom-call(bf16[512,1024]{1,0:T(8,128)(2,1)} %get-tuple-element.109.x_ref.refs_0_, ...), custom_call_target="tpu_custom_call" | custom-call | flops 469762048 | bytes 1048576 | tf_op jit(solution)/shard_map/attention_forward/pallas_call | solution.py:179
  112.0 22.3 %collective-permute-done.2 = bf16[544,1024]{1,0:T(8,128)(2,1)} collective-permute-done((bf16[544,1024]{1,0:T(8,128)(2,1)}, bf16[544,1024]{1,0:T(8,128)(2,1)}, u32[]{:S(2)}, u32[]{:S(2)}) %collective-permute-start.2) | collective-permute-done | bytes 1114144 | tf_op jit(solution)/shard_map/ppermute | solution.py:869
  141.0 21.7 %attention_forward.3 = (bf16[512,1024]{1,0:T(8,128)(2,1)}, bf16[512,512]{1,0:T(8,128)(2,1)}, bf16[512,512]{1,0:T(8,128)(2,1)}, bf16[512,1024]{1,0:T(8,128)(2,1)}...) custom-call(bf16[512,1024]{1,0:T(8,128)(2,1)} %get-tuple-element.118.x_ref.refs_0_, ...), custom_call_target="tpu_custom_call" | custom-call | flops 469762048 | bytes 1048576 | tf_op jit(solution)/shard_map/attention_forward/pallas_call | solution.py:179
  167.6 5.4 collective-permute-done.9
  198.7 11.1 %dispatch.4 = (bf16[4,2,4,144,1024]{4,3,2,1,0:T(8,128)(2,1)}, bf16[4,2,4,144,1024]{4,3,2,1,0:T(8,128)(2,1)}) custom-call(bf16[8,32]{1,0:T(8,128)(2,1)} %fusion.1.sel_ref, bf16[4,544,1024]{2,1,0:T(8,128)(2,1)} %pad_maximum_fusion.pay_ref, bf16[4,512,1024]{2,1,0:T(8,128)(2,1)} %pad_maximum_fusion.2.grad_ref), custom_call_target="tpu_custom_call" | custom-call | flops 301989888 | bytes 1310720 | tf_op jit(solution)/shard_map/dispatch/pallas_call | solution.py:250
  212.3 10.8 %dispatch.5 = (bf16[4,2,4,144,1024]{4,3,2,1,0:T(8,128)(2,1)}, bf16[4,2,4,144,1024]{4,3,2,1,0:T(8,128)(2,1)}) custom-call(bf16[8,32]{1,0:T(8,128)(2,1)} %fusion.1.sel_ref, bf16[4,544,1024]{2,1,0:T(8,128)(2,1)} %collective-permute-done.8.pay_ref, bf16[4,512,1024]{2,1,0:T(8,128)(2,1)} %collective-permute-done.11.grad_ref, ...), custom_call_target="tpu_custom_call", output_to_operand_aliasing={{0}: (3, {}), {1}: (4, {})} | custom-call | flops 301989888 | bytes 1310720 | tf_op jit(solution)/shard_map/dispatch/pallas_call | solution.py:250
  223.1 34.8 %experts.4 = (bf16[2,1152,1024]{2,1,0:T(8,128)(2,1)}, bf16[2,1152,1024]{2,1,0:T(8,128)(2,1)}, f32[2,1152,1]{2,1,0:T(8,128)}, bf16[4,2,768,512]{3,2,1,0:T(8,128)(2,1)}) custom-call(bf16[4,1152,1024]{2,1,0:T(8,128)(2,1)} %bitcast.86, bf16[4,1152,1024]{2,1,0:T(8,128)(2,1)} %bitcast.88, bf16[4,2,768,512]{3,2,1,0:T(8,128)(2,1)} %bitcast.111), custom_call_target="tpu_custom_call" | custom-call | flops 1358954496 | bytes 1966080 | tf_op jit(solution)/shard_map/experts/pallas_call | solution.py:391
  267.0 10.8 %dispatch.6 = (bf16[4,2,4,144,1024]{4,3,2,1,0:T(8,128)(2,1)}, bf16[4,2,4,144,1024]{4,3,2,1,0:T(8,128)(2,1)}) custom-call(bf16[8,32]{1,0:T(8,128)(2,1)} %fusion.1.sel_ref, bf16[4,544,1024]{2,1,0:T(8,128)(2,1)} %pad_maximum_fusion.1.pay_ref, bf16[4,512,1024]{2,1,0:T(8,128)(2,1)} %pad_maximum_fusion.3.grad_ref), custom_call_target="tpu_custom_call" | custom-call | flops 301989888 | bytes 1310720 | tf_op jit(solution)/shard_map/dispatch/pallas_call | solution.py:250
  277.9 10.8 %dispatch.7 = (bf16[4,2,4,144,1024]{4,3,2,1,0:T(8,128)(2,1)}, bf16[4,2,4,144,1024]{4,3,2,1,0:T(8,128)(2,1)}) custom-call(bf16[8,32]{1,0:T(8,128)(2,1)} %fusion.1.sel_ref, bf16[4,544,1024]{2,1,0:T(8,128)(2,1)} %collective-permute-done.15.pay_ref, ...), custom_call_target="tpu_custom_call", output_to_operand_aliasing={{0}: (3, {}), {1}: (4, {})} | custom-call | flops 301989888 | bytes 1310720 | tf_op jit(solution)/shard_map/dispatch/pallas_call | solution.py:250
  288.7 17.8 %all-gather.7.cloned.1.call-done = bf16[8,768,512]{2,1,0:T(8,128)(2,1)} async-done(((bf16[2,768,512]{2,1,0:T(8,128)(2,1)}), bf16[8,768,512]{2,1,0:T(8,128)(2,1)}) %all-gather.7.cloned.1.call-update) | async-done | bytes 6291472 | tf_op jit(solution)/shard_map/all_gather | solution.py:947
  306.5 34.9 %experts.5 = (bf16[2,1152,1024]{2,1,0:T(8,128)(2,1)}, bf16[2,1152,1024]{2,1,0:T(8,128)(2,1)}, f32[2,1152,1]{2,1,0:T(8,128)}, bf16[4,2,768,512]{3,2,1,0:T(8,128)(2,1)}) custom-call(bf16[4,1152,1024]{2,1,0:T(8,128)(2,1)} %bitcast.87, bf16[4,1152,1024]{2,1,0:T(8,128)(2,1)} %bitcast.89, bf16[4,2,768,512]{3,2,1,0:T(8,128)(2,1)} %bitcast.113), custom_call_target="tpu_custom_call" | custom-call | flops 1358954496 | bytes 1966080 | tf_op jit(solution)/shard_map/experts/pallas_call | solution.py:391
  341.4 12.3 %combine.4 = bf16[4,1056,1024]{2,1,0:T(8,128)(2,1)} custom-call(bf16[8,32]{1,0:T(8,128)(2,1)} %fusion.1.sel_ref, bf16[4,544,1024]{2,1,0:T(8,128)(2,1)} %collective-permute-done.8.pay_ref, bf16[2,8,144,1024]{3,2,1,0:T(8,128)(2,1)} %bitcast.94, bf16[2,8,144,1024]{3,2,1,0:T(8,128)(2,1)} %bitcast.102, bf16[2,8,144,1024]{3,2,1,0:T(8,128)(2,1)} %bitcast.96, ...), custom_call_target="tpu_custom_call" | custom-call | flops 4831838208 | bytes 20971520 | tf_op jit(solution)/shard_map/combine/pallas_call | solution.py:491
  353.6 13.9 %collective-permute-done.19.refs_6_ = bf16[4,1056,1024]{2,1,0:T(8,128)(2,1)} collective-permute-done((bf16[4,1056,1024]{2,1,0:T(8,128)(2,1)}, bf16[4,1056,1024]{2,1,0:T(8,128)(2,1)}, u32[]{:S(2)}, u32[]{:S(2)}) %collective-permute-start.19) | collective-permute-done | bytes 8650784 | tf_op jit(solution)/shard_map/ppermute | solution.py:869
  367.5 15.8 %combine.5 = (bf16[528,1024]{1,0:T(8,128)(2,1)}, bf16[528,1024]{1,0:T(8,128)(2,1)}, bf16[528,1024]{1,0:T(8,128)(2,1)}, bf16[528,1024]{1,0:T(8,128)(2,1)}, bf16[5...) custom-call(bf16[8,32]{1,0:T(8,128)(2,1)} %fusion.1.sel_ref, ...), custom_call_target="tpu_custom_call" | custom-call | flops 4831838208 | bytes 20971520 | tf_op jit(solution)/shard_map/combine/pallas_call | solution.py:491
  386.3 35.8 %experts.6 = (bf16[2,1152,1024]{2,1,0:T(8,128)(2,1)}, bf16[2,1152,1024]{2,1,0:T(8,128)(2,1)}, f32[2,1152,1]{2,1,0:T(8,128)}, bf16[4,2,768,512]{3,2,1,0:T(8,128)(2,1)}) custom-call(bf16[4,1152,1024]{2,1,0:T(8,128)(2,1)} %bitcast.106, bf16[4,1152,1024]{2,1,0:T(8,128)(2,1)} %bitcast.108, bf16[4,2,768,512]{3,2,1,0:T(8,128)(2,1)} %bitcast.112, ...), custom_call_target="tpu_custom_call" | custom-call | flops 21743271936 | bytes 31457280 | tf_op jit(solution)/shard_map/experts/pallas_call | solution.py:391
  429.1 36.8 %experts.7 = (bf16[2,1152,1024]{2,1,0:T(8,128)(2,1)}, bf16[2,1152,1024]{2,1,0:T(8,128)(2,1)}, f32[2,1152,1]{2,1,0:T(8,128)}, bf16[4,2,768,512]{3,2,1,0:T(8,128)(2,1)}) custom-call(bf16[4,1152,1024]{2,1,0:T(8,128)(2,1)} %bitcast.107, bf16[4,1152,1024]{2,1,0:T(8,128)(2,1)} %bitcast.109, bf16[4,2,768,512]{3,2,1,0:T(8,128)(2,1)} %bitcast.114, ...), custom_call_target="tpu_custom_call" | custom-call | flops 21743271936 | bytes 31457280 | tf_op jit(solution)/shard_map/experts/pallas_call | solution.py:391
  466.0 12.3 %combine.6 = bf16[4,1056,1024]{2,1,0:T(8,128)(2,1)} custom-call(bf16[8,32]{1,0:T(8,128)(2,1)} %fusion.1.sel_ref, bf16[4,544,1024]{2,1,0:T(8,128)(2,1)} %collective-permute-done.15.pay_ref, bf16[2,8,144,1024]{3,2,1,0:T(8,128)(2,1)} %bitcast.90, bf16[2,8,144,1024]{3,2,1,0:T(8,128)(2,1)} %bitcast.98, bf16[2,8,144,1024]{3,2,1,0:T(8,128)(2,1)} %bitcast.92, ...), custom_call_target="tpu_custom_call" | custom-call | flops 4831838208 | bytes 20971520 | tf_op jit(solution)/shard_map/combine/pallas_call | solution.py:491
  481.4 10.9 %collective-permute-done.24.refs_6_ = bf16[4,1056,1024]{2,1,0:T(8,128)(2,1)} collective-permute-done((bf16[4,1056,1024]{2,1,0:T(8,128)(2,1)}, bf16[4,1056,1024]{2,1,0:T(8,128)(2,1)}, u32[]{:S(2)}, u32[]{:S(2)}) %collective-permute-start.24) | collective-permute-done | bytes 8650784 | tf_op jit(solution)/shard_map/ppermute | solution.py:869
  492.2 15.8 %combine.7 = (bf16[528,1024]{1,0:T(8,128)(2,1)}, bf16[528,1024]{1,0:T(8,128)(2,1)}, bf16[528,1024]{1,0:T(8,128)(2,1)}, bf16[528,1024]{1,0:T(8,128)(2,1)}, bf16[5...) custom-call(bf16[8,32]{1,0:T(8,128)(2,1)} %fusion.1.sel_ref, ...), custom_call_target="tpu_custom_call" | custom-call | flops 4831838208 | bytes 20971520 | tf_op jit(solution)/shard_map/combine/pallas_call | solution.py:491
  512.1 37.4 %attention_backward.2 = (bf16[512,1024]{1,0:T(8,128)(2,1)}, f32[512,1024]{1,0:T(8,128)}, bf16[1024,3200]{1,0:T(8,128)(2,1)}) custom-call(bf16[512,1024]{1,0:T(8,128)(2,1)} %get-tuple-element.109.x_ref.refs_0_, bf16[1024,3200]{1,0:T(8,128)(2,1)} %gather_layer.1.w_ref.refs_1_, f32[1,1024]{1,0:T(1,128)} %bitcast.142, f32[1,1024]{1,0:T(1,128)} %bitcast.138, ...), custom_call_target="tpu_custom_call" | custom-call | flops 17179869184 | bytes 41943040 | tf_op jit(solution)/shard_map/attention_backward/pallas_call | solution.py:636
  561.5 19.0 %collective-permute-done.29.refs_20_ = bf16[528,1024]{1,0:T(8,128)(2,1)S(1)} collective-permute-done((bf16[528,1024]{1,0:T(8,128)(2,1)S(1)}, bf16[528,1024]{1,0:T(8,128)(2,1)S(1)}, u32[]{:S(2)}, u32[]{:S(2)}) %collective-permute-start.29) | collective-permute-done | bytes 1081376 | tf_op jit(solution)/shard_map/ppermute | solution.py:869
  585.3 39.2 %attention_backward.3 = (bf16[512,1024]{1,0:T(8,128)(2,1)}, f32[512,1024]{1,0:T(8,128)}, bf16[1024,3200]{1,0:T(8,128)(2,1)}) custom-call(bf16[512,1024]{1,0:T(8,128)(2,1)} %get-tuple-element.118.x_ref.refs_0_, bf16[1024,3200]{1,0:T(8,128)(2,1)} %gather_layer.1.w_ref.refs_1_, f32[1,1024]{1,0:T(1,128)} %bitcast.143, f32[1,1024]{1,0:T(1,128)} %bitcast.139, ...), custom_call_target="tpu_custom_call" | custom-call | flops 17179869184 | bytes 41943040 | tf_op jit(solution)/shard_map/attention_backward/pallas_call | solution.py:636
  624.5 51.6 %reduce_layer.1 = f32[32,3200]{1,0:T(8,128)} custom-call(bf16[1024,3200]{1,0:T(8,128)(2,1)} %get-tuple-element.201.pack_ref), custom_call_target="tpu_custom_call" | custom-call | bytes 1073741824 | tf_op jit(solution)/shard_map/reduce_layer/pallas_call | solution.py:846
  (165 shorter events, 121.9 us)
Async XLA Ops:
  7.2 215.9 %all-gather.5.cloned.1.call-start = ((), (), s32[]{:S(2)}) async-start(), calls=%async_computation.4 | async-start | bytes 7864320 | tf_op jit(solution)/shard_map/all_gather | solution.py:947
  11.3 295.2 %all-gather.7.cloned.1.call-start = ((), (), s32[]{:S(2)}) async-start(), calls=%async_computation.5 | async-start | bytes 7864320 | tf_op jit(solution)/shard_map/all_gather | solution.py:947
  13.7 70.9 %collective-permute-start = (bf16[512,1024]{1,0:T(8,128)(2,1)S(1)}, bf16[512,1024]{1,0:T(8,128)(2,1)}, u32[]{:S(2)}, u32[]{:S(2)}) collective-permute-start(bf16[512,1024]{1,0:T(8,128)(2,1)S(1)} %get-tuple-element.253.refs_8_), channel_id=1, source_target_pairs={{0,8},{4,12},{8,0},{12,4},{16,24},{20,28},{24,16},{28,20},{1,9},{5... | collective-permute-start | bytes 3145736 | tf_op jit(solution)/shard_map/ppermute | solution.py:869
  16.7 67.9 %collective-permute-start.1 = (bf16[512,1024]{1,0:T(8,128)(2,1)S(1)}, bf16[512,1024]{1,0:T(8,128)(2,1)}, u32[]{:S(2)}, u32[]{:S(2)}) collective-permute-start(bf16[512,1024]{1,0:T(8,128)(2,1)S(1)} %get-tuple-element.253.refs_8_), channel_id=1, source_target_pairs={{0,16},{4,20},{8,24},{12,28},{16,0},{20,4},{24,8},{28,12},{1,17},{... | collective-permute-start | bytes 3145736 | tf_op jit(solution)/shard_map/ppermute | solution.py:869
  107.6 55.1 %collective-permute-start.5 = (bf16[544,1024]{1,0:T(8,128)(2,1)}, bf16[544,1024]{1,0:T(8,128)(2,1)}, u32[]{:S(2)}, u32[]{:S(2)}) collective-permute-start(bf16[544,1024]{1,0:T(8,128)(2,1)} %get-tuple-element.116.refs_15_), channel_id=1, source_target_pairs={{0,16},{4,20},{8,24},{12,28},{16,0},{20,4},{24,8},{28,12},{1,17},{... | collective-permute-start | bytes 3342344 | tf_op jit(solution)/shard_map/ppermute | solution.py:869
  110.5 55.5 %collective-permute-start.10 = (bf16[256,1024]{1,0:T(8,128)(2,1)}, bf16[256,1024]{1,0:T(8,128)(2,1)}, u32[]{:S(2)}, u32[]{:S(2)}) collective-permute-start(bf16[256,1024]{1,0:T(8,128)(2,1)} %slice.119), channel_id=1, source_target_pairs={{0,8},{4,12},{8,0},{12,4},{16,24},{20,28},{24,16},{28,20},{1,9},{5... | collective-permute-start | bytes 1572872 | tf_op jit(solution)/shard_map/ppermute | solution.py:869
  134.3 44.9 %collective-permute-start.3 = (bf16[512,1024]{1,0:T(8,128)(2,1)}, bf16[512,1024]{1,0:T(8,128)(2,1)}, u32[]{:S(2)}, u32[]{:S(2)}) collective-permute-start(bf16[512,1024]{1,0:T(8,128)(2,1)} %get-tuple-element.121.refs_8_), channel_id=1, source_target_pairs={{0,8},{4,12},{8,0},{12,4},{16,24},{20,28},{24,16},{28,20},{1,9},{5... | collective-permute-start | bytes 3145736 | tf_op jit(solution)/shard_map/ppermute | solution.py:869
  135.4 43.9 %collective-permute-start.4 = (bf16[512,1024]{1,0:T(8,128)(2,1)}, bf16[512,1024]{1,0:T(8,128)(2,1)}, u32[]{:S(2)}, u32[]{:S(2)}) collective-permute-start(bf16[512,1024]{1,0:T(8,128)(2,1)} %get-tuple-element.121.refs_8_), channel_id=1, source_target_pairs={{0,16},{4,20},{8,24},{12,28},{16,0},{20,4},{24,8},{28,12},{1,17},{... | collective-permute-start | bytes 3145736 | tf_op jit(solution)/shard_map/ppermute | solution.py:869
  138.3 34.7 %collective-permute-start.9 = (bf16[256,1024]{1,0:T(8,128)(2,1)}, bf16[256,1024]{1,0:T(8,128)(2,1)}, u32[]{:S(2)}, u32[]{:S(2)}) collective-permute-start(bf16[256,1024]{1,0:T(8,128)(2,1)} %slice.118), channel_id=1, source_target_pairs={{0,16},{4,20},{8,24},{12,28},{16,0},{20,4},{24,8},{28,12},{1,17},{... | collective-permute-start | bytes 1572872 | tf_op jit(solution)/shard_map/ppermute | solution.py:869
  190.2 495.7 %reduce-scatter.3.cloned.1.call-start = ((), (), s32[]{:S(2)}) async-start(), calls=%async_computation.2 | async-start | bytes 7864320 | tf_op jit(solution)/shard_map/reduce_scatter | solution.py:1053
  190.8 67.1 %collective-permute-start.14 = (bf16[544,1024]{1,0:T(8,128)(2,1)}, bf16[544,1024]{1,0:T(8,128)(2,1)}, u32[]{:S(2)}, u32[]{:S(2)}) collective-permute-start(bf16[544,1024]{1,0:T(8,128)(2,1)} %get-tuple-element.134.refs_15_), channel_id=1, source_target_pairs={{0,24},{4,28},{8,16},{12,20},{16,8},{20,12},{24,0},{28,4},{1,25},{... | collective-permute-start | bytes 3342344 | tf_op jit(solution)/shard_map/ppermute | solution.py:869
  192.8 65.0 %collective-permute-start.13 = (bf16[544,1024]{1,0:T(8,128)(2,1)}, bf16[544,1024]{1,0:T(8,128)(2,1)}, u32[]{:S(2)}, u32[]{:S(2)}) collective-permute-start(bf16[544,1024]{1,0:T(8,128)(2,1)} %get-tuple-element.134.refs_15_), channel_id=1, source_target_pairs={{0,16},{4,20},{8,24},{12,28},{16,0},{20,4},{24,8},{28,12},{1,17},{... | collective-permute-start | bytes 3342344 | tf_op jit(solution)/shard_map/ppermute | solution.py:869
  193.2 64.6 %collective-permute-start.12 = (bf16[544,1024]{1,0:T(8,128)(2,1)}, bf16[544,1024]{1,0:T(8,128)(2,1)}, u32[]{:S(2)}, u32[]{:S(2)}) collective-permute-start(bf16[544,1024]{1,0:T(8,128)(2,1)} %get-tuple-element.134.refs_15_), channel_id=1, source_target_pairs={{0,8},{4,12},{8,0},{12,4},{16,24},{20,28},{24,16},{28,20},{1,9},{5... | collective-permute-start | bytes 3342344 | tf_op jit(solution)/shard_map/ppermute | solution.py:869
  209.8 51.9 %collective-permute-start.17 = (bf16[256,1024]{1,0:T(8,128)(2,1)}, bf16[256,1024]{1,0:T(8,128)(2,1)}, u32[]{:S(2)}, u32[]{:S(2)}) collective-permute-start(bf16[256,1024]{1,0:T(8,128)(2,1)} %slice.122), channel_id=1, source_target_pairs={{0,8},{4,12},{8,0},{12,4},{16,24},{20,28},{24,16},{28,20},{1,9},{5... | collective-permute-start | bytes 1572872 | tf_op jit(solution)/shard_map/ppermute | solution.py:869
  210.7 51.1 %collective-permute-start.16 = (bf16[256,1024]{1,0:T(8,128)(2,1)}, bf16[256,1024]{1,0:T(8,128)(2,1)}, u32[]{:S(2)}, u32[]{:S(2)}) collective-permute-start(bf16[256,1024]{1,0:T(8,128)(2,1)} %slice.121), channel_id=1, source_target_pairs={{0,16},{4,20},{8,24},{12,28},{16,0},{20,4},{24,8},{28,12},{1,17},{... | collective-permute-start | bytes 1572872 | tf_op jit(solution)/shard_map/ppermute | solution.py:869
  383.3 38.8 %collective-permute-start.20 = (bf16[528,1024]{1,0:T(8,128)(2,1)}, bf16[528,1024]{1,0:T(8,128)(2,1)}, u32[]{:S(2)}, u32[]{:S(2)}) collective-permute-start(bf16[528,1024]{1,0:T(8,128)(2,1)} %get-tuple-element.152), channel_id=1, source_target_pairs={{0,16},{4,20},{8,24},{12,28},{16,0},{20,4},{24,8},{28,12},{1,17},{... | collective-permute-start | bytes 3244040 | tf_op jit(solution)/shard_map/ppermute | solution.py:869
  384.9 37.3 %collective-permute-start.21 = (bf16[528,1024]{1,0:T(8,128)(2,1)}, bf16[528,1024]{1,0:T(8,128)(2,1)}, u32[]{:S(2)}, u32[]{:S(2)}) collective-permute-start(bf16[528,1024]{1,0:T(8,128)(2,1)} %get-tuple-element.161), channel_id=1, source_target_pairs={{0,8},{4,12},{8,0},{12,4},{16,24},{20,28},{24,16},{28,20},{1,9},{5... | collective-permute-start | bytes 3244040 | tf_op jit(solution)/shard_map/ppermute | solution.py:869
  427.9 257.9 %reduce-scatter.5.cloned.1.call-start = ((), (), s32[]{:S(2)}) async-start(), calls=%async_computation.3 | async-start | bytes 7864320 | tf_op jit(solution)/shard_map/reduce_scatter | solution.py:1053
  428.0 38.0 %collective-permute-start.22 = (bf16[528,1024]{1,0:T(8,128)(2,1)}, bf16[528,1024]{1,0:T(8,128)(2,1)}, u32[]{:S(2)}, u32[]{:S(2)}) collective-permute-start(bf16[528,1024]{1,0:T(8,128)(2,1)} %add_convert_fusion.3), channel_id=1, source_target_pairs={{0,8},{4,12},{8,0},{12,4},{16,24},{20,28},{24,16},{28,20},{1,9},{5... | collective-permute-start | bytes 3244040 | tf_op jit(solution)/shard_map/ppermute | solution.py:869
  428.6 37.4 %collective-permute-start.23 = (bf16[528,1024]{1,0:T(8,128)(2,1)}, bf16[528,1024]{1,0:T(8,128)(2,1)}, u32[]{:S(2)}, u32[]{:S(2)}) collective-permute-start(bf16[528,1024]{1,0:T(8,128)(2,1)} %add_convert_fusion.2), channel_id=1, source_target_pairs={{0,16},{4,20},{8,24},{12,28},{16,0},{20,4},{24,8},{28,12},{1,17},{... | collective-permute-start | bytes 3244040 | tf_op jit(solution)/shard_map/ppermute | solution.py:869
  508.0 53.5 %collective-permute-start.27 = (bf16[528,1024]{1,0:T(8,128)(2,1)}, bf16[528,1024]{1,0:T(8,128)(2,1)}, u32[]{:S(2)}, u32[]{:S(2)}) collective-permute-start(bf16[528,1024]{1,0:T(8,128)(2,1)} %get-tuple-element.187), channel_id=1, source_target_pairs={{0,8},{4,12},{8,0},{12,4},{16,24},{20,28},{24,16},{28,20},{1,9},{5... | collective-permute-start | bytes 3244040 | tf_op jit(solution)/shard_map/ppermute | solution.py:869
  509.5 40.0 %collective-permute-start.28 = (bf16[528,1024]{1,0:T(8,128)(2,1)}, bf16[528,1024]{1,0:T(8,128)(2,1)}, u32[]{:S(2)}, u32[]{:S(2)}) collective-permute-start(bf16[528,1024]{1,0:T(8,128)(2,1)} %get-tuple-element.189), channel_id=1, source_target_pairs={{0,16},{4,20},{8,24},{12,28},{16,0},{20,4},{24,8},{28,12},{1,17},{... | collective-permute-start | bytes 3244040 | tf_op jit(solution)/shard_map/ppermute | solution.py:869
  511.0 47.3 %collective-permute-start.30 = (bf16[528,1024]{1,0:T(8,128)(2,1)}, bf16[528,1024]{1,0:T(8,128)(2,1)}, u32[]{:S(2)}, u32[]{:S(2)}) collective-permute-start(bf16[528,1024]{1,0:T(8,128)(2,1)} %get-tuple-element.194), channel_id=1, source_target_pairs={{0,8},{4,12},{8,0},{12,4},{16,24},{20,28},{24,16},{28,20},{1,9},{5... | collective-permute-start | bytes 3244040 | tf_op jit(solution)/shard_map/ppermute | solution.py:869
  511.6 49.9 %collective-permute-start.32 = (bf16[528,1024]{1,0:T(8,128)(2,1)}, bf16[528,1024]{1,0:T(8,128)(2,1)}, u32[]{:S(2)}, u32[]{:S(2)}) collective-permute-start(bf16[528,1024]{1,0:T(8,128)(2,1)} %get-tuple-element.197), channel_id=1, source_target_pairs={{0,16},{4,20},{8,24},{12,28},{16,0},{20,4},{24,8},{28,12},{1,17},{... | collective-permute-start | bytes 3244040 | tf_op jit(solution)/shard_map/ppermute | solution.py:869
  (37 other events, 628.6 us)
Sparse Core Ops, SparseCore 0:
  11.3 131.4 all-gather.4
  190.3 116.1 all-gather.6
  428.0 107.1 reduce-scatter.2
  537.4 111.2 reduce-scatter.4

commit v4 on v3

--- a/solution.py
+++ b/solution.py
@@ -60,7 +60,7 @@
     return block * cosine + partner * sine
 
 
-def hint(flops, transcendentals, bytes_accessed, share=16):
+def hint(flops, transcendentals, bytes_accessed, share=256):
     return pl.CostEstimate(
         flops=flops // share, transcendentals=transcendentals // share,
         bytes_accessed=bytes_accessed // share,
@@ -408,7 +408,7 @@
         compiler_params=pltpu.CompilerParams(vmem_limit_bytes=VMEM_LIMIT),
         cost_estimate=hint(
             flops=18 * count * total * width * hidden, transcendentals=count * total * hidden,
-            bytes_accessed=30 << 20, share=16 if prior is None else 1,
+            bytes_accessed=30 << 20, share=256 if prior is None else 1,
         ),
         name="experts",
     )(*operands)
@@ -466,38 +466,38 @@
         out_refs[0][0, rows + half :, :] = second.astype(BF)
 
 
-def combine(sel, pays, produced, returned, dots, side, other):
+def combine(sel, pays, produced, returned, dots, side, first, span, other):
     count, total_rows, width = pays.shape
     groups, each = len(produced), produced[0].shape[0]
     local = groups * each
     experts = sel.shape[1]
     rows = total_rows - experts
-    pick = lambda last: pl.BlockSpec((each, 1, CAP, last), lambda s: (0, side * count + s, 0, 0))
+    pick = lambda last: pl.BlockSpec((each, 1, CAP, last), lambda s: (0, side * count + first + s, 0, 0))
     in_specs = [
         pl.BlockSpec(sel.shape, lambda s: (0, 0)),
-        pl.BlockSpec((1, experts, width), lambda s: (s, rows // experts, 0)),
+        pl.BlockSpec((1, experts, width), lambda s: (first + s, rows // experts, 0)),
     ]
     in_specs += [pick(width)] * (2 * groups) + [pick(1)] * groups
     operands = [sel, pays, *produced, *returned, *dots]
     total = 2 * rows + experts
     out_spec = pl.BlockSpec((1, total, width), lambda s: (s, 0, 0))
-    out_shape = (jax.ShapeDtypeStruct((count, total, width), BF),)
+    out_shape = (jax.ShapeDtypeStruct((span, total, width), BF),)
     out_specs = (out_spec,)
     if other is not None:
         operands.append(other)
         in_specs.append(out_spec)
-        out_shape = (jax.ShapeDtypeStruct((total // 2, width), BF),) * (2 * count)
-        out_specs = (pl.BlockSpec((total // 2, width), lambda s: (0, 0)),) * (2 * count)
+        out_shape = (jax.ShapeDtypeStruct((total // 2, width), BF),) * (2 * span)
+        out_specs = (pl.BlockSpec((total // 2, width), lambda s: (0, 0)),) * (2 * span)
     return pl.pallas_call(
         functools.partial(combine_kernel, groups=groups, local=local, received=other is not None),
         out_shape=out_shape,
-        grid=(count,),
+        grid=(span,),
         in_specs=in_specs,
         out_specs=out_specs,
         scratch_shapes=[pltpu.VMEM((rows, rows), BF)],
         compiler_params=pltpu.CompilerParams(vmem_limit_bytes=VMEM_LIMIT),
         cost_estimate=hint(
-            flops=4 * count * local * CAP * rows * width, transcendentals=0, bytes_accessed=20 << 20, share=1
+            flops=4 * span * local * CAP * rows * width, transcendentals=0, bytes_accessed=20 << 20, share=1
         ),
         name="combine",
     )(*operands)
@@ -513,7 +513,7 @@
     term_refs = refs[17 : 17 + 2 * terms]
     rest = refs[17 + 2 * terms :]
     if carried:
-        prior_ref, rest = rest[0], rest[1:]
+        prior_ref, rest = rest[0], rest[3:]
     out_ref, in_grad_ref, pack_ref, bias_ref, wide_ref, att_grad_ref, qkv_grad_ref, branch_ref, normed_ref = rest
     rows, width = x_ref.shape
     step = 256
@@ -532,7 +532,7 @@
 
     half = experts // 2
     residual = res_ref[...]
-    out_ref[...] = (residual + RESIDUAL_SCALE * gathered(0, 0, rows)).astype(BF)
+    out_ref[0] = (residual + RESIDUAL_SCALE * gathered(0, 0, rows)).astype(BF)
     tail = jnp.concatenate([gathered(0, rows, rows + half), gathered(1, 0, half)], axis=0)
     weighted = tail[:, :rows] + tail[:, rows:]
     chosen = weighted - gate_ref[...] * jnp.sum(weighted, axis=0, keepdims=True)
@@ -545,7 +545,7 @@
     u = moe_grad * gain_two_ref[...]
     inner = jnp.sum(u * residual, axis=1, keepdims=True) * (1.0 / width)
     res_grad = grad_ref[...].astype(F32) + scale * u - residual * (scale * scale * scale * inner)
-    in_grad_ref[...] = res_grad
+    in_grad_ref[0] = res_grad
     branch_ref[...] = (RESIDUAL_SCALE * res_grad).astype(BF)
     bias_ref[...] = jnp.where(id_col_ref[...] <= id_row_ref[...], 0.0, NEG_FILL)
 
@@ -616,7 +616,7 @@
     gain_one_grad = jnp.sum(normed_grad * x * scale, axis=0, keepdims=True)
     u = normed_grad * gain_one_ref[...]
     inner = jnp.sum(u * x, axis=1, keepdims=True) * (1.0 / width)
-    in_grad_ref[...] = in_grad_ref[...] + scale * u - x * (scale * scale * scale * inner)
+    in_grad_ref[0] = in_grad_ref[0] + scale * u - x * (scale * scale * scale * inner)
     lanes = lane_iota((width, LANES))
     one = jnp.broadcast_to(gain_one_grad, (LANES, width)).T
     two = jnp.broadcast_to(gain_two_grad, (LANES, width)).T
@@ -626,12 +626,19 @@
 
 
 def attention_backward(
-    x, pack, gain_one, gain_two, ids, tables, grad, saved, terms, prior, q_width, kv_width, experts
+    index, micro, x, pack, gain_one, gain_two, ids, tables, grad, saved, terms, prior, made, q_width, kv_width,
+    experts,
 ):
     rows, width = x.shape
     operands = [x, pack, gain_one, gain_two, ids[None, :], ids[:, None], *tables, grad, *saved, *terms]
+    whole = pl.BlockSpec(memory_space=pltpu.VMEM)
+    in_specs = [whole] * len(operands)
+    aliases = {}
     if prior is not None:
-        operands.append(prior)
+        operands += [prior, *made]
+        in_specs += [whole] + [pl.BlockSpec(memory_space=pl.ANY)] * 2
+        aliases = {len(operands) - 2: 0, len(operands) - 1: 1}
+    row_spec = pl.BlockSpec((1, rows, width), lambda i: (index, 0, 0))
     flops = 4 * rows * width * (q_width + 2 * kv_width + width) + 20 * QUERY_HEADS * rows * rows * 128
     return pl.pallas_call(
         functools.partial(
@@ -639,10 +646,14 @@
             experts=experts, carried=prior is not None,
         ),
         out_shape=(
-            jax.ShapeDtypeStruct((rows, width), BF),
-            jax.ShapeDtypeStruct((rows, width), F32),
+            jax.ShapeDtypeStruct((micro, rows, width), BF),
+            jax.ShapeDtypeStruct((micro, rows, width), F32),
             jax.ShapeDtypeStruct(pack.shape, BF),
         ),
+        grid=(1,),
+        in_specs=in_specs,
+        out_specs=(row_spec, row_spec, whole),
+        input_output_aliases=aliases,
         scratch_shapes=[
             pltpu.VMEM((rows, rows), F32),
             pltpu.VMEM((rows, width), F32),
@@ -984,7 +995,7 @@
         pay_near = None
         if square and m == 0:
             one, two = send_near(pay, owners)
-            ready = (one,)
+            ready = (saved[-1][4],)
             pay_near = after(one, saved[-1][4]), after(two, saved[-1][4])
         elif m:
             pay = after(pay, *arrived[m - 1][0][1:])
@@ -1003,19 +1014,26 @@
             [done[m, g][i].reshape(group, 2 * chips, CAP, -1) for g in range(len(weights))]
             for i in range(3)
         ]
-        (sent,) = combine(sel, after(pays[m][1], *earlier), *parts, 1, None)
-        return combine(sel, pays[m][0], *parts, 0, swap(sent, 1, owners))
-
-    outputs, input_grads = [], []
-
-    def backward(m, found, prior):
+        kept, before = [], earlier
+        sent = {}
+        span = chips // 2
+        for first in (span, 0):
+            (sent[first],) = combine(sel, after(pays[m][1], *before), *parts, 1, first, span, None)
+            before = (sent[first],)
+        for first in (span, 0):
+            found = combine(
+                sel, after(pays[m][0], *before), *parts, 0, first, span, swap(sent[first], 1, owners)
+            )
+            before = (found[0],)
+            kept = list(found) + kept
+        return kept
+
+    def backward(m, found, made, prior):
         out, in_grad, prior = attention_backward(
-            inputs[m, 0], pack, gain_one, gain_two, block_ids[m, 0], tables, out_grad[m, 0], saved[m],
-            found, prior, q_width, kv_width, experts,
+            m, micro, inputs[m, 0], pack, gain_one, gain_two, block_ids[m, 0], tables, out_grad[m, 0],
+            saved[m], found, prior, made, q_width, kv_width, experts,
         )
-        outputs.append(out)
-        input_grads.append(in_grad)
-        return prior
+        return (out, in_grad), prior
 
     added, far, rest = (), (), ()
     for m in range(micro):
@@ -1031,7 +1049,7 @@
                 expert_part(m - 1, g, moved[m][0])
             kept = returned(m - 1, far)
             near = scatter_near(kept, owners, *rest)
-            expert_part(m, 0, kept[-1])
+            expert_part(m, 0, kept[0], kept[-1])
             added, far = scatter_far(kept, near, owners, done[m, 0][2])
             rest = scatter_rest(kept, owners, *far)
             terms.append(scattered(kept, near, far, rest))
@@ -1040,13 +1058,13 @@
     kept = returned(micro - 1, far)
     near = scatter_near(kept, owners, *rest)
     last_rest = scatter_rest(kept, owners, *rest)
-    prior, held_back = None, ()
+    made, prior, held_back = None, None, ()
     for m in range(micro - 1):
-        prior = backward(m, [after(terms[m][0], kept[-1])] + terms[m][1:], prior)
+        made, prior = backward(m, [after(terms[m][0], kept[0], kept[-1])] + terms[m][1:], made, prior)
         held_back = (prior,)
     last_far = scatter_far(kept, near, owners, *held_back)[1]
     terms.append(scattered(kept, near, last_far, last_rest))
-    prior = backward(micro - 1, terms[-1], prior)
+    made, prior = backward(micro - 1, terms[-1], made, prior)
     sums = []
     for g in range(len(weights)):
         summed = after(done[micro - 1, g][3], *(far if g else added))
@@ -1058,8 +1076,8 @@
     grad_down = stacked[:, 2 * in_rows :].reshape(held, cuts, down_rows, hidden)
     grad_down = grad_down.transpose(0, 2, 1, 3).reshape(held, down_rows, width)
     return (
-        jnp.stack(outputs)[:, None],
-        jnp.stack(input_grads)[:, None],
+        made[0][:, None],
+        made[1][:, None],
         cut[5][:, 0], cut[0], cut[1], cut[2], cut[3], cut[6][:, 0], cut[4],
         stacked[:, :in_rows], stacked[:, in_rows : 2 * in_rows], grad_down,
     )

time: 704 us -> 694 us (0.986)
  waiting for transfers between devices: 107 us -> 91.5 us
  Pallas kernels: 473 us -> 488 us
    ppermute x33 -> x35, waiting for transfers between devices: 88.7 us -> 74.4 us  [swap(): return lax.ppermute(value, 'fsdp', [(i, i ^ distance) for i in range(size)])]
    pallas_call x4 -> x8, Pallas kernels: 56.2 us -> 68 us  [combine(): pl.pallas_call(functools.partial(combine_kernel, groups=groups, local=loc...]
    ppermute x33 -> x35, starting transfers between devices: 34.9 us -> 34.1 us  [swap(): return lax.ppermute(value, 'fsdp', [(i, i ^ distance) for i in range(size)])]
  transfers between devices with their start and end apart: 37 -> 39, of which waited for: 10 -> 11; matrix products, arithmetic and copies ran while one was open for 7% -> 6% of each run, Pallas kernels for 59% -> 65%
where the time goes in v4:
time: 694 us; the launch traced here: 690 us
  Pallas kernels  488 us (70%)
  waiting for transfers between devices  91.5 us (13%)
  starting transfers between devices  34.7 us (5%)
  local copies, waits for them, and re-layouts  30.9 us (4%)
  other arithmetic  30.7 us (4%)
  between operations  14.5 us (2%)
    pallas_call x4, Pallas kernels, experts_step(): pl.pallas_call(functools.partial(expert_kernel, chunk=rows // 3, tile=256...  143 us
    pallas_call x2, Pallas kernels, attention_backward(): pl.pallas_call(functools.partial(attention_backward_kernel, terms=len(ter...  76.4 us
    ppermute x35, waiting for transfers between devices, swap(): return lax.ppermute(value, 'fsdp', [(i, i ^ distance) for i in range(size)])  74.4 us
    pallas_call x8, Pallas kernels, combine(): pl.pallas_call(functools.partial(combine_kernel, groups=groups, local=loc...  68 us
    pallas_call x1, Pallas kernels, gather_layer(): pl.pallas_call(functools.partial(gather_layer_kernel, chips=chips, depth=...  59.6 us
    pallas_call x1, Pallas kernels, reduce_layer(): pl.pallas_call(functools.partial(reduce_layer_kernel, chips=chips, depth=...  53.9 us
    pallas_call x2, Pallas kernels, attention_forward(): pl.pallas_call(functools.partial(attention_forward_kernel, q_width=q_widt...  43.7 us
    pallas_call x4, Pallas kernels, dispatch(): pl.pallas_call(functools.partial(dispatch_kernel, local=local), out_shape...  43.3 us
  transfers between devices with their start and end apart: 39, of which 11 were waited for; matrix products, arithmetic and copies ran while one was open for 6% of the time, Pallas kernels for 65%

profile of v4, /device:TPU:0, one launch (start us, length us, event | category | flops | bytes accessed | tf_op | source)
XLA Modules:
  0.0 689.7 jit_solution(9604273823362795819)
XLA Ops:
  19.2 59.6 %gather_layer.1.w_ref.refs_1_ = bf16[1024,3200]{1,0:T(8,128)(2,1)} custom-call(bf16[32,3200]{1,0:T(8,128)(2,1)} %concatenate.18.w_ref), custom_call_target="tpu_custom_call" | custom-call | tf_op jit(solution)/shard_map/gather_layer/pallas_call | solution.py:754
  84.6 22.0 %attention_forward.2 = (bf16[512,1024]{1,0:T(8,128)(2,1)}, bf16[512,512]{1,0:T(8,128)(2,1)}, bf16[512,512]{1,0:T(8,128)(2,1)}, bf16[512,1024]{1,0:T(8,128)(2,1)}...) custom-call(bf16[512,1024]{1,0:T(8,128)(2,1)} %get-tuple-element.115.x_ref.refs_0_, ...), custom_call_target="tpu_custom_call" | custom-call | flops 29360128 | bytes 65536 | tf_op jit(solution)/shard_map/attention_forward/pallas_call | solution.py:179
  113.7 21.7 %attention_forward.3 = (bf16[512,1024]{1,0:T(8,128)(2,1)}, bf16[512,512]{1,0:T(8,128)(2,1)}, bf16[512,512]{1,0:T(8,128)(2,1)}, bf16[512,1024]{1,0:T(8,128)(2,1)}...) custom-call(bf16[512,1024]{1,0:T(8,128)(2,1)} %get-tuple-element.117.x_ref.refs_0_, ...), custom_call_target="tpu_custom_call" | custom-call | flops 29360128 | bytes 65536 | tf_op jit(solution)/shard_map/attention_forward/pallas_call | solution.py:179
  147.1 26.4 %collective-permute-done.10 = bf16[256,1024]{1,0:T(8,128)(2,1)S(1)} collective-permute-done((bf16[256,1024]{1,0:T(8,128)(2,1)S(1)}, bf16[256,1024]{1,0:T(8,128)(2,1)S(1)}, u32[]{:S(2)}, u32[]{:S(2)}) %collective-permute-start.10) | collective-permute-done | bytes 524320 | tf_op jit(solution)/shard_map/ppermute | solution.py:880
  204.0 10.8 %dispatch.4 = (bf16[4,2,4,144,1024]{4,3,2,1,0:T(8,128)(2,1)}, bf16[4,2,4,144,1024]{4,3,2,1,0:T(8,128)(2,1)}) custom-call(bf16[8,32]{1,0:T(8,128)(2,1)} %fusion.1.sel_ref, bf16[4,544,1024]{2,1,0:T(8,128)(2,1)} %pad_maximum_fusion.pay_ref, bf16[4,512,1024]{2,1,0:T(8,128)(2,1)} %pad_maximum_fusion.2.grad_ref), custom_call_target="tpu_custom_call" | custom-call | flops 18874368 | bytes 81920 | tf_op jit(solution)/shard_map/dispatch/pallas_call | solution.py:250
  214.8 10.9 %dispatch.5 = (bf16[4,2,4,144,1024]{4,3,2,1,0:T(8,128)(2,1)}, bf16[4,2,4,144,1024]{4,3,2,1,0:T(8,128)(2,1)}) custom-call(bf16[8,32]{1,0:T(8,128)(2,1)} %fusion.1.sel_ref, bf16[4,544,1024]{2,1,0:T(8,128)(2,1)} %collective-permute-done.9.pay_ref, bf16[4,512,1024]{2,1,0:T(8,128)(2,1)} %collective-permute-done.12.grad_ref, ...), custom_call_target="tpu_custom_call", output_to_operand_aliasing={{0}: (3, {}), {1}: (4, {})} | custom-call | flops 18874368 | bytes 81920 | tf_op jit(solution)/shard_map/dispatch/pallas_call | solution.py:250
  225.7 34.8 %experts.4 = (bf16[2,1152,1024]{2,1,0:T(8,128)(2,1)}, bf16[2,1152,1024]{2,1,0:T(8,128)(2,1)}, f32[2,1152,1]{2,1,0:T(8,128)}, bf16[4,2,768,512]{3,2,1,0:T(8,128)(2,1)}) custom-call(bf16[4,1152,1024]{2,1,0:T(8,128)(2,1)} %bitcast.80, bf16[4,1152,1024]{2,1,0:T(8,128)(2,1)} %bitcast.82, bf16[4,2,768,512]{3,2,1,0:T(8,128)(2,1)} %bitcast.137), custom_call_target="tpu_custom_call" | custom-call | flops 84934656 | bytes 122880 | tf_op jit(solution)/shard_map/experts/pallas_call | solution.py:391
  268.7 10.9 %dispatch.6 = (bf16[4,2,4,144,1024]{4,3,2,1,0:T(8,128)(2,1)}, bf16[4,2,4,144,1024]{4,3,2,1,0:T(8,128)(2,1)}) custom-call(bf16[8,32]{1,0:T(8,128)(2,1)} %fusion.1.sel_ref, bf16[4,544,1024]{2,1,0:T(8,128)(2,1)} %pad_maximum_fusion.1.pay_ref, bf16[4,512,1024]{2,1,0:T(8,128)(2,1)} %pad_maximum_fusion.3.grad_ref), custom_call_target="tpu_custom_call" | custom-call | flops 18874368 | bytes 81920 | tf_op jit(solution)/shard_map/dispatch/pallas_call | solution.py:250
  279.6 10.8 %dispatch.7 = (bf16[4,2,4,144,1024]{4,3,2,1,0:T(8,128)(2,1)}, bf16[4,2,4,144,1024]{4,3,2,1,0:T(8,128)(2,1)}) custom-call(bf16[8,32]{1,0:T(8,128)(2,1)} %fusion.1.sel_ref, bf16[4,544,1024]{2,1,0:T(8,128)(2,1)} %collective-permute-done.15.pay_ref, ...), custom_call_target="tpu_custom_call", output_to_operand_aliasing={{0}: (3, {}), {1}: (4, {})} | custom-call | flops 18874368 | bytes 81920 | tf_op jit(solution)/shard_map/dispatch/pallas_call | solution.py:250
  290.4 16.9 %all-gather.7.cloned.1.call-done = bf16[8,768,512]{2,1,0:T(8,128)(2,1)} async-done(((bf16[2,768,512]{2,1,0:T(8,128)(2,1)}), bf16[8,768,512]{2,1,0:T(8,128)(2,1)}) %all-gather.7.cloned.1.call-update) | async-done | bytes 6291472 | tf_op jit(solution)/shard_map/all_gather | solution.py:958
  307.3 35.0 %experts.5 = (bf16[2,1152,1024]{2,1,0:T(8,128)(2,1)}, bf16[2,1152,1024]{2,1,0:T(8,128)(2,1)}, f32[2,1152,1]{2,1,0:T(8,128)}, bf16[4,2,768,512]{3,2,1,0:T(8,128)(2,1)}) custom-call(bf16[4,1152,1024]{2,1,0:T(8,128)(2,1)} %bitcast.81, bf16[4,1152,1024]{2,1,0:T(8,128)(2,1)} %bitcast.83, bf16[4,2,768,512]{3,2,1,0:T(8,128)(2,1)} %bitcast.139), custom_call_target="tpu_custom_call" | custom-call | flops 84934656 | bytes 122880 | tf_op jit(solution)/shard_map/experts/pallas_call | solution.py:391
  349.8 7.5 %combine.9 = bf16[2,1056,1024]{2,1,0:T(8,128)(2,1)} custom-call(bf16[8,32]{1,0:T(8,128)(2,1)} %fusion.1.sel_ref, bf16[4,544,1024]{2,1,0:T(8,128)(2,1)} %collective-permute-done.9.pay_ref, bf16[2,8,144,1024]{3,2,1,0:T(8,128)(2,1)} %bitcast.93, bf16[2,8,144,1024]{3,2,1,0:T(8,128)(2,1)} %bitcast.109, bf16[2,8,144,1024]{3,2,1,0:T(8,128)(2,1)} %bitcast.97, ...), custom_call_target="tpu_custom_call" | custom-call | flops 2415919104 | bytes 20971520 | tf_op jit(solution)/shard_map/combine/pallas_call | solution.py:491
  357.8 9.4 %combine.10 = (bf16[528,1024]{1,0:T(8,128)(2,1)}, bf16[528,1024]{1,0:T(8,128)(2,1)}, bf16[528,1024]{1,0:T(8,128)(2,1)}, bf16[528,1024]{1,0:T(8,128)(2,1)}) custom-call(bf16[8,32]{1,0:T(8,128)(2,1)} %fusion.1.sel_ref, bf16[4,544,1024]{2,1,0:T(8,128)(2,1)} %pad_maximum_fusion.pay_ref, bf16[2,8,144,1024]{3,2,1,0:T(8,128)(2,1)} %bitcast.94, ...), custom_call_target="tpu_custom_call" | custom-call | flops 2415919104 | bytes 20971520 | tf_op jit(solution)/shard_map/combine/pallas_call | solution.py:491
  368.7 9.4 %combine.11 = (bf16[528,1024]{1,0:T(8,128)(2,1)}, bf16[528,1024]{1,0:T(8,128)(2,1)}, bf16[528,1024]{1,0:T(8,128)(2,1)}, bf16[528,1024]{1,0:T(8,128)(2,1)}) custom-call(bf16[8,32]{1,0:T(8,128)(2,1)} %fusion.1.sel_ref, bf16[4,544,1024]{2,1,0:T(8,128)(2,1)} %pad_maximum_fusion.pay_ref, bf16[2,8,144,1024]{3,2,1,0:T(8,128)(2,1)} %bitcast.95, ...), custom_call_target="tpu_custom_call" | custom-call | flops 2415919104 | bytes 20971520 | tf_op jit(solution)/shard_map/combine/pallas_call | solution.py:491
  379.6 35.7 %experts.6 = (bf16[2,1152,1024]{2,1,0:T(8,128)(2,1)}, bf16[2,1152,1024]{2,1,0:T(8,128)(2,1)}, f32[2,1152,1]{2,1,0:T(8,128)}, bf16[4,2,768,512]{3,2,1,0:T(8,128)(2,1)}) custom-call(bf16[4,1152,1024]{2,1,0:T(8,128)(2,1)} %bitcast.132, bf16[4,1152,1024]{2,1,0:T(8,128)(2,1)} %bitcast.134, bf16[4,2,768,512]{3,2,1,0:T(8,128)(2,1)} %bitcast.138, ...), custom_call_target="tpu_custom_call" | custom-call | flops 21743271936 | bytes 31457280 | tf_op jit(solution)/shard_map/experts/pallas_call | solution.py:391
  422.2 37.2 %experts.7 = (bf16[2,1152,1024]{2,1,0:T(8,128)(2,1)}, bf16[2,1152,1024]{2,1,0:T(8,128)(2,1)}, f32[2,1152,1]{2,1,0:T(8,128)}, bf16[4,2,768,512]{3,2,1,0:T(8,128)(2,1)}) custom-call(bf16[4,1152,1024]{2,1,0:T(8,128)(2,1)} %bitcast.133, bf16[4,1152,1024]{2,1,0:T(8,128)(2,1)} %bitcast.135, bf16[4,2,768,512]{3,2,1,0:T(8,128)(2,1)} %bitcast.140, ...), custom_call_target="tpu_custom_call" | custom-call | flops 21743271936 | bytes 31457280 | tf_op jit(solution)/shard_map/experts/pallas_call | solution.py:391
  459.4 7.5 %combine.12 = bf16[2,1056,1024]{2,1,0:T(8,128)(2,1)} custom-call(bf16[8,32]{1,0:T(8,128)(2,1)} %fusion.1.sel_ref, bf16[4,544,1024]{2,1,0:T(8,128)(2,1)} %collective-permute-done.15.pay_ref, bf16[2,8,144,1024]{3,2,1,0:T(8,128)(2,1)} %bitcast.84, bf16[2,8,144,1024]{3,2,1,0:T(8,128)(2,1)} %bitcast.100, bf16[2,8,144,1024]{3,2,1,0:T(8,128)(2,1)} %bitcast.88, ...), custom_call_target="tpu_custom_call" | custom-call | flops 2415919104 | bytes 20971520 | tf_op jit(solution)/shard_map/combine/pallas_call | solution.py:491
  467.0 7.5 %combine.13 = bf16[2,1056,1024]{2,1,0:T(8,128)(2,1)} custom-call(bf16[8,32]{1,0:T(8,128)(2,1)} %fusion.1.sel_ref, bf16[4,544,1024]{2,1,0:T(8,128)(2,1)} %collective-permute-done.15.pay_ref, bf16[2,8,144,1024]{3,2,1,0:T(8,128)(2,1)} %bitcast.85, bf16[2,8,144,1024]{3,2,1,0:T(8,128)(2,1)} %bitcast.101, bf16[2,8,144,1024]{3,2,1,0:T(8,128)(2,1)} %bitcast.89, ...), custom_call_target="tpu_custom_call" | custom-call | flops 2415919104 | bytes 20971520 | tf_op jit(solution)/shard_map/combine/pallas_call | solution.py:491
  478.0 9.4 %combine.14 = (bf16[528,1024]{1,0:T(8,128)(2,1)}, bf16[528,1024]{1,0:T(8,128)(2,1)}, bf16[528,1024]{1,0:T(8,128)(2,1)}, bf16[528,1024]{1,0:T(8,128)(2,1)}) custom-call(bf16[8,32]{1,0:T(8,128)(2,1)} %fusion.1.sel_ref, bf16[4,544,1024]{2,1,0:T(8,128)(2,1)} %pad_maximum_fusion.1.pay_ref, bf16[2,8,144,1024]{3,2,1,0:T(8,128)(2,1)} %bitcast.86, ...), custom_call_target="tpu_custom_call" | custom-call | flops 2415919104 | bytes 20971520 | tf_op jit(solution)/shard_map/combine/pallas_call | solution.py:491
  487.4 9.7 %combine.15 = (bf16[528,1024]{1,0:T(8,128)(2,1)}, bf16[528,1024]{1,0:T(8,128)(2,1)}, bf16[528,1024]{1,0:T(8,128)(2,1)}, bf16[528,1024]{1,0:T(8,128)(2,1)}) custom-call(bf16[8,32]{1,0:T(8,128)(2,1)} %fusion.1.sel_ref, bf16[4,544,1024]{2,1,0:T(8,128)(2,1)} %pad_maximum_fusion.1.pay_ref, bf16[2,8,144,1024]{3,2,1,0:T(8,128)(2,1)} %bitcast.87, ...), custom_call_target="tpu_custom_call" | custom-call | flops 2415919104 | bytes 20971520 | tf_op jit(solution)/shard_map/combine/pallas_call | solution.py:491
  506.5 37.1 %attention_backward.2 = (bf16[2,512,1024]{2,1,0:T(8,128)(2,1)}, f32[2,512,1024]{2,1,0:T(8,128)}, bf16[1024,3200]{1,0:T(8,128)(2,1)}) custom-call(bf16[512,1024]{1,0:T(8,128)(2,1)} %get-tuple-element.115.x_ref.refs_0_, bf16[1024,3200]{1,0:T(8,128)(2,1)} %gather_layer.1.w_ref.refs_1_, f32[1,1024]{1,0:T(1,128)} %bitcast.158, f32[1,1024]{1,0:T(1,128)} %bitcast.154, ...), custom_call_target="tpu_custom_call" | custom-call | flops 17179869184 | bytes 41943040 | tf_op jit(solution)/shard_map/attention_backward/pallas_call | solution.py:643
  555.8 17.8 %collective-permute-done.31.refs_20_ = bf16[528,1024]{1,0:T(8,128)(2,1)S(1)} collective-permute-done((bf16[528,1024]{1,0:T(8,128)(2,1)S(1)}, bf16[528,1024]{1,0:T(8,128)(2,1)S(1)}, u32[]{:S(2)}, u32[]{:S(2)}) %collective-permute-start.31) | collective-permute-done | bytes 1081376 | tf_op jit(solution)/shard_map/ppermute | solution.py:880
  577.2 39.3 %attention_backward.3 = (bf16[2,512,1024]{2,1,0:T(8,128)(2,1)}, f32[2,512,1024]{2,1,0:T(8,128)}, bf16[1024,3200]{1,0:T(8,128)(2,1)}) custom-call(bf16[512,1024]{1,0:T(8,128)(2,1)} %get-tuple-element.117.x_ref.refs_0_, bf16[1024,3200]{1,0:T(8,128)(2,1)} %gather_layer.1.w_ref.refs_1_, ...), custom_call_target="tpu_custom_call", output_to_operand_aliasing={{0}: (24, {}), {1}: (25, {})} | custom-call | flops 17179869184 | bytes 41943040 | tf_op jit(solution)/shard_map/attention_backward/pallas_call | solution.py:643
  616.5 53.9 %reduce_layer.1 = f32[32,3200]{1,0:T(8,128)} custom-call(bf16[1024,3200]{1,0:T(8,128)(2,1)} %get-tuple-element.213.pack_ref), custom_call_target="tpu_custom_call" | custom-call | bytes 1073741824 | tf_op jit(solution)/shard_map/reduce_layer/pallas_call | solution.py:857
  (173 shorter events, 134.1 us)
Async XLA Ops:
  7.2 218.5 %all-gather.5.cloned.1.call-start = ((), (), s32[]{:S(2)}) async-start(), calls=%async_computation.4 | async-start | bytes 7864320 | tf_op jit(solution)/shard_map/all_gather | solution.py:958
  11.3 296.0 %all-gather.7.cloned.1.call-start = ((), (), s32[]{:S(2)}) async-start(), calls=%async_computation.5 | async-start | bytes 7864320 | tf_op jit(solution)/shard_map/all_gather | solution.py:958
  13.7 70.9 %collective-permute-start = (bf16[512,1024]{1,0:T(8,128)(2,1)S(1)}, bf16[512,1024]{1,0:T(8,128)(2,1)}, u32[]{:S(2)}, u32[]{:S(2)}) collective-permute-start(bf16[512,1024]{1,0:T(8,128)(2,1)S(1)} %get-tuple-element.264.refs_8_), channel_id=1, source_target_pairs={{0,8},{4,12},{8,0},{12,4},{16,24},{20,28},{24,16},{28,20},{1,9},{5... | collective-permute-start | bytes 3145736 | tf_op jit(solution)/shard_map/ppermute | solution.py:880
  16.6 67.9 %collective-permute-start.1 = (bf16[512,1024]{1,0:T(8,128)(2,1)S(1)}, bf16[512,1024]{1,0:T(8,128)(2,1)}, u32[]{:S(2)}, u32[]{:S(2)}) collective-permute-start(bf16[512,1024]{1,0:T(8,128)(2,1)S(1)} %get-tuple-element.264.refs_8_), channel_id=1, source_target_pairs={{0,16},{4,20},{8,24},{12,28},{16,0},{20,4},{24,8},{28,12},{1,17},{... | collective-permute-start | bytes 3145736 | tf_op jit(solution)/shard_map/ppermute | solution.py:880
  135.5 39.1 %collective-permute-start.7 = (bf16[512,1024]{1,0:T(8,128)(2,1)}, bf16[512,1024]{1,0:T(8,128)(2,1)S(1)}, u32[]{:S(2)}, u32[]{:S(2)}) collective-permute-start(bf16[512,1024]{1,0:T(8,128)(2,1)} %get-tuple-element.130.refs_8_), channel_id=1, source_target_pairs={{0,8},{4,12},{8,0},{12,4},{16,24},{20,28},{24,16},{28,20},{1,9},{5... | collective-permute-start | bytes 3145736 | tf_op jit(solution)/shard_map/ppermute | solution.py:880
  136.0 38.6 %collective-permute-start.8 = (bf16[512,1024]{1,0:T(8,128)(2,1)}, bf16[512,1024]{1,0:T(8,128)(2,1)S(1)}, u32[]{:S(2)}, u32[]{:S(2)}) collective-permute-start(bf16[512,1024]{1,0:T(8,128)(2,1)} %get-tuple-element.130.refs_8_), channel_id=1, source_target_pairs={{0,16},{4,20},{8,24},{12,28},{16,0},{20,4},{24,8},{28,12},{1,17},{... | collective-permute-start | bytes 3145736 | tf_op jit(solution)/shard_map/ppermute | solution.py:880
  138.1 35.3 %collective-permute-start.10 = (bf16[256,1024]{1,0:T(8,128)(2,1)S(1)}, bf16[256,1024]{1,0:T(8,128)(2,1)S(1)}, u32[]{:S(2)}, u32[]{:S(2)}) collective-permute-start(bf16[256,1024]{1,0:T(8,128)(2,1)S(1)} %slice.118), channel_id=1, source_target_pairs={{0,16},{4,20},{8,24},{12,28},{16,0},{20,4},{24,8},{28,12},{1,17},{... | collective-permute-start | bytes 1572872 | tf_op jit(solution)/shard_map/ppermute | solution.py:880
  140.3 39.0 %collective-permute-start.5 = (bf16[272,1024]{1,0:T(8,128)(2,1)S(1)}, bf16[272,1024]{1,0:T(8,128)(2,1)S(1)}, u32[]{:S(2)}, u32[]{:S(2)}) collective-permute-start(bf16[272,1024]{1,0:T(8,128)(2,1)S(1)} %slice.101), channel_id=1, source_target_pairs={{0,8},{4,12},{8,0},{12,4},{16,24},{20,28},{24,16},{28,20},{1,9},{5... | collective-permute-start | bytes 1671176 | tf_op jit(solution)/shard_map/ppermute | solution.py:880
  145.6 38.1 %collective-permute-start.4 = (bf16[272,1024]{1,0:T(8,128)(2,1)S(1)}, bf16[272,1024]{1,0:T(8,128)(2,1)S(1)}, u32[]{:S(2)}, u32[]{:S(2)}) collective-permute-start(bf16[272,1024]{1,0:T(8,128)(2,1)S(1)} %slice.100), channel_id=1, source_target_pairs={{0,16},{4,20},{8,24},{12,28},{16,0},{20,4},{24,8},{28,12},{1,17},{... | collective-permute-start | bytes 1671176 | tf_op jit(solution)/shard_map/ppermute | solution.py:880
  191.5 484.9 %reduce-scatter.3.cloned.1.call-start = ((), (), s32[]{:S(2)}) async-start(), calls=%async_computation.2 | async-start | bytes 7864320 | tf_op jit(solution)/shard_map/reduce_scatter | solution.py:1071
  191.9 68.5 %collective-permute-start.14 = (bf16[544,1024]{1,0:T(8,128)(2,1)}, bf16[544,1024]{1,0:T(8,128)(2,1)}, u32[]{:S(2)}, u32[]{:S(2)}) collective-permute-start(bf16[544,1024]{1,0:T(8,128)(2,1)} %get-tuple-element.129.refs_15_), channel_id=1, source_target_pairs={{0,24},{4,28},{8,16},{12,20},{16,8},{20,12},{24,0},{28,4},{1,25},{... | collective-permute-start | bytes 3342344 | tf_op jit(solution)/shard_map/ppermute | solution.py:880
  193.5 67.0 %collective-permute-start.13 = (bf16[544,1024]{1,0:T(8,128)(2,1)}, bf16[544,1024]{1,0:T(8,128)(2,1)}, u32[]{:S(2)}, u32[]{:S(2)}) collective-permute-start(bf16[544,1024]{1,0:T(8,128)(2,1)} %get-tuple-element.129.refs_15_), channel_id=1, source_target_pairs={{0,16},{4,20},{8,24},{12,28},{16,0},{20,4},{24,8},{28,12},{1,17},{... | collective-permute-start | bytes 3342344 | tf_op jit(solution)/shard_map/ppermute | solution.py:880
  195.0 65.5 %collective-permute-start.6 = (bf16[544,1024]{1,0:T(8,128)(2,1)}, bf16[544,1024]{1,0:T(8,128)(2,1)}, u32[]{:S(2)}, u32[]{:S(2)}) collective-permute-start(bf16[544,1024]{1,0:T(8,128)(2,1)} %get-tuple-element.129.refs_15_), channel_id=1, source_target_pairs={{0,8},{4,12},{8,0},{12,4},{16,24},{20,28},{24,16},{28,20},{1,9},{5... | collective-permute-start | bytes 3342344 | tf_op jit(solution)/shard_map/ppermute | solution.py:880
  201.4 63.2 %collective-permute-start.17 = (bf16[256,1024]{1,0:T(8,128)(2,1)}, bf16[256,1024]{1,0:T(8,128)(2,1)}, u32[]{:S(2)}, u32[]{:S(2)}) collective-permute-start(bf16[256,1024]{1,0:T(8,128)(2,1)} %slice.122), channel_id=1, source_target_pairs={{0,8},{4,12},{8,0},{12,4},{16,24},{20,28},{24,16},{28,20},{1,9},{5... | collective-permute-start | bytes 1572872 | tf_op jit(solution)/shard_map/ppermute | solution.py:880
  202.8 61.8 %collective-permute-start.16 = (bf16[256,1024]{1,0:T(8,128)(2,1)}, bf16[256,1024]{1,0:T(8,128)(2,1)}, u32[]{:S(2)}, u32[]{:S(2)}) collective-permute-start(bf16[256,1024]{1,0:T(8,128)(2,1)} %slice.121), channel_id=1, source_target_pairs={{0,16},{4,20},{8,24},{12,28},{16,0},{20,4},{24,8},{28,12},{1,17},{... | collective-permute-start | bytes 1572872 | tf_op jit(solution)/shard_map/ppermute | solution.py:880
  367.2 48.1 %collective-permute-start.21 = (bf16[528,1024]{1,0:T(8,128)(2,1)}, bf16[528,1024]{1,0:T(8,128)(2,1)}, u32[]{:S(2)}, u32[]{:S(2)}) collective-permute-start(bf16[528,1024]{1,0:T(8,128)(2,1)} %get-tuple-element.162), channel_id=1, source_target_pairs={{0,16},{4,20},{8,24},{12,28},{16,0},{20,4},{24,8},{28,12},{1,17},{... | collective-permute-start | bytes 3244040 | tf_op jit(solution)/shard_map/ppermute | solution.py:880
  378.1 37.2 %collective-permute-start.23 = (bf16[528,1024]{1,0:T(8,128)(2,1)}, bf16[528,1024]{1,0:T(8,128)(2,1)}, u32[]{:S(2)}, u32[]{:S(2)}) collective-permute-start(bf16[528,1024]{1,0:T(8,128)(2,1)} %get-tuple-element.169), channel_id=1, source_target_pairs={{0,8},{4,12},{8,0},{12,4},{16,24},{20,28},{24,16},{28,20},{1,9},{5... | collective-permute-start | bytes 3244040 | tf_op jit(solution)/shard_map/ppermute | solution.py:880
  421.0 255.4 %reduce-scatter.5.cloned.1.call-start = ((), (), s32[]{:S(2)}) async-start(), calls=%async_computation.3 | async-start | bytes 7864320 | tf_op jit(solution)/shard_map/reduce_scatter | solution.py:1071
  421.1 38.3 %collective-permute-start.22 = (bf16[528,1024]{1,0:T(8,128)(2,1)}, bf16[528,1024]{1,0:T(8,128)(2,1)}, u32[]{:S(2)}, u32[]{:S(2)}) collective-permute-start(bf16[528,1024]{1,0:T(8,128)(2,1)} %add_convert_fusion.3), channel_id=1, source_target_pairs={{0,8},{4,12},{8,0},{12,4},{16,24},{20,28},{24,16},{28,20},{1,9},{5... | collective-permute-start | bytes 3244040 | tf_op jit(solution)/shard_map/ppermute | solution.py:880
  421.7 37.7 %collective-permute-start.24 = (bf16[528,1024]{1,0:T(8,128)(2,1)}, bf16[528,1024]{1,0:T(8,128)(2,1)}, u32[]{:S(2)}, u32[]{:S(2)}) collective-permute-start(bf16[528,1024]{1,0:T(8,128)(2,1)} %add_convert_fusion.2), channel_id=1, source_target_pairs={{0,16},{4,20},{8,24},{12,28},{16,0},{20,4},{24,8},{28,12},{1,17},{... | collective-permute-start | bytes 3244040 | tf_op jit(solution)/shard_map/ppermute | solution.py:880
  502.4 53.4 %collective-permute-start.29 = (bf16[528,1024]{1,0:T(8,128)(2,1)}, bf16[528,1024]{1,0:T(8,128)(2,1)}, u32[]{:S(2)}, u32[]{:S(2)}) collective-permute-start(bf16[528,1024]{1,0:T(8,128)(2,1)} %get-tuple-element.190), channel_id=1, source_target_pairs={{0,8},{4,12},{8,0},{12,4},{16,24},{20,28},{24,16},{28,20},{1,9},{5... | collective-permute-start | bytes 3244040 | tf_op jit(solution)/shard_map/ppermute | solution.py:880
  502.9 40.7 %collective-permute-start.30 = (bf16[528,1024]{1,0:T(8,128)(2,1)}, bf16[528,1024]{1,0:T(8,128)(2,1)}, u32[]{:S(2)}, u32[]{:S(2)}) collective-permute-start(bf16[528,1024]{1,0:T(8,128)(2,1)} %get-tuple-element.193), channel_id=1, source_target_pairs={{0,16},{4,20},{8,24},{12,28},{16,0},{20,4},{24,8},{28,12},{1,17},{... | collective-permute-start | bytes 3244040 | tf_op jit(solution)/shard_map/ppermute | solution.py:880
  504.4 48.2 %collective-permute-start.32 = (bf16[528,1024]{1,0:T(8,128)(2,1)}, bf16[528,1024]{1,0:T(8,128)(2,1)}, u32[]{:S(2)}, u32[]{:S(2)}) collective-permute-start(bf16[528,1024]{1,0:T(8,128)(2,1)} %get-tuple-element.205), channel_id=1, source_target_pairs={{0,8},{4,12},{8,0},{12,4},{16,24},{20,28},{24,16},{28,20},{1,9},{5... | collective-permute-start | bytes 3244040 | tf_op jit(solution)/shard_map/ppermute | solution.py:880
  505.9 49.9 %collective-permute-start.34 = (bf16[528,1024]{1,0:T(8,128)(2,1)}, bf16[528,1024]{1,0:T(8,128)(2,1)}, u32[]{:S(2)}, u32[]{:S(2)}) collective-permute-start(bf16[528,1024]{1,0:T(8,128)(2,1)} %get-tuple-element.208), channel_id=1, source_target_pairs={{0,16},{4,20},{8,24},{12,28},{16,0},{20,4},{24,8},{28,12},{1,17},{... | collective-permute-start | bytes 3244040 | tf_op jit(solution)/shard_map/ppermute | solution.py:880
  (40 other events, 712.5 us)
Sparse Core Ops, SparseCore 0:
  11.3 131.4 all-gather.4
  191.6 115.6 all-gather.6
  421.2 107.1 reduce-scatter.2
  530.5 111.2 reduce-scatter.4

commit v5 on v4

--- a/solution.py
+++ b/solution.py
@@ -901,7 +901,8 @@
     if earlier:
         pieces = [pieces[0]] + [after(p, *earlier) for p in pieces[1:]]
     chips = size // 2
-    mine = jnp.stack(pieces[: chips - 1] + [jnp.concatenate(pieces[chips - 1 :])])
+    last = pieces[chips - 1 :]
+    mine = jnp.stack(pieces[: chips - 1] + [jnp.concatenate(last) if last[1:] else last[0]])
     return mine, swap(mine, 1, size)
 
 
@@ -976,31 +977,37 @@
             x, pack, gain_one, gain_two, block_ids[m, 0], routes[m, 0], tables, q_width, kv_width, experts
         )
 
-    def dispatched(m, pay, grad):
-        carried = None
-        for side in range(2):
-            carried = dispatch(sel, pay[side], grad[side], side, 2, held, carried)
+    def dispatched(pay, grad, carried):
+        side = 0 if carried is None else 1
+        return dispatch(sel, pay[side], grad[side], side, 2, held, carried)
+
+    def flat(carried):
         return [c.reshape(held, 2 * chips * CAP, width) for c in carried]
 
     saved, arrived, pays, moved, done, terms = [], [], [], [], {}, []
     ready = ()
     for m in range(micro):
         grad = after(out_grad[m, 0], *ready)
-        grad_near = send_near(grad, owners) if square else None
+        grad_near = None
+        if square and m:
+            grad_near = tuple(after(near, first_half[0]) for near in send_near(grad, owners))
+        found_grad = gather_chips(grad, grad_near, owners)
         if m == 0:
-            saved.append(forward(0, after(inputs[0, 0], *(grad_near if square else ()))))
+            saved.append(forward(0, after(inputs[0, 0], *found_grad[1:])))
             for n in range(1, micro):
                 saved.append(forward(n, after(inputs[n, 0], saved[n - 1][4])))
-        pay = saved[m][6]
+        pay = after(saved[m][6], *ready, *(grad_near or ()))
         pay_near = None
         if square and m == 0:
             one, two = send_near(pay, owners)
-            ready = (saved[-1][4],)
             pay_near = after(one, saved[-1][4]), after(two, saved[-1][4])
-        elif m:
-            pay = after(pay, *arrived[m - 1][0][1:])
-            ready = (pay,)
-        arrived.append((gather_chips(pay, pay_near, owners), gather_chips(grad, grad_near, owners), grad_near))
+        found_pay = gather_chips(pay, pay_near, owners)
+        ready = tuple(found_pay[chips - 1 :])
+        arrived.append((found_pay, found_grad, grad_near))
+        if m == 0:
+            first_grad = both_cores(found_grad, owners)
+            pays.append(both_cores(found_pay, owners, first_grad[0]))
+            first_half = dispatched(pays[0], first_grad, None)
 
     def expert_part(m, g, *earlier):
         prior = done[m - 1, g][3] if m else None
@@ -1037,17 +1044,19 @@
 
     added, far, rest = (), (), ()
     for m in range(micro):
-        held_back = (done[m - 1, 0][2],) if m else ()
-        pay_held = arrived[m + 1][2] if m == 0 and micro > 1 and square else held_back
-        pays.append(both_cores(arrived[m][0], owners, *pay_held))
-        moved.append(dispatched(m, pays[m], both_cores(arrived[m][1], owners, *held_back)))
-        hold = arrived[m + 1][2] if m + 1 < micro and square else ()
         if m == 0:
+            moved.append(flat(dispatched(pays[0], first_grad, first_half)))
+            hold = arrived[1][2] if micro > 1 and square else ()
             expert_part(0, 0, *hold)
         else:
+            found_grad = both_cores(arrived[m][1], owners, done[m - 1, 0][2])
+            pays.append(both_cores(arrived[m][0], owners, found_grad[0]))
+            half = dispatched(pays[m], found_grad, None)
             for g in range(1, len(weights)):
-                expert_part(m - 1, g, moved[m][0])
+                expert_part(m - 1, g, half[0])
             kept = returned(m - 1, far)
+            other = after(pays[m][1], kept[0], kept[-1])
+            moved.append(flat(dispatched((None, other), found_grad, half)))
             near = scatter_near(kept, owners, *rest)
             expert_part(m, 0, kept[0], kept[-1])
             added, far = scatter_far(kept, near, owners, done[m, 0][2])

time: 694 us -> 688 us (level)
  waiting for transfers between devices: 91.5 us -> 68 us
  Pallas kernels: 488 us -> 510 us
    pallas_call x1, Pallas kernels: 59.6 us -> 81.7 us  [gather_layer(): pl.pallas_call(functools.partial(gather_layer_kernel, chips=chips, depth=...]
    all_gather x2, waiting for transfers between devices: 16.9 us -> 0.01 us  [local(): lax.all_gather(packed[g:g + group], 'dp', axis=0, tiled=False)]
    ppermute x35 -> x34, waiting for transfers between devices: 74.4 us -> 67.2 us  [swap(): return lax.ppermute(value, 'fsdp', [(i, i ^ distance) for i in range(size)])]
    ppermute x35 -> x34, starting transfers between devices: 34.1 us -> 31.3 us  [swap(): return lax.ppermute(value, 'fsdp', [(i, i ^ distance) for i in range(size)])]
    another operation x7 -> x6, other arithmetic: 16 us -> 16.1 us  [both_cores(): jnp.stack(pieces[:chips - 1] + [jnp.concatenate(last) if last[1:] else la...]
  transfers between devices with their start and end apart: 39 -> 38, of which waited for: 11 -> 10; matrix products, arithmetic and copies ran while one was open for 6% -> 7% of each run, Pallas kernels for 65% -> 68%
where the time goes in v5:
time: 688 us; the launch traced here: 684 us
  Pallas kernels  510 us (74%)
  waiting for transfers between devices  68 us (10%)
  starting transfers between devices  31.5 us (5%)
  other arithmetic  30.9 us (4%)
  local copies, waits for them, and re-layouts  29.9 us (4%)
  between operations  14.3 us (2%)
    pallas_call x4, Pallas kernels, experts_step(): pl.pallas_call(functools.partial(expert_kernel, chunk=rows // 3, tile=256...  141 us
    pallas_call x1, Pallas kernels, gather_layer(): pl.pallas_call(functools.partial(gather_layer_kernel, chips=chips, depth=...  81.7 us
    pallas_call x2, Pallas kernels, attention_backward(): pl.pallas_call(functools.partial(attention_backward_kernel, terms=len(ter...  76.5 us
    pallas_call x8, Pallas kernels, combine(): pl.pallas_call(functools.partial(combine_kernel, groups=groups, local=loc...  68 us
    ppermute x34, waiting for transfers between devices, swap(): return lax.ppermute(value, 'fsdp', [(i, i ^ distance) for i in range(size)])  67.2 us
    pallas_call x1, Pallas kernels, reduce_layer(): pl.pallas_call(functools.partial(reduce_layer_kernel, chips=chips, depth=...  55.1 us
    pallas_call x2, Pallas kernels, attention_forward(): pl.pallas_call(functools.partial(attention_forward_kernel, q_width=q_widt...  43.8 us
    pallas_call x4, Pallas kernels, dispatch(): pl.pallas_call(functools.partial(dispatch_kernel, local=local), out_shape...  43.6 us
  transfers between devices with their start and end apart: 38, of which 10 were waited for; matrix products, arithmetic and copies ran while one was open for 7% of the time, Pallas kernels for 68%

profile of v5, /device:TPU:0, one launch (start us, length us, event | category | flops | bytes accessed | tf_op | source)
XLA Modules:
  0.0 684.4 jit_solution(11930384174274113235)
XLA Ops:
  20.0 81.7 %gather_layer.1.w_ref.refs_1_ = bf16[1024,3200]{1,0:T(8,128)(2,1)} custom-call(bf16[32,3200]{1,0:T(8,128)(2,1)} %concatenate.15.w_ref), custom_call_target="tpu_custom_call" | custom-call | tf_op jit(solution)/shard_map/gather_layer/pallas_call | solution.py:754
  107.6 22.0 %attention_forward.2 = (bf16[512,1024]{1,0:T(8,128)(2,1)}, bf16[512,512]{1,0:T(8,128)(2,1)}, bf16[512,512]{1,0:T(8,128)(2,1)}, bf16[512,1024]{1,0:T(8,128)(2,1)}...) custom-call(bf16[512,1024]{1,0:T(8,128)(2,1)} %get-tuple-element.118.x_ref.refs_0_, ...), custom_call_target="tpu_custom_call" | custom-call | flops 29360128 | bytes 65536 | tf_op jit(solution)/shard_map/attention_forward/pallas_call | solution.py:179
  133.7 21.8 %attention_forward.3 = (bf16[512,1024]{1,0:T(8,128)(2,1)}, bf16[512,512]{1,0:T(8,128)(2,1)}, bf16[512,512]{1,0:T(8,128)(2,1)}, bf16[512,1024]{1,0:T(8,128)(2,1)}...) custom-call(bf16[512,1024]{1,0:T(8,128)(2,1)} %get-tuple-element.120.x_ref.refs_0_, ...), custom_call_target="tpu_custom_call" | custom-call | flops 29360128 | bytes 65536 | tf_op jit(solution)/shard_map/attention_forward/pallas_call | solution.py:179
  181.3 11.0 %dispatch.4 = (bf16[4,2,4,144,1024]{4,3,2,1,0:T(8,128)(2,1)}, bf16[4,2,4,144,1024]{4,3,2,1,0:T(8,128)(2,1)}) custom-call(bf16[8,32]{1,0:T(8,128)(2,1)} %fusion.1.sel_ref, bf16[4,544,1024]{2,1,0:T(8,128)(2,1)} %pad_maximum_fusion.pay_ref, bf16[4,512,1024]{2,1,0:T(8,128)(2,1)} %pad_maximum_fusion.2.grad_ref), custom_call_target="tpu_custom_call" | custom-call | flops 18874368 | bytes 81920 | tf_op jit(solution)/shard_map/dispatch/pallas_call | solution.py:250
  192.3 12.0 %collective-permute-done.8 = bf16[512,1024]{1,0:T(8,128)(2,1)} collective-permute-done((bf16[512,1024]{1,0:T(8,128)(2,1)}, bf16[512,1024]{1,0:T(8,128)(2,1)}, u32[]{:S(2)}, u32[]{:S(2)}) %collective-permute-start.8) | collective-permute-done | bytes 1048608 | tf_op jit(solution)/shard_map/ppermute | solution.py:880
  213.9 10.9 %dispatch.5 = (bf16[4,2,4,144,1024]{4,3,2,1,0:T(8,128)(2,1)}, bf16[4,2,4,144,1024]{4,3,2,1,0:T(8,128)(2,1)}) custom-call(bf16[8,32]{1,0:T(8,128)(2,1)} %fusion.1.sel_ref, bf16[4,544,1024]{2,1,0:T(8,128)(2,1)} %collective-permute-done.10.pay_ref, ...), custom_call_target="tpu_custom_call", output_to_operand_aliasing={{0}: (3, {}), {1}: (4, {})} | custom-call | flops 18874368 | bytes 81920 | tf_op jit(solution)/shard_map/dispatch/pallas_call | solution.py:250
  224.8 34.7 %experts.4 = (bf16[2,1152,1024]{2,1,0:T(8,128)(2,1)}, bf16[2,1152,1024]{2,1,0:T(8,128)(2,1)}, f32[2,1152,1]{2,1,0:T(8,128)}, bf16[4,2,768,512]{3,2,1,0:T(8,128)(2,1)}) custom-call(bf16[4,1152,1024]{2,1,0:T(8,128)(2,1)} %bitcast.79, bf16[4,1152,1024]{2,1,0:T(8,128)(2,1)} %bitcast.81, bf16[4,2,768,512]{3,2,1,0:T(8,128)(2,1)} %bitcast.138), custom_call_target="tpu_custom_call" | custom-call | flops 84934656 | bytes 122880 | tf_op jit(solution)/shard_map/experts/pallas_call | solution.py:391
  275.0 10.8 %dispatch.6 = (bf16[4,2,4,144,1024]{4,3,2,1,0:T(8,128)(2,1)}, bf16[4,2,4,144,1024]{4,3,2,1,0:T(8,128)(2,1)}) custom-call(bf16[8,32]{1,0:T(8,128)(2,1)} %fusion.1.sel_ref, bf16[4,544,1024]{2,1,0:T(8,128)(2,1)} %pad_maximum_fusion.1.pay_ref, bf16[4,512,1024]{2,1,0:T(8,128)(2,1)} %pad_maximum_fusion.3.grad_ref), custom_call_target="tpu_custom_call" | custom-call | flops 18874368 | bytes 81920 | tf_op jit(solution)/shard_map/dispatch/pallas_call | solution.py:250
  285.8 35.2 %experts.5 = (bf16[2,1152,1024]{2,1,0:T(8,128)(2,1)}, bf16[2,1152,1024]{2,1,0:T(8,128)(2,1)}, f32[2,1152,1]{2,1,0:T(8,128)}, bf16[4,2,768,512]{3,2,1,0:T(8,128)(2,1)}) custom-call(bf16[4,1152,1024]{2,1,0:T(8,128)(2,1)} %bitcast.80, bf16[4,1152,1024]{2,1,0:T(8,128)(2,1)} %bitcast.82, bf16[4,2,768,512]{3,2,1,0:T(8,128)(2,1)} %bitcast.136), custom_call_target="tpu_custom_call" | custom-call | flops 84934656 | bytes 122880 | tf_op jit(solution)/shard_map/experts/pallas_call | solution.py:391
  321.0 7.5 %combine.8 = bf16[2,1056,1024]{2,1,0:T(8,128)(2,1)} custom-call(bf16[8,32]{1,0:T(8,128)(2,1)} %fusion.1.sel_ref, bf16[4,544,1024]{2,1,0:T(8,128)(2,1)} %collective-permute-done.10.pay_ref, bf16[2,8,144,1024]{3,2,1,0:T(8,128)(2,1)} %bitcast.91, bf16[2,8,144,1024]{3,2,1,0:T(8,128)(2,1)} %bitcast.107, bf16[2,8,144,1024]{3,2,1,0:T(8,128)(2,1)} %bitcast.95, ...), custom_call_target="tpu_custom_call" | custom-call | flops 2415919104 | bytes 20971520 | tf_op jit(solution)/shard_map/combine/pallas_call | solution.py:491
  337.0 9.4 %combine.10 = (bf16[528,1024]{1,0:T(8,128)(2,1)}, bf16[528,1024]{1,0:T(8,128)(2,1)}, bf16[528,1024]{1,0:T(8,128)(2,1)}, bf16[528,1024]{1,0:T(8,128)(2,1)}) custom-call(bf16[8,32]{1,0:T(8,128)(2,1)} %fusion.1.sel_ref, bf16[4,544,1024]{2,1,0:T(8,128)(2,1)} %pad_maximum_fusion.pay_ref, bf16[2,8,144,1024]{3,2,1,0:T(8,128)(2,1)} %bitcast.93, ...), custom_call_target="tpu_custom_call" | custom-call | flops 2415919104 | bytes 20971520 | tf_op jit(solution)/shard_map/combine/pallas_call | solution.py:491
  348.8 9.4 %combine.11 = (bf16[528,1024]{1,0:T(8,128)(2,1)}, bf16[528,1024]{1,0:T(8,128)(2,1)}, bf16[528,1024]{1,0:T(8,128)(2,1)}, bf16[528,1024]{1,0:T(8,128)(2,1)}) custom-call(bf16[8,32]{1,0:T(8,128)(2,1)} %fusion.1.sel_ref, bf16[4,544,1024]{2,1,0:T(8,128)(2,1)} %pad_maximum_fusion.pay_ref, bf16[2,8,144,1024]{3,2,1,0:T(8,128)(2,1)} %bitcast.94, ...), custom_call_target="tpu_custom_call" | custom-call | flops 2415919104 | bytes 20971520 | tf_op jit(solution)/shard_map/combine/pallas_call | solution.py:491
  358.2 11.0 %dispatch.7 = (bf16[4,2,4,144,1024]{4,3,2,1,0:T(8,128)(2,1)}, bf16[4,2,4,144,1024]{4,3,2,1,0:T(8,128)(2,1)}) custom-call(bf16[8,32]{1,0:T(8,128)(2,1)} %fusion.1.sel_ref, bf16[4,544,1024]{2,1,0:T(8,128)(2,1)} %collective-permute-done.16.pay_ref, ...), custom_call_target="tpu_custom_call", output_to_operand_aliasing={{0}: (3, {}), {1}: (4, {})} | custom-call | flops 18874368 | bytes 81920 | tf_op jit(solution)/shard_map/dispatch/pallas_call | solution.py:250
  369.2 35.7 %experts.6 = (bf16[2,1152,1024]{2,1,0:T(8,128)(2,1)}, bf16[2,1152,1024]{2,1,0:T(8,128)(2,1)}, f32[2,1152,1]{2,1,0:T(8,128)}, bf16[4,2,768,512]{3,2,1,0:T(8,128)(2,1)}) custom-call(bf16[4,1152,1024]{2,1,0:T(8,128)(2,1)} %bitcast.131, bf16[4,1152,1024]{2,1,0:T(8,128)(2,1)} %bitcast.133, bf16[4,2,768,512]{3,2,1,0:T(8,128)(2,1)} %bitcast.139, ...), custom_call_target="tpu_custom_call" | custom-call | flops 21743271936 | bytes 31457280 | tf_op jit(solution)/shard_map/experts/pallas_call | solution.py:391
  412.4 35.7 %experts.7 = (bf16[2,1152,1024]{2,1,0:T(8,128)(2,1)}, bf16[2,1152,1024]{2,1,0:T(8,128)(2,1)}, f32[2,1152,1]{2,1,0:T(8,128)}, bf16[4,2,768,512]{3,2,1,0:T(8,128)(2,1)}) custom-call(bf16[4,1152,1024]{2,1,0:T(8,128)(2,1)} %bitcast.132, bf16[4,1152,1024]{2,1,0:T(8,128)(2,1)} %bitcast.134, bf16[4,2,768,512]{3,2,1,0:T(8,128)(2,1)} %bitcast.137, ...), custom_call_target="tpu_custom_call" | custom-call | flops 21743271936 | bytes 31457280 | tf_op jit(solution)/shard_map/experts/pallas_call | solution.py:391
  448.2 7.5 %combine.12 = bf16[2,1056,1024]{2,1,0:T(8,128)(2,1)} custom-call(bf16[8,32]{1,0:T(8,128)(2,1)} %fusion.1.sel_ref, bf16[4,544,1024]{2,1,0:T(8,128)(2,1)} %collective-permute-done.16.pay_ref, bf16[2,8,144,1024]{3,2,1,0:T(8,128)(2,1)} %bitcast.83, bf16[2,8,144,1024]{3,2,1,0:T(8,128)(2,1)} %bitcast.99, bf16[2,8,144,1024]{3,2,1,0:T(8,128)(2,1)} %bitcast.87, ...), custom_call_target="tpu_custom_call" | custom-call | flops 2415919104 | bytes 20971520 | tf_op jit(solution)/shard_map/combine/pallas_call | solution.py:491
  455.7 7.6 %combine.13 = bf16[2,1056,1024]{2,1,0:T(8,128)(2,1)} custom-call(bf16[8,32]{1,0:T(8,128)(2,1)} %fusion.1.sel_ref, bf16[4,544,1024]{2,1,0:T(8,128)(2,1)} %collective-permute-done.16.pay_ref, bf16[2,8,144,1024]{3,2,1,0:T(8,128)(2,1)} %bitcast.84, bf16[2,8,144,1024]{3,2,1,0:T(8,128)(2,1)} %bitcast.100, bf16[2,8,144,1024]{3,2,1,0:T(8,128)(2,1)} %bitcast.88, ...), custom_call_target="tpu_custom_call" | custom-call | flops 2415919104 | bytes 20971520 | tf_op jit(solution)/shard_map/combine/pallas_call | solution.py:491
  466.1 9.4 %combine.14 = (bf16[528,1024]{1,0:T(8,128)(2,1)}, bf16[528,1024]{1,0:T(8,128)(2,1)}, bf16[528,1024]{1,0:T(8,128)(2,1)}, bf16[528,1024]{1,0:T(8,128)(2,1)}) custom-call(bf16[8,32]{1,0:T(8,128)(2,1)} %fusion.1.sel_ref, bf16[4,544,1024]{2,1,0:T(8,128)(2,1)} %pad_maximum_fusion.1.pay_ref, bf16[2,8,144,1024]{3,2,1,0:T(8,128)(2,1)} %bitcast.85, ...), custom_call_target="tpu_custom_call" | custom-call | flops 2415919104 | bytes 20971520 | tf_op jit(solution)/shard_map/combine/pallas_call | solution.py:491
  475.5 14.4 %collective-permute-done.27.refs_22_ = bf16[528,1024]{1,0:T(8,128)(2,1)} collective-permute-done((bf16[528,1024]{1,0:T(8,128)(2,1)}, bf16[528,1024]{1,0:T(8,128)(2,1)}, u32[]{:S(2)}, u32[]{:S(2)}) %collective-permute-start.27) | collective-permute-done | bytes 1081376 | tf_op jit(solution)/shard_map/ppermute | solution.py:880
  492.5 9.6 %combine.15 = (bf16[528,1024]{1,0:T(8,128)(2,1)}, bf16[528,1024]{1,0:T(8,128)(2,1)}, bf16[528,1024]{1,0:T(8,128)(2,1)}, bf16[528,1024]{1,0:T(8,128)(2,1)}) custom-call(bf16[8,32]{1,0:T(8,128)(2,1)} %fusion.1.sel_ref, bf16[4,544,1024]{2,1,0:T(8,128)(2,1)} %pad_maximum_fusion.1.pay_ref, bf16[2,8,144,1024]{3,2,1,0:T(8,128)(2,1)} %bitcast.86, ...), custom_call_target="tpu_custom_call" | custom-call | flops 2415919104 | bytes 20971520 | tf_op jit(solution)/shard_map/combine/pallas_call | solution.py:491
  504.3 37.3 %attention_backward.2 = (bf16[2,512,1024]{2,1,0:T(8,128)(2,1)}, f32[2,512,1024]{2,1,0:T(8,128)}, bf16[1024,3200]{1,0:T(8,128)(2,1)}) custom-call(bf16[512,1024]{1,0:T(8,128)(2,1)} %get-tuple-element.118.x_ref.refs_0_, bf16[1024,3200]{1,0:T(8,128)(2,1)} %gather_layer.1.w_ref.refs_1_, f32[1,1024]{1,0:T(1,128)} %bitcast.155, f32[1,1024]{1,0:T(1,128)} %bitcast.151, ...), custom_call_target="tpu_custom_call" | custom-call | flops 17179869184 | bytes 41943040 | tf_op jit(solution)/shard_map/attention_backward/pallas_call | solution.py:643
  547.4 19.9 %collective-permute-done.32.refs_21_ = bf16[528,1024]{1,0:T(8,128)(2,1)S(1)} collective-permute-done((bf16[528,1024]{1,0:T(8,128)(2,1)S(1)}, bf16[528,1024]{1,0:T(8,128)(2,1)S(1)}, u32[]{:S(2)}, u32[]{:S(2)}) %collective-permute-start.32) | collective-permute-done | bytes 1081376 | tf_op jit(solution)/shard_map/ppermute | solution.py:880
  570.9 39.2 %attention_backward.3 = (bf16[2,512,1024]{2,1,0:T(8,128)(2,1)}, f32[2,512,1024]{2,1,0:T(8,128)}, bf16[1024,3200]{1,0:T(8,128)(2,1)}) custom-call(bf16[512,1024]{1,0:T(8,128)(2,1)} %get-tuple-element.120.x_ref.refs_0_, bf16[1024,3200]{1,0:T(8,128)(2,1)} %gather_layer.1.w_ref.refs_1_, ...), custom_call_target="tpu_custom_call", output_to_operand_aliasing={{0}: (24, {}), {1}: (25, {})} | custom-call | flops 17179869184 | bytes 41943040 | tf_op jit(solution)/shard_map/attention_backward/pallas_call | solution.py:643
  610.1 55.1 %reduce_layer.1 = f32[32,3200]{1,0:T(8,128)} custom-call(bf16[1024,3200]{1,0:T(8,128)(2,1)} %get-tuple-element.219.pack_ref), custom_call_target="tpu_custom_call" | custom-call | bytes 1073741824 | tf_op jit(solution)/shard_map/reduce_layer/pallas_call | solution.py:857
  (160 shorter events, 121.3 us)
Async XLA Ops:
  7.2 217.6 %all-gather.5.cloned.1.call-start = ((), (), s32[]{:S(2)}) async-start(), calls=%async_computation.4 | async-start | bytes 7864320 | tf_op jit(solution)/shard_map/all_gather | solution.py:959
  11.2 274.6 %all-gather.7.cloned.1.call-start = ((), (), s32[]{:S(2)}) async-start(), calls=%async_computation.5 | async-start | bytes 7864320 | tf_op jit(solution)/shard_map/all_gather | solution.py:959
  12.0 659.2 %reduce-scatter.3.cloned.1.call-start = ((), (), s32[]{:S(2)}) async-start(), calls=%async_computation.2 | async-start | bytes 7864320 | tf_op jit(solution)/shard_map/reduce_scatter | solution.py:1080
  14.5 93.1 %collective-permute-start = (bf16[512,1024]{1,0:T(8,128)(2,1)S(1)}, bf16[512,1024]{1,0:T(8,128)(2,1)}, u32[]{:S(2)}, u32[]{:S(2)}) collective-permute-start(bf16[512,1024]{1,0:T(8,128)(2,1)S(1)} %get-tuple-element.270.refs_8_), channel_id=1, source_target_pairs={{0,8},{4,12},{8,0},{12,4},{16,24},{20,28},{24,16},{28,20},{1,9},{5... | collective-permute-start | bytes 3145736 | tf_op jit(solution)/shard_map/ppermute | solution.py:880
  17.5 90.2 %collective-permute-start.1 = (bf16[512,1024]{1,0:T(8,128)(2,1)S(1)}, bf16[512,1024]{1,0:T(8,128)(2,1)}, u32[]{:S(2)}, u32[]{:S(2)}) collective-permute-start(bf16[512,1024]{1,0:T(8,128)(2,1)S(1)} %get-tuple-element.270.refs_8_), channel_id=1, source_target_pairs={{0,16},{4,20},{8,24},{12,28},{16,0},{20,4},{24,8},{28,12},{1,17},{... | collective-permute-start | bytes 3145736 | tf_op jit(solution)/shard_map/ppermute | solution.py:880
  19.0 88.7 %collective-permute-start.2 = (bf16[512,1024]{1,0:T(8,128)(2,1)S(1)}, bf16[512,1024]{1,0:T(8,128)(2,1)}, u32[]{:S(2)}, u32[]{:S(2)}) collective-permute-start(bf16[512,1024]{1,0:T(8,128)(2,1)S(1)} %get-tuple-element.270.refs_8_), channel_id=1, source_target_pairs={{0,24},{4,28},{8,16},{12,20},{16,8},{20,12},{24,0},{28,4},{1,25},{... | collective-permute-start | bytes 3145736 | tf_op jit(solution)/shard_map/ppermute | solution.py:880
  131.0 28.7 %collective-permute-start.5 = (bf16[544,1024]{1,0:T(8,128)(2,1)}, bf16[544,1024]{1,0:T(8,128)(2,1)}, u32[]{:S(2)}, u32[]{:S(2)}) collective-permute-start(bf16[544,1024]{1,0:T(8,128)(2,1)} %get-tuple-element.129.refs_15_), channel_id=1, source_target_pairs={{0,16},{4,20},{8,24},{12,28},{16,0},{20,4},{24,8},{28,12},{1,17},{... | collective-permute-start | bytes 3342344 | tf_op jit(solution)/shard_map/ppermute | solution.py:880
  178.4 34.9 %collective-permute-start.10 = (bf16[4,544,1024]{2,1,0:T(8,128)(2,1)}, bf16[4,544,1024]{2,1,0:T(8,128)(2,1)}, u32[]{:S(2)}, u32[]{:S(2)}) collective-permute-start(bf16[4,544,1024]{2,1,0:T(8,128)(2,1)} %pad_maximum_fusion.pay_ref), channel_id=1, source_target_pairs={{0,4},{4,0},{8,12},{12,8},{16,20},{20,16},{24,28},{28,24},{1,5},{5... | collective-permute-start | bytes 13369352 | tf_op jit(solution)/shard_map/ppermute | solution.py:880
  178.4 31.3 %collective-permute-start.11 = (bf16[4,512,1024]{2,1,0:T(8,128)(2,1)}, bf16[4,512,1024]{2,1,0:T(8,128)(2,1)}, u32[]{:S(2)}, u32[]{:S(2)}) collective-permute-start(bf16[4,512,1024]{2,1,0:T(8,128)(2,1)} %pad_maximum_fusion.2.grad_ref), channel_id=1, source_target_pairs={{0,4},{4,0},{8,12},{12,8},{16,20},{20,16},{24,28},{28,24},{1,5},{5... | collective-permute-start | bytes 12582920 | tf_op jit(solution)/shard_map/ppermute | solution.py:880
  204.4 66.8 %collective-permute-start.9 = (bf16[544,1024]{1,0:T(8,128)(2,1)}, bf16[544,1024]{1,0:T(8,128)(2,1)}, u32[]{:S(2)}, u32[]{:S(2)}) collective-permute-start(bf16[544,1024]{1,0:T(8,128)(2,1)} %get-tuple-element.140.refs_15_), channel_id=1, source_target_pairs={{0,8},{4,12},{8,0},{12,4},{16,24},{20,28},{24,16},{28,20},{1,9},{5... | collective-permute-start | bytes 3342344 | tf_op jit(solution)/shard_map/ppermute | solution.py:880
  205.7 65.5 %collective-permute-start.14 = (bf16[544,1024]{1,0:T(8,128)(2,1)}, bf16[544,1024]{1,0:T(8,128)(2,1)}, u32[]{:S(2)}, u32[]{:S(2)}) collective-permute-start(bf16[544,1024]{1,0:T(8,128)(2,1)} %get-tuple-element.140.refs_15_), channel_id=1, source_target_pairs={{0,16},{4,20},{8,24},{12,28},{16,0},{20,4},{24,8},{28,12},{1,17},{... | collective-permute-start | bytes 3342344 | tf_op jit(solution)/shard_map/ppermute | solution.py:880
  206.7 64.5 %collective-permute-start.15 = (bf16[544,1024]{1,0:T(8,128)(2,1)}, bf16[544,1024]{1,0:T(8,128)(2,1)}, u32[]{:S(2)}, u32[]{:S(2)}) collective-permute-start(bf16[544,1024]{1,0:T(8,128)(2,1)} %get-tuple-element.140.refs_15_), channel_id=1, source_target_pairs={{0,24},{4,28},{8,16},{12,20},{16,8},{20,12},{24,0},{28,4},{1,25},{... | collective-permute-start | bytes 3342344 | tf_op jit(solution)/shard_map/ppermute | solution.py:880
  209.8 56.4 %collective-permute-start.12 = (bf16[256,1024]{1,0:T(8,128)(2,1)}, bf16[256,1024]{1,0:T(8,128)(2,1)}, u32[]{:S(2)}, u32[]{:S(2)}) collective-permute-start(bf16[256,1024]{1,0:T(8,128)(2,1)} %slice.97), channel_id=1, source_target_pairs={{0,16},{4,20},{8,24},{12,28},{16,0},{20,4},{24,8},{28,12},{1,17},{... | collective-permute-start | bytes 1572872 | tf_op jit(solution)/shard_map/ppermute | solution.py:880
  213.3 52.9 %collective-permute-start.13 = (bf16[256,1024]{1,0:T(8,128)(2,1)}, bf16[256,1024]{1,0:T(8,128)(2,1)}, u32[]{:S(2)}, u32[]{:S(2)}) collective-permute-start(bf16[256,1024]{1,0:T(8,128)(2,1)} %slice.98), channel_id=1, source_target_pairs={{0,8},{4,12},{8,0},{12,4},{16,24},{20,28},{24,16},{28,20},{1,9},{5... | collective-permute-start | bytes 1572872 | tf_op jit(solution)/shard_map/ppermute | solution.py:880
  346.5 58.4 %collective-permute-start.22 = (bf16[528,1024]{1,0:T(8,128)(2,1)}, bf16[528,1024]{1,0:T(8,128)(2,1)}, u32[]{:S(2)}, u32[]{:S(2)}) collective-permute-start(bf16[528,1024]{1,0:T(8,128)(2,1)} %get-tuple-element.175), channel_id=1, source_target_pairs={{0,8},{4,12},{8,0},{12,4},{16,24},{20,28},{24,16},{28,20},{1,9},{5... | collective-permute-start | bytes 3244040 | tf_op jit(solution)/shard_map/ppermute | solution.py:880
  347.3 60.6 %collective-permute-start.19 = (bf16[528,1024]{1,0:T(8,128)(2,1)}, bf16[528,1024]{1,0:T(8,128)(2,1)}, u32[]{:S(2)}, u32[]{:S(2)}) collective-permute-start(bf16[528,1024]{1,0:T(8,128)(2,1)} %get-tuple-element.165), channel_id=1, source_target_pairs={{0,16},{4,20},{8,24},{12,28},{16,0},{20,4},{24,8},{28,12},{1,17},{... | collective-permute-start | bytes 3244040 | tf_op jit(solution)/shard_map/ppermute | solution.py:880
  410.6 260.6 %reduce-scatter.5.cloned.1.call-start = ((), (), s32[]{:S(2)}) async-start(), calls=%async_computation.3 | async-start | bytes 7864320 | tf_op jit(solution)/shard_map/reduce_scatter | solution.py:1080
  410.7 37.4 %collective-permute-start.23 = (bf16[528,1024]{1,0:T(8,128)(2,1)}, bf16[528,1024]{1,0:T(8,128)(2,1)}, u32[]{:S(2)}, u32[]{:S(2)}) collective-permute-start(bf16[528,1024]{1,0:T(8,128)(2,1)} %add_convert_fusion.2), channel_id=1, source_target_pairs={{0,16},{4,20},{8,24},{12,28},{16,0},{20,4},{24,8},{28,12},{1,17},{... | collective-permute-start | bytes 3244040 | tf_op jit(solution)/shard_map/ppermute | solution.py:880
  411.3 36.8 %collective-permute-start.21 = (bf16[528,1024]{1,0:T(8,128)(2,1)}, bf16[528,1024]{1,0:T(8,128)(2,1)}, u32[]{:S(2)}, u32[]{:S(2)}) collective-permute-start(bf16[528,1024]{1,0:T(8,128)(2,1)} %add_convert_fusion.3), channel_id=1, source_target_pairs={{0,8},{4,12},{8,0},{12,4},{16,24},{20,28},{24,16},{28,20},{1,9},{5... | collective-permute-start | bytes 3244040 | tf_op jit(solution)/shard_map/ppermute | solution.py:880
  463.3 29.2 %collective-permute-start.25 = (bf16[2,1056,1024]{2,1,0:T(8,128)(2,1)}, bf16[2,1056,1024]{2,1,0:T(8,128)(2,1)}, u32[]{:S(2)}, u32[]{:S(2)}) collective-permute-start(bf16[2,1056,1024]{2,1,0:T(8,128)(2,1)} %combine.13), channel_id=1, source_target_pairs={{0,4},{4,0},{8,12},{12,8},{16,20},{20,16},{24,28},{28,24},{1,5},{5... | collective-permute-start | bytes 12976136 | tf_op jit(solution)/shard_map/ppermute | solution.py:880
  490.6 56.8 %collective-permute-start.33 = (bf16[528,1024]{1,0:T(8,128)(2,1)}, bf16[528,1024]{1,0:T(8,128)(2,1)}, u32[]{:S(2)}, u32[]{:S(2)}) collective-permute-start(bf16[528,1024]{1,0:T(8,128)(2,1)} %get-tuple-element.214), channel_id=1, source_target_pairs={{0,16},{4,20},{8,24},{12,28},{16,0},{20,4},{24,8},{28,12},{1,17},{... | collective-permute-start | bytes 3244040 | tf_op jit(solution)/shard_map/ppermute | solution.py:880
  491.7 49.9 %collective-permute-start.31 = (bf16[528,1024]{1,0:T(8,128)(2,1)}, bf16[528,1024]{1,0:T(8,128)(2,1)}, u32[]{:S(2)}, u32[]{:S(2)}) collective-permute-start(bf16[528,1024]{1,0:T(8,128)(2,1)} %get-tuple-element.211), channel_id=1, source_target_pairs={{0,8},{4,12},{8,0},{12,4},{16,24},{20,28},{24,16},{28,20},{1,9},{5... | collective-permute-start | bytes 3244040 | tf_op jit(solution)/shard_map/ppermute | solution.py:880
  502.1 42.8 %collective-permute-start.29 = (bf16[528,1024]{1,0:T(8,128)(2,1)}, bf16[528,1024]{1,0:T(8,128)(2,1)}, u32[]{:S(2)}, u32[]{:S(2)}) collective-permute-start(bf16[528,1024]{1,0:T(8,128)(2,1)} %get-tuple-element.199), channel_id=1, source_target_pairs={{0,16},{4,20},{8,24},{12,28},{16,0},{20,4},{24,8},{28,12},{1,17},{... | collective-permute-start | bytes 3244040 | tf_op jit(solution)/shard_map/ppermute | solution.py:880
  503.6 43.8 %collective-permute-start.28 = (bf16[528,1024]{1,0:T(8,128)(2,1)}, bf16[528,1024]{1,0:T(8,128)(2,1)}, u32[]{:S(2)}, u32[]{:S(2)}) collective-permute-start(bf16[528,1024]{1,0:T(8,128)(2,1)} %get-tuple-element.196), channel_id=1, source_target_pairs={{0,8},{4,12},{8,0},{12,4},{16,24},{20,28},{24,16},{28,20},{1,9},{5... | collective-permute-start | bytes 3244040 | tf_op jit(solution)/shard_map/ppermute | solution.py:880
  (35 other events, 702.7 us)
Sparse Core Ops, SparseCore 0:
  11.3 133.3 all-gather.4
  146.9 114.4 all-gather.6
  410.7 110.7 reduce-scatter.2
  523.7 111.2 reduce-scatter.4

commit v6 on v5

--- a/solution.py
+++ b/solution.py
@@ -184,7 +184,7 @@
         scratch_shapes=[pltpu.VMEM((rows, width), BF), pltpu.VMEM((rows, rows), F32)],
         compiler_params=pltpu.CompilerParams(vmem_limit_bytes=VMEM_LIMIT),
         cost_estimate=hint(
-            flops=flops, transcendentals=QUERY_HEADS * rows * rows, bytes_accessed=16 << 20
+            flops=flops, transcendentals=QUERY_HEADS * rows * rows, bytes_accessed=64 << 20, share=1
         ),
         name="attention_forward",
     )(x, pack, gain_one, gain_two, ids[None, :], ids[:, None], *tables, picks)
@@ -913,11 +913,11 @@
     return [swap(after(kept[6], *earlier), 2, size), swap(after(kept[7], *earlier), 4, size)]
 
 
-def scatter_far(kept, near, size, *earlier):
+def scatter_far(kept, near, size, *earlier, rest=()):
     if size != 8:
         return (), ()
     add = lambda a, b: (a.astype(F32) + b.astype(F32)).astype(BF)
-    by_one, by_two = after(near[0], *earlier), after(near[1], *earlier)
+    by_one, by_two = after(near[0], *earlier), after(near[1], *earlier, *rest[:1])
     one_sum, two_sum = add(kept[3], by_two), add(kept[4], by_one)
     return (one_sum, two_sum), (swap(one_sum, 2, size), swap(two_sum, 4, size))
 
@@ -985,7 +985,7 @@
         return [c.reshape(held, 2 * chips * CAP, width) for c in carried]
 
     saved, arrived, pays, moved, done, terms = [], [], [], [], {}, []
-    ready = ()
+    ready = (pack,)
     for m in range(micro):
         grad = after(out_grad[m, 0], *ready)
         grad_near = None
@@ -993,9 +993,9 @@
             grad_near = tuple(after(near, first_half[0]) for near in send_near(grad, owners))
         found_grad = gather_chips(grad, grad_near, owners)
         if m == 0:
-            saved.append(forward(0, after(inputs[0, 0], *found_grad[1:])))
+            saved.append(forward(0, inputs[0, 0]))
             for n in range(1, micro):
-                saved.append(forward(n, after(inputs[n, 0], saved[n - 1][4])))
+                saved.append(forward(n, after(inputs[n, 0], saved[n - 1][4], *found_grad[1:])))
         pay = after(saved[m][6], *ready, *(grad_near or ()))
         pay_near = None
         if square and m == 0:
@@ -1021,12 +1021,12 @@
             [done[m, g][i].reshape(group, 2 * chips, CAP, -1) for g in range(len(weights))]
             for i in range(3)
         ]
-        kept, before = [], earlier
+        kept, before = [], ()
         sent = {}
         span = chips // 2
         for first in (span, 0):
             (sent[first],) = combine(sel, after(pays[m][1], *before), *parts, 1, first, span, None)
-            before = (sent[first],)
+            before = (sent[first], *earlier)
         for first in (span, 0):
             found = combine(
                 sel, after(pays[m][0], *before), *parts, 0, first, span, swap(sent[first], 1, owners)
@@ -1054,29 +1054,29 @@
             half = dispatched(pays[m], found_grad, None)
             for g in range(1, len(weights)):
                 expert_part(m - 1, g, half[0])
-            kept = returned(m - 1, far)
+            kept = returned(m - 1, (*far, *rest))
             other = after(pays[m][1], kept[0], kept[-1])
             moved.append(flat(dispatched((None, other), found_grad, half)))
-            near = scatter_near(kept, owners, *rest)
+            near = scatter_near(kept, owners)
             expert_part(m, 0, kept[0], kept[-1])
             added, far = scatter_far(kept, near, owners, done[m, 0][2])
-            rest = scatter_rest(kept, owners, *far)
+            rest = scatter_rest(kept, owners, *near)
             terms.append(scattered(kept, near, far, rest))
     for g in range(1, len(weights)):
         expert_part(micro - 1, g, *added)
-    kept = returned(micro - 1, far)
-    near = scatter_near(kept, owners, *rest)
-    last_rest = scatter_rest(kept, owners, *rest)
+    kept = returned(micro - 1, (*far, *rest))
+    near = scatter_near(kept, owners)
+    last_rest = scatter_rest(kept, owners)
     made, prior, held_back = None, None, ()
     for m in range(micro - 1):
         made, prior = backward(m, [after(terms[m][0], kept[0], kept[-1])] + terms[m][1:], made, prior)
         held_back = (prior,)
-    last_far = scatter_far(kept, near, owners, *held_back)[1]
+    last_far = scatter_far(kept, near, owners, *held_back, rest=last_rest)[1]
     terms.append(scattered(kept, near, last_far, last_rest))
     made, prior = backward(micro - 1, terms[-1], made, prior)
     sums = []
     for g in range(len(weights)):
-        summed = after(done[micro - 1, g][3], *(far if g else added))
+        summed = after(done[micro - 1, g][3], *((kept[0], kept[-1]) if g else added))
         sums.append(lax.psum_scatter(summed, "dp", scatter_dimension=0, tiled=True)[0])
     layer = reduce_layer(prior, chips, depth, 5)
     marks = np.cumsum([0, q_width, kv_width, kv_width, width, experts, 1, 1])

time: 688 us -> 667 us (0.969)
  Pallas kernels: 510 us -> 484 us
  waiting for transfers between devices: 68 us -> 78.4 us
    pallas_call x1, Pallas kernels: 81.7 us -> 50 us  [gather_layer(): pl.pallas_call(functools.partial(gather_layer_kernel, chips=chips, depth=...]
    ppermute x34, waiting for transfers between devices: 67.2 us -> 78.3 us  [swap(): return lax.ppermute(value, 'fsdp', [(i, i ^ distance) for i in range(size)])]
  transfers between devices with their start and end apart: 38 -> 38, of which waited for: 10 -> 12; matrix products, arithmetic and copies ran while one was open for 7% -> 7% of each run, Pallas kernels for 68% -> 67%
where the time goes in v6:
time: 667 us; the launch traced here: 663 us
  Pallas kernels  484 us (73%)
  waiting for transfers between devices  78.4 us (12%)
  other arithmetic  31.2 us (5%)
  local copies, waits for them, and re-layouts  28.8 us (4%)
  starting transfers between devices  26.3 us (4%)
  between operations  14.3 us (2%)
    pallas_call x4, Pallas kernels, experts_step(): pl.pallas_call(functools.partial(expert_kernel, chunk=rows // 3, tile=256...  141 us
    ppermute x34, waiting for transfers between devices, swap(): return lax.ppermute(value, 'fsdp', [(i, i ^ distance) for i in range(size)])  78.3 us
    pallas_call x2, Pallas kernels, attention_backward(): pl.pallas_call(functools.partial(attention_backward_kernel, terms=len(ter...  76.4 us
    pallas_call x8, Pallas kernels, combine(): pl.pallas_call(functools.partial(combine_kernel, groups=groups, local=loc...  67.9 us
    pallas_call x1, Pallas kernels, reduce_layer(): pl.pallas_call(functools.partial(reduce_layer_kernel, chips=chips, depth=...  61.3 us
    pallas_call x1, Pallas kernels, gather_layer(): pl.pallas_call(functools.partial(gather_layer_kernel, chips=chips, depth=...  50 us
    pallas_call x2, Pallas kernels, attention_forward(): pl.pallas_call(functools.partial(attention_forward_kernel, q_width=q_widt...  43.6 us
    pallas_call x4, Pallas kernels, dispatch(): pl.pallas_call(functools.partial(dispatch_kernel, local=local), out_shape...  43.6 us
  transfers between devices with their start and end apart: 38, of which 12 were waited for; matrix products, arithmetic and copies ran while one was open for 7% of the time, Pallas kernels for 67%

profile of v6, /device:TPU:0, one launch (start us, length us, event | category | flops | bytes accessed | tf_op | source)
XLA Modules:
  0.0 663.1 jit_solution(13805047941574679595)
XLA Ops:
  12.3 50.0 %gather_layer.1.w_ref.refs_1_ = bf16[1024,3200]{1,0:T(8,128)(2,1)} custom-call(bf16[32,3200]{1,0:T(8,128)(2,1)} %concatenate.15.w_ref), custom_call_target="tpu_custom_call" | custom-call | tf_op jit(solution)/shard_map/gather_layer/pallas_call | solution.py:754
  73.4 21.9 %attention_forward.2 = (bf16[512,1024]{1,0:T(8,128)(2,1)}, bf16[512,512]{1,0:T(8,128)(2,1)}, bf16[512,512]{1,0:T(8,128)(2,1)}, bf16[512,1024]{1,0:T(8,128)(2,1)}...) custom-call(bf16[512,1024]{1,0:T(8,128)(2,1)} %get-tuple-element.263.x_ref.refs_0_, ...), custom_call_target="tpu_custom_call" | custom-call | flops 7516192768 | bytes 67108864 | tf_op jit(solution)/shard_map/attention_forward/pallas_call | solution.py:179
  97.9 15.6 %collective-permute-done.1 = bf16[512,1024]{1,0:T(8,128)(2,1)} collective-permute-done((bf16[512,1024]{1,0:T(8,128)(2,1)}, bf16[512,1024]{1,0:T(8,128)(2,1)}, u32[]{:S(2)}, u32[]{:S(2)}) %collective-permute-start.1) | collective-permute-done | bytes 1048608 | tf_op jit(solution)/shard_map/ppermute | solution.py:880
  113.6 21.7 %attention_forward.3 = (bf16[512,1024]{1,0:T(8,128)(2,1)}, bf16[512,512]{1,0:T(8,128)(2,1)}, bf16[512,512]{1,0:T(8,128)(2,1)}, bf16[512,1024]{1,0:T(8,128)(2,1)}...) custom-call(bf16[512,1024]{1,0:T(8,128)(2,1)} %get-tuple-element.116.x_ref.refs_0_, ...), custom_call_target="tpu_custom_call" | custom-call | flops 7516192768 | bytes 67108864 | tf_op jit(solution)/shard_map/attention_forward/pallas_call | solution.py:179
  143.0 8.2 %collective-permute-done.4 = bf16[272,1024]{1,0:T(8,128)(2,1)S(1)} collective-permute-done((bf16[272,1024]{1,0:T(8,128)(2,1)S(1)}, bf16[272,1024]{1,0:T(8,128)(2,1)S(1)}, u32[]{:S(2)}, u32[]{:S(2)}) %collective-permute-start.4) | collective-permute-done | bytes 557088 | tf_op jit(solution)/shard_map/ppermute | solution.py:880
  160.0 11.0 %dispatch.4 = (bf16[4,2,4,144,1024]{4,3,2,1,0:T(8,128)(2,1)}, bf16[4,2,4,144,1024]{4,3,2,1,0:T(8,128)(2,1)}) custom-call(bf16[8,32]{1,0:T(8,128)(2,1)} %fusion.1.sel_ref, bf16[4,544,1024]{2,1,0:T(8,128)(2,1)} %pad_maximum_fusion.pay_ref, bf16[4,512,1024]{2,1,0:T(8,128)(2,1)} %pad_maximum_fusion.2.grad_ref), custom_call_target="tpu_custom_call" | custom-call | flops 18874368 | bytes 81920 | tf_op jit(solution)/shard_map/dispatch/pallas_call | solution.py:250
  171.0 11.0 %collective-permute-done.8 = bf16[512,1024]{1,0:T(8,128)(2,1)} collective-permute-done((bf16[512,1024]{1,0:T(8,128)(2,1)}, bf16[512,1024]{1,0:T(8,128)(2,1)}, u32[]{:S(2)}, u32[]{:S(2)}) %collective-permute-start.8) | collective-permute-done | bytes 1048608 | tf_op jit(solution)/shard_map/ppermute | solution.py:880
  192.0 10.8 %dispatch.5 = (bf16[4,2,4,144,1024]{4,3,2,1,0:T(8,128)(2,1)}, bf16[4,2,4,144,1024]{4,3,2,1,0:T(8,128)(2,1)}) custom-call(bf16[8,32]{1,0:T(8,128)(2,1)} %fusion.1.sel_ref, bf16[4,544,1024]{2,1,0:T(8,128)(2,1)} %collective-permute-done.10.pay_ref, ...), custom_call_target="tpu_custom_call", output_to_operand_aliasing={{0}: (3, {}), {1}: (4, {})} | custom-call | flops 18874368 | bytes 81920 | tf_op jit(solution)/shard_map/dispatch/pallas_call | solution.py:250
  202.9 34.7 %experts.4 = (bf16[2,1152,1024]{2,1,0:T(8,128)(2,1)}, bf16[2,1152,1024]{2,1,0:T(8,128)(2,1)}, f32[2,1152,1]{2,1,0:T(8,128)}, bf16[4,2,768,512]{3,2,1,0:T(8,128)(2,1)}) custom-call(bf16[4,1152,1024]{2,1,0:T(8,128)(2,1)} %bitcast.78, bf16[4,1152,1024]{2,1,0:T(8,128)(2,1)} %bitcast.80, bf16[4,2,768,512]{3,2,1,0:T(8,128)(2,1)} %bitcast.137), custom_call_target="tpu_custom_call" | custom-call | flops 84934656 | bytes 122880 | tf_op jit(solution)/shard_map/experts/pallas_call | solution.py:391
  253.7 10.8 %dispatch.6 = (bf16[4,2,4,144,1024]{4,3,2,1,0:T(8,128)(2,1)}, bf16[4,2,4,144,1024]{4,3,2,1,0:T(8,128)(2,1)}) custom-call(bf16[8,32]{1,0:T(8,128)(2,1)} %fusion.1.sel_ref, bf16[4,544,1024]{2,1,0:T(8,128)(2,1)} %pad_maximum_fusion.1.pay_ref, bf16[4,512,1024]{2,1,0:T(8,128)(2,1)} %pad_maximum_fusion.3.grad_ref), custom_call_target="tpu_custom_call" | custom-call | flops 18874368 | bytes 81920 | tf_op jit(solution)/shard_map/dispatch/pallas_call | solution.py:250
  264.5 35.2 %experts.5 = (bf16[2,1152,1024]{2,1,0:T(8,128)(2,1)}, bf16[2,1152,1024]{2,1,0:T(8,128)(2,1)}, f32[2,1152,1]{2,1,0:T(8,128)}, bf16[4,2,768,512]{3,2,1,0:T(8,128)(2,1)}) custom-call(bf16[4,1152,1024]{2,1,0:T(8,128)(2,1)} %bitcast.79, bf16[4,1152,1024]{2,1,0:T(8,128)(2,1)} %bitcast.81, bf16[4,2,768,512]{3,2,1,0:T(8,128)(2,1)} %bitcast.135), custom_call_target="tpu_custom_call" | custom-call | flops 84934656 | bytes 122880 | tf_op jit(solution)/shard_map/experts/pallas_call | solution.py:391
  315.7 9.5 %combine.10 = (bf16[528,1024]{1,0:T(8,128)(2,1)}, bf16[528,1024]{1,0:T(8,128)(2,1)}, bf16[528,1024]{1,0:T(8,128)(2,1)}, bf16[528,1024]{1,0:T(8,128)(2,1)}) custom-call(bf16[8,32]{1,0:T(8,128)(2,1)} %fusion.1.sel_ref, bf16[4,544,1024]{2,1,0:T(8,128)(2,1)} %pad_maximum_fusion.pay_ref, bf16[2,8,144,1024]{3,2,1,0:T(8,128)(2,1)} %bitcast.92, ...), custom_call_target="tpu_custom_call" | custom-call | flops 2415919104 | bytes 20971520 | tf_op jit(solution)/shard_map/combine/pallas_call | solution.py:491
  326.8 9.4 %combine.11 = (bf16[528,1024]{1,0:T(8,128)(2,1)}, bf16[528,1024]{1,0:T(8,128)(2,1)}, bf16[528,1024]{1,0:T(8,128)(2,1)}, bf16[528,1024]{1,0:T(8,128)(2,1)}) custom-call(bf16[8,32]{1,0:T(8,128)(2,1)} %fusion.1.sel_ref, bf16[4,544,1024]{2,1,0:T(8,128)(2,1)} %pad_maximum_fusion.pay_ref, bf16[2,8,144,1024]{3,2,1,0:T(8,128)(2,1)} %bitcast.93, ...), custom_call_target="tpu_custom_call" | custom-call | flops 2415919104 | bytes 20971520 | tf_op jit(solution)/shard_map/combine/pallas_call | solution.py:491
  336.3 11.0 %dispatch.7 = (bf16[4,2,4,144,1024]{4,3,2,1,0:T(8,128)(2,1)}, bf16[4,2,4,144,1024]{4,3,2,1,0:T(8,128)(2,1)}) custom-call(bf16[8,32]{1,0:T(8,128)(2,1)} %fusion.1.sel_ref, bf16[4,544,1024]{2,1,0:T(8,128)(2,1)} %collective-permute-done.16.pay_ref, ...), custom_call_target="tpu_custom_call", output_to_operand_aliasing={{0}: (3, {}), {1}: (4, {})} | custom-call | flops 18874368 | bytes 81920 | tf_op jit(solution)/shard_map/dispatch/pallas_call | solution.py:250
  347.3 35.7 %experts.6 = (bf16[2,1152,1024]{2,1,0:T(8,128)(2,1)}, bf16[2,1152,1024]{2,1,0:T(8,128)(2,1)}, f32[2,1152,1]{2,1,0:T(8,128)}, bf16[4,2,768,512]{3,2,1,0:T(8,128)(2,1)}) custom-call(bf16[4,1152,1024]{2,1,0:T(8,128)(2,1)} %bitcast.130, bf16[4,1152,1024]{2,1,0:T(8,128)(2,1)} %bitcast.132, bf16[4,2,768,512]{3,2,1,0:T(8,128)(2,1)} %bitcast.138, ...), custom_call_target="tpu_custom_call" | custom-call | flops 21743271936 | bytes 31457280 | tf_op jit(solution)/shard_map/experts/pallas_call | solution.py:391
  392.9 35.6 %experts.7 = (bf16[2,1152,1024]{2,1,0:T(8,128)(2,1)}, bf16[2,1152,1024]{2,1,0:T(8,128)(2,1)}, f32[2,1152,1]{2,1,0:T(8,128)}, bf16[4,2,768,512]{3,2,1,0:T(8,128)(2,1)}) custom-call(bf16[4,1152,1024]{2,1,0:T(8,128)(2,1)} %bitcast.131, bf16[4,1152,1024]{2,1,0:T(8,128)(2,1)} %bitcast.133, bf16[4,2,768,512]{3,2,1,0:T(8,128)(2,1)} %bitcast.136, ...), custom_call_target="tpu_custom_call" | custom-call | flops 21743271936 | bytes 31457280 | tf_op jit(solution)/shard_map/experts/pallas_call | solution.py:391
  428.5 7.6 %combine.12 = bf16[2,1056,1024]{2,1,0:T(8,128)(2,1)} custom-call(bf16[8,32]{1,0:T(8,128)(2,1)} %fusion.1.sel_ref, bf16[4,544,1024]{2,1,0:T(8,128)(2,1)} %collective-permute-done.16.pay_ref, bf16[2,8,144,1024]{3,2,1,0:T(8,128)(2,1)} %bitcast.82, bf16[2,8,144,1024]{3,2,1,0:T(8,128)(2,1)} %bitcast.98, bf16[2,8,144,1024]{3,2,1,0:T(8,128)(2,1)} %bitcast.86, ...), custom_call_target="tpu_custom_call" | custom-call | flops 2415919104 | bytes 20971520 | tf_op jit(solution)/shard_map/combine/pallas_call | solution.py:491
  438.7 7.5 %combine.13 = bf16[2,1056,1024]{2,1,0:T(8,128)(2,1)} custom-call(bf16[8,32]{1,0:T(8,128)(2,1)} %fusion.1.sel_ref, bf16[4,544,1024]{2,1,0:T(8,128)(2,1)} %collective-permute-done.16.pay_ref, bf16[2,8,144,1024]{3,2,1,0:T(8,128)(2,1)} %bitcast.83, bf16[2,8,144,1024]{3,2,1,0:T(8,128)(2,1)} %bitcast.99, bf16[2,8,144,1024]{3,2,1,0:T(8,128)(2,1)} %bitcast.87, ...), custom_call_target="tpu_custom_call" | custom-call | flops 2415919104 | bytes 20971520 | tf_op jit(solution)/shard_map/combine/pallas_call | solution.py:491
  446.3 9.4 %combine.14 = (bf16[528,1024]{1,0:T(8,128)(2,1)}, bf16[528,1024]{1,0:T(8,128)(2,1)}, bf16[528,1024]{1,0:T(8,128)(2,1)}, bf16[528,1024]{1,0:T(8,128)(2,1)}) custom-call(bf16[8,32]{1,0:T(8,128)(2,1)} %fusion.1.sel_ref, bf16[4,544,1024]{2,1,0:T(8,128)(2,1)} %pad_maximum_fusion.1.pay_ref, bf16[2,8,144,1024]{3,2,1,0:T(8,128)(2,1)} %bitcast.84, ...), custom_call_target="tpu_custom_call" | custom-call | flops 2415919104 | bytes 20971520 | tf_op jit(solution)/shard_map/combine/pallas_call | solution.py:491
  455.7 9.6 %combine.15 = (bf16[528,1024]{1,0:T(8,128)(2,1)}, bf16[528,1024]{1,0:T(8,128)(2,1)}, bf16[528,1024]{1,0:T(8,128)(2,1)}, bf16[528,1024]{1,0:T(8,128)(2,1)}) custom-call(bf16[8,32]{1,0:T(8,128)(2,1)} %fusion.1.sel_ref, bf16[4,544,1024]{2,1,0:T(8,128)(2,1)} %pad_maximum_fusion.1.pay_ref, bf16[2,8,144,1024]{3,2,1,0:T(8,128)(2,1)} %bitcast.85, ...), custom_call_target="tpu_custom_call" | custom-call | flops 2415919104 | bytes 20971520 | tf_op jit(solution)/shard_map/combine/pallas_call | solution.py:491
  469.4 37.3 %attention_backward.2 = (bf16[2,512,1024]{2,1,0:T(8,128)(2,1)}, f32[2,512,1024]{2,1,0:T(8,128)}, bf16[1024,3200]{1,0:T(8,128)(2,1)}) custom-call(bf16[512,1024]{1,0:T(8,128)(2,1)} %get-tuple-element.263.x_ref.refs_0_, bf16[1024,3200]{1,0:T(8,128)(2,1)} %gather_layer.1.w_ref.refs_1_, f32[1,1024]{1,0:T(1,128)} %bitcast.154, f32[1,1024]{1,0:T(1,128)} %bitcast.150, ...), custom_call_target="tpu_custom_call" | custom-call | flops 17179869184 | bytes 41943040 | tf_op jit(solution)/shard_map/attention_backward/pallas_call | solution.py:643
  518.3 19.9 %collective-permute-done.32.refs_21_ = bf16[528,1024]{1,0:T(8,128)(2,1)S(1)} collective-permute-done((bf16[528,1024]{1,0:T(8,128)(2,1)S(1)}, bf16[528,1024]{1,0:T(8,128)(2,1)S(1)}, u32[]{:S(2)}, u32[]{:S(2)}) %collective-permute-start.32) | collective-permute-done | bytes 1081376 | tf_op jit(solution)/shard_map/ppermute | solution.py:880
  543.5 39.1 %attention_backward.3 = (bf16[2,512,1024]{2,1,0:T(8,128)(2,1)}, f32[2,512,1024]{2,1,0:T(8,128)}, bf16[1024,3200]{1,0:T(8,128)(2,1)}) custom-call(bf16[512,1024]{1,0:T(8,128)(2,1)} %get-tuple-element.116.x_ref.refs_0_, bf16[1024,3200]{1,0:T(8,128)(2,1)} %gather_layer.1.w_ref.refs_1_, ...), custom_call_target="tpu_custom_call", output_to_operand_aliasing={{0}: (24, {}), {1}: (25, {})} | custom-call | flops 17179869184 | bytes 41943040 | tf_op jit(solution)/shard_map/attention_backward/pallas_call | solution.py:643
  582.5 61.3 %reduce_layer.1 = f32[32,3200]{1,0:T(8,128)} custom-call(bf16[1024,3200]{1,0:T(8,128)(2,1)} %get-tuple-element.211.pack_ref), custom_call_target="tpu_custom_call" | custom-call | bytes 1073741824 | tf_op jit(solution)/shard_map/reduce_layer/pallas_call | solution.py:857
  (156 shorter events, 125.0 us)
Async XLA Ops:
  7.2 195.7 %all-gather.5.cloned.1.call-start = ((), (), s32[]{:S(2)}) async-start(), calls=%async_computation.4 | async-start | bytes 7864320 | tf_op jit(solution)/shard_map/all_gather | solution.py:959
  11.2 253.2 %all-gather.7.cloned.1.call-start = ((), (), s32[]{:S(2)}) async-start(), calls=%async_computation.5 | async-start | bytes 7864320 | tf_op jit(solution)/shard_map/all_gather | solution.py:959
  64.7 48.8 %collective-permute-start.1 = (bf16[512,1024]{1,0:T(8,128)(2,1)}, bf16[512,1024]{1,0:T(8,128)(2,1)}, u32[]{:S(2)}, u32[]{:S(2)}) collective-permute-start(bf16[512,1024]{1,0:T(8,128)(2,1)} %get-tuple-element.115.refs_8_), channel_id=1, source_target_pairs={{0,16},{4,20},{8,24},{12,28},{16,0},{20,4},{24,8},{28,12},{1,17},{... | collective-permute-start | bytes 3145736 | tf_op jit(solution)/shard_map/ppermute | solution.py:880
  64.7 48.8 %collective-permute-start.2 = (bf16[512,1024]{1,0:T(8,128)(2,1)}, bf16[512,1024]{1,0:T(8,128)(2,1)}, u32[]{:S(2)}, u32[]{:S(2)}) collective-permute-start(bf16[512,1024]{1,0:T(8,128)(2,1)} %get-tuple-element.115.refs_8_), channel_id=1, source_target_pairs={{0,24},{4,28},{8,16},{12,20},{16,8},{20,12},{24,0},{28,4},{1,25},{... | collective-permute-start | bytes 3145736 | tf_op jit(solution)/shard_map/ppermute | solution.py:880
  67.4 582.5 %reduce-scatter.3.cloned.1.call-start = ((), (), s32[]{:S(2)}) async-start(), calls=%async_computation.2 | async-start | bytes 7864320 | tf_op jit(solution)/shard_map/reduce_scatter | solution.py:1080
  95.3 40.6 %collective-permute-start.3 = (bf16[544,1024]{1,0:T(8,128)(2,1)}, bf16[544,1024]{1,0:T(8,128)(2,1)}, u32[]{:S(2)}, u32[]{:S(2)}) collective-permute-start(bf16[544,1024]{1,0:T(8,128)(2,1)} %get-tuple-element.126.refs_15_), channel_id=1, source_target_pairs={{0,8},{4,12},{8,0},{12,4},{16,24},{20,28},{24,16},{28,20},{1,9},{5... | collective-permute-start | bytes 3342344 | tf_op jit(solution)/shard_map/ppermute | solution.py:880
  96.2 40.9 %collective-permute-start.5 = (bf16[544,1024]{1,0:T(8,128)(2,1)}, bf16[544,1024]{1,0:T(8,128)(2,1)}, u32[]{:S(2)}, u32[]{:S(2)}) collective-permute-start(bf16[544,1024]{1,0:T(8,128)(2,1)} %get-tuple-element.126.refs_15_), channel_id=1, source_target_pairs={{0,16},{4,20},{8,24},{12,28},{16,0},{20,4},{24,8},{28,12},{1,17},{... | collective-permute-start | bytes 3342344 | tf_op jit(solution)/shard_map/ppermute | solution.py:880
  156.2 34.9 %collective-permute-start.10 = (bf16[4,544,1024]{2,1,0:T(8,128)(2,1)}, bf16[4,544,1024]{2,1,0:T(8,128)(2,1)}, u32[]{:S(2)}, u32[]{:S(2)}) collective-permute-start(bf16[4,544,1024]{2,1,0:T(8,128)(2,1)} %pad_maximum_fusion.pay_ref), channel_id=1, source_target_pairs={{0,4},{4,0},{8,12},{12,8},{16,20},{20,16},{24,28},{28,24},{1,5},{5... | collective-permute-start | bytes 13369352 | tf_op jit(solution)/shard_map/ppermute | solution.py:880
  183.5 66.4 %collective-permute-start.9 = (bf16[544,1024]{1,0:T(8,128)(2,1)}, bf16[544,1024]{1,0:T(8,128)(2,1)}, u32[]{:S(2)}, u32[]{:S(2)}) collective-permute-start(bf16[544,1024]{1,0:T(8,128)(2,1)} %get-tuple-element.137.refs_15_), channel_id=1, source_target_pairs={{0,8},{4,12},{8,0},{12,4},{16,24},{20,28},{24,16},{28,20},{1,9},{5... | collective-permute-start | bytes 3342344 | tf_op jit(solution)/shard_map/ppermute | solution.py:880
  184.4 65.5 %collective-permute-start.14 = (bf16[544,1024]{1,0:T(8,128)(2,1)}, bf16[544,1024]{1,0:T(8,128)(2,1)}, u32[]{:S(2)}, u32[]{:S(2)}) collective-permute-start(bf16[544,1024]{1,0:T(8,128)(2,1)} %get-tuple-element.137.refs_15_), channel_id=1, source_target_pairs={{0,16},{4,20},{8,24},{12,28},{16,0},{20,4},{24,8},{28,12},{1,17},{... | collective-permute-start | bytes 3342344 | tf_op jit(solution)/shard_map/ppermute | solution.py:880
  184.8 65.2 %collective-permute-start.15 = (bf16[544,1024]{1,0:T(8,128)(2,1)}, bf16[544,1024]{1,0:T(8,128)(2,1)}, u32[]{:S(2)}, u32[]{:S(2)}) collective-permute-start(bf16[544,1024]{1,0:T(8,128)(2,1)} %get-tuple-element.137.refs_15_), channel_id=1, source_target_pairs={{0,24},{4,28},{8,16},{12,20},{16,8},{20,12},{24,0},{28,4},{1,25},{... | collective-permute-start | bytes 3342344 | tf_op jit(solution)/shard_map/ppermute | solution.py:880
  188.9 56.0 %collective-permute-start.12 = (bf16[256,1024]{1,0:T(8,128)(2,1)}, bf16[256,1024]{1,0:T(8,128)(2,1)}, u32[]{:S(2)}, u32[]{:S(2)}) collective-permute-start(bf16[256,1024]{1,0:T(8,128)(2,1)} %slice.97), channel_id=1, source_target_pairs={{0,16},{4,20},{8,24},{12,28},{16,0},{20,4},{24,8},{28,12},{1,17},{... | collective-permute-start | bytes 1572872 | tf_op jit(solution)/shard_map/ppermute | solution.py:880
  191.0 53.9 %collective-permute-start.13 = (bf16[256,1024]{1,0:T(8,128)(2,1)}, bf16[256,1024]{1,0:T(8,128)(2,1)}, u32[]{:S(2)}, u32[]{:S(2)}) collective-permute-start(bf16[256,1024]{1,0:T(8,128)(2,1)} %slice.98), channel_id=1, source_target_pairs={{0,8},{4,12},{8,0},{12,4},{16,24},{20,28},{24,16},{28,20},{1,9},{5... | collective-permute-start | bytes 1572872 | tf_op jit(solution)/shard_map/ppermute | solution.py:880
  325.2 57.7 %collective-permute-start.21 = (bf16[528,1024]{1,0:T(8,128)(2,1)}, bf16[528,1024]{1,0:T(8,128)(2,1)}, u32[]{:S(2)}, u32[]{:S(2)}) collective-permute-start(bf16[528,1024]{1,0:T(8,128)(2,1)} %get-tuple-element.173), channel_id=1, source_target_pairs={{0,8},{4,12},{8,0},{12,4},{16,24},{20,28},{24,16},{28,20},{1,9},{5... | collective-permute-start | bytes 3244040 | tf_op jit(solution)/shard_map/ppermute | solution.py:880
  326.2 59.8 %collective-permute-start.20 = (bf16[528,1024]{1,0:T(8,128)(2,1)}, bf16[528,1024]{1,0:T(8,128)(2,1)}, u32[]{:S(2)}, u32[]{:S(2)}) collective-permute-start(bf16[528,1024]{1,0:T(8,128)(2,1)} %get-tuple-element.162), channel_id=1, source_target_pairs={{0,16},{4,20},{8,24},{12,28},{16,0},{20,4},{24,8},{28,12},{1,17},{... | collective-permute-start | bytes 3244040 | tf_op jit(solution)/shard_map/ppermute | solution.py:880
  388.7 261.2 %reduce-scatter.5.cloned.1.call-start = ((), (), s32[]{:S(2)}) async-start(), calls=%async_computation.3 | async-start | bytes 7864320 | tf_op jit(solution)/shard_map/reduce_scatter | solution.py:1080
  388.7 50.0 %collective-permute-start.23 = (bf16[528,1024]{1,0:T(8,128)(2,1)}, bf16[528,1024]{1,0:T(8,128)(2,1)}, u32[]{:S(2)}, u32[]{:S(2)}) collective-permute-start(bf16[528,1024]{1,0:T(8,128)(2,1)} %add_convert_fusion.2), channel_id=1, source_target_pairs={{0,16},{4,20},{8,24},{12,28},{16,0},{20,4},{24,8},{28,12},{1,17},{... | collective-permute-start | bytes 3244040 | tf_op jit(solution)/shard_map/ppermute | solution.py:880
  390.2 48.5 %collective-permute-start.22 = (bf16[528,1024]{1,0:T(8,128)(2,1)}, bf16[528,1024]{1,0:T(8,128)(2,1)}, u32[]{:S(2)}, u32[]{:S(2)}) collective-permute-start(bf16[528,1024]{1,0:T(8,128)(2,1)} %add_convert_fusion.3), channel_id=1, source_target_pairs={{0,8},{4,12},{8,0},{12,4},{16,24},{20,28},{24,16},{28,20},{1,9},{5... | collective-permute-start | bytes 3244040 | tf_op jit(solution)/shard_map/ppermute | solution.py:880
  391.2 46.4 %collective-permute-start.25 = (bf16[528,1024]{1,0:T(8,128)(2,1)}, bf16[528,1024]{1,0:T(8,128)(2,1)}, u32[]{:S(2)}, u32[]{:S(2)}) collective-permute-start(bf16[528,1024]{1,0:T(8,128)(2,1)} %get-tuple-element.184), channel_id=1, source_target_pairs={{0,16},{4,20},{8,24},{12,28},{16,0},{20,4},{24,8},{28,12},{1,17},{... | collective-permute-start | bytes 3244040 | tf_op jit(solution)/shard_map/ppermute | solution.py:880
  391.8 47.0 %collective-permute-start.24 = (bf16[528,1024]{1,0:T(8,128)(2,1)}, bf16[528,1024]{1,0:T(8,128)(2,1)}, u32[]{:S(2)}, u32[]{:S(2)}) collective-permute-start(bf16[528,1024]{1,0:T(8,128)(2,1)} %get-tuple-element.182), channel_id=1, source_target_pairs={{0,8},{4,12},{8,0},{12,4},{16,24},{20,28},{24,16},{28,20},{1,9},{5... | collective-permute-start | bytes 3244040 | tf_op jit(solution)/shard_map/ppermute | solution.py:880
  465.3 44.2 %collective-permute-start.29 = (bf16[528,1024]{1,0:T(8,128)(2,1)}, bf16[528,1024]{1,0:T(8,128)(2,1)}, u32[]{:S(2)}, u32[]{:S(2)}) collective-permute-start(bf16[528,1024]{1,0:T(8,128)(2,1)} %get-tuple-element.193), channel_id=1, source_target_pairs={{0,16},{4,20},{8,24},{12,28},{16,0},{20,4},{24,8},{28,12},{1,17},{... | collective-permute-start | bytes 3244040 | tf_op jit(solution)/shard_map/ppermute | solution.py:880
  465.9 40.8 %collective-permute-start.31 = (bf16[528,1024]{1,0:T(8,128)(2,1)}, bf16[528,1024]{1,0:T(8,128)(2,1)}, u32[]{:S(2)}, u32[]{:S(2)}) collective-permute-start(bf16[528,1024]{1,0:T(8,128)(2,1)} %get-tuple-element.204), channel_id=1, source_target_pairs={{0,8},{4,12},{8,0},{12,4},{16,24},{20,28},{24,16},{28,20},{1,9},{5... | collective-permute-start | bytes 3244040 | tf_op jit(solution)/shard_map/ppermute | solution.py:880
  466.9 51.4 %collective-permute-start.33 = (bf16[528,1024]{1,0:T(8,128)(2,1)}, bf16[528,1024]{1,0:T(8,128)(2,1)}, u32[]{:S(2)}, u32[]{:S(2)}) collective-permute-start(bf16[528,1024]{1,0:T(8,128)(2,1)} %get-tuple-element.206), channel_id=1, source_target_pairs={{0,16},{4,20},{8,24},{12,28},{16,0},{20,4},{24,8},{28,12},{1,17},{... | collective-permute-start | bytes 3244040 | tf_op jit(solution)/shard_map/ppermute | solution.py:880
  468.3 47.0 %collective-permute-start.28 = (bf16[528,1024]{1,0:T(8,128)(2,1)}, bf16[528,1024]{1,0:T(8,128)(2,1)}, u32[]{:S(2)}, u32[]{:S(2)}) collective-permute-start(bf16[528,1024]{1,0:T(8,128)(2,1)} %get-tuple-element.191), channel_id=1, source_target_pairs={{0,8},{4,12},{8,0},{12,4},{16,24},{20,28},{24,16},{28,20},{1,9},{5... | collective-permute-start | bytes 3244040 | tf_op jit(solution)/shard_map/ppermute | solution.py:880
  (33 other events, 401.0 us)
Sparse Core Ops, SparseCore 0:
  11.4 127.4 all-gather.4
  141.0 114.5 all-gather.6
  388.8 116.7 reduce-scatter.2
  507.8 113.8 reduce-scatter.4

commit v7 on v6

--- a/solution.py
+++ b/solution.py
@@ -917,7 +917,7 @@
     if size != 8:
         return (), ()
     add = lambda a, b: (a.astype(F32) + b.astype(F32)).astype(BF)
-    by_one, by_two = after(near[0], *earlier), after(near[1], *earlier, *rest[:1])
+    by_one, by_two = after(near[0], *earlier, *rest[1:]), after(near[1], *earlier, *rest[:1])
     one_sum, two_sum = add(kept[3], by_two), add(kept[4], by_one)
     return (one_sum, two_sum), (swap(one_sum, 2, size), swap(two_sum, 4, size))
 
@@ -1071,12 +1071,12 @@
     for m in range(micro - 1):
         made, prior = backward(m, [after(terms[m][0], kept[0], kept[-1])] + terms[m][1:], made, prior)
         held_back = (prior,)
-    last_far = scatter_far(kept, near, owners, *held_back, rest=last_rest)[1]
+    last_added, last_far = scatter_far(kept, near, owners, *held_back, rest=last_rest)
     terms.append(scattered(kept, near, last_far, last_rest))
     made, prior = backward(micro - 1, terms[-1], made, prior)
     sums = []
     for g in range(len(weights)):
-        summed = after(done[micro - 1, g][3], *((kept[0], kept[-1]) if g else added))
+        summed = after(done[micro - 1, g][3], *(last_added if g else added))
         sums.append(lax.psum_scatter(summed, "dp", scatter_dimension=0, tiled=True)[0])
     layer = reduce_layer(prior, chips, depth, 5)
     marks = np.cumsum([0, q_width, kv_width, kv_width, width, experts, 1, 1])

time: 667 us -> 667 us (level)
  transfers between devices with their start and end apart: 38 -> 38, of which waited for: 12 -> 11; matrix products, arithmetic and copies ran while one was open for 7% -> 7% of each run, Pallas kernels for 67% -> 67%
where the time goes in v7:
time: 667 us; the launch traced here: 663 us
  Pallas kernels  490 us (73%)
  waiting for transfers between devices  72.2 us (11%)
  other arithmetic  31.1 us (5%)
  local copies, waits for them, and re-layouts  29.5 us (4%)
  starting transfers between devices  26 us (4%)
  between operations  14.4 us (2%)
    pallas_call x4, Pallas kernels, experts_step(): pl.pallas_call(functools.partial(expert_kernel, chunk=rows // 3, tile=256...  141 us
    pallas_call x2, Pallas kernels, attention_backward(): pl.pallas_call(functools.partial(attention_backward_kernel, terms=len(ter...  76.5 us
    ppermute x34, waiting for transfers between devices, swap(): return lax.ppermute(value, 'fsdp', [(i, i ^ distance) for i in range(size)])  72.1 us
    pallas_call x8, Pallas kernels, combine(): pl.pallas_call(functools.partial(combine_kernel, groups=groups, local=loc...  68 us
    pallas_call x1, Pallas kernels, reduce_layer(): pl.pallas_call(functools.partial(reduce_layer_kernel, chips=chips, depth=...  66.6 us
    pallas_call x1, Pallas kernels, gather_layer(): pl.pallas_call(functools.partial(gather_layer_kernel, chips=chips, depth=...  50 us
    pallas_call x2, Pallas kernels, attention_forward(): pl.pallas_call(functools.partial(attention_forward_kernel, q_width=q_widt...  43.6 us
    pallas_call x4, Pallas kernels, dispatch(): pl.pallas_call(functools.partial(dispatch_kernel, local=local), out_shape...  43.6 us
  transfers between devices with their start and end apart: 38, of which 11 were waited for; matrix products, arithmetic and copies ran while one was open for 7% of the time, Pallas kernels for 67%

profile of v7, /device:TPU:0, one launch (start us, length us, event | category | flops | bytes accessed | tf_op | source)
XLA Modules:
  0.0 662.7 jit_solution(10147574512314883829)
XLA Ops:
  12.3 50.0 %gather_layer.1.w_ref.refs_1_ = bf16[1024,3200]{1,0:T(8,128)(2,1)} custom-call(bf16[32,3200]{1,0:T(8,128)(2,1)} %concatenate.15.w_ref), custom_call_target="tpu_custom_call" | custom-call | tf_op jit(solution)/shard_map/gather_layer/pallas_call | solution.py:754
  73.4 21.9 %attention_forward.2 = (bf16[512,1024]{1,0:T(8,128)(2,1)}, bf16[512,512]{1,0:T(8,128)(2,1)}, bf16[512,512]{1,0:T(8,128)(2,1)}, bf16[512,1024]{1,0:T(8,128)(2,1)}...) custom-call(bf16[512,1024]{1,0:T(8,128)(2,1)} %get-tuple-element.263.x_ref.refs_0_, ...), custom_call_target="tpu_custom_call" | custom-call | flops 7516192768 | bytes 67108864 | tf_op jit(solution)/shard_map/attention_forward/pallas_call | solution.py:179
  97.9 15.6 %collective-permute-done.1 = bf16[512,1024]{1,0:T(8,128)(2,1)} collective-permute-done((bf16[512,1024]{1,0:T(8,128)(2,1)}, bf16[512,1024]{1,0:T(8,128)(2,1)}, u32[]{:S(2)}, u32[]{:S(2)}) %collective-permute-start.1) | collective-permute-done | bytes 1048608 | tf_op jit(solution)/shard_map/ppermute | solution.py:880
  113.6 21.7 %attention_forward.3 = (bf16[512,1024]{1,0:T(8,128)(2,1)}, bf16[512,512]{1,0:T(8,128)(2,1)}, bf16[512,512]{1,0:T(8,128)(2,1)}, bf16[512,1024]{1,0:T(8,128)(2,1)}...) custom-call(bf16[512,1024]{1,0:T(8,128)(2,1)} %get-tuple-element.116.x_ref.refs_0_, ...), custom_call_target="tpu_custom_call" | custom-call | flops 7516192768 | bytes 67108864 | tf_op jit(solution)/shard_map/attention_forward/pallas_call | solution.py:179
  143.0 8.2 %collective-permute-done.4 = bf16[272,1024]{1,0:T(8,128)(2,1)S(1)} collective-permute-done((bf16[272,1024]{1,0:T(8,128)(2,1)S(1)}, bf16[272,1024]{1,0:T(8,128)(2,1)S(1)}, u32[]{:S(2)}, u32[]{:S(2)}) %collective-permute-start.4) | collective-permute-done | bytes 557088 | tf_op jit(solution)/shard_map/ppermute | solution.py:880
  160.0 11.0 %dispatch.4 = (bf16[4,2,4,144,1024]{4,3,2,1,0:T(8,128)(2,1)}, bf16[4,2,4,144,1024]{4,3,2,1,0:T(8,128)(2,1)}) custom-call(bf16[8,32]{1,0:T(8,128)(2,1)} %fusion.1.sel_ref, bf16[4,544,1024]{2,1,0:T(8,128)(2,1)} %pad_maximum_fusion.pay_ref, bf16[4,512,1024]{2,1,0:T(8,128)(2,1)} %pad_maximum_fusion.2.grad_ref), custom_call_target="tpu_custom_call" | custom-call | flops 18874368 | bytes 81920 | tf_op jit(solution)/shard_map/dispatch/pallas_call | solution.py:250
  171.0 11.0 %collective-permute-done.8 = bf16[512,1024]{1,0:T(8,128)(2,1)} collective-permute-done((bf16[512,1024]{1,0:T(8,128)(2,1)}, bf16[512,1024]{1,0:T(8,128)(2,1)}, u32[]{:S(2)}, u32[]{:S(2)}) %collective-permute-start.8) | collective-permute-done | bytes 1048608 | tf_op jit(solution)/shard_map/ppermute | solution.py:880
  192.0 10.8 %dispatch.5 = (bf16[4,2,4,144,1024]{4,3,2,1,0:T(8,128)(2,1)}, bf16[4,2,4,144,1024]{4,3,2,1,0:T(8,128)(2,1)}) custom-call(bf16[8,32]{1,0:T(8,128)(2,1)} %fusion.1.sel_ref, bf16[4,544,1024]{2,1,0:T(8,128)(2,1)} %collective-permute-done.10.pay_ref, ...), custom_call_target="tpu_custom_call", output_to_operand_aliasing={{0}: (3, {}), {1}: (4, {})} | custom-call | flops 18874368 | bytes 81920 | tf_op jit(solution)/shard_map/dispatch/pallas_call | solution.py:250
  202.9 34.7 %experts.4 = (bf16[2,1152,1024]{2,1,0:T(8,128)(2,1)}, bf16[2,1152,1024]{2,1,0:T(8,128)(2,1)}, f32[2,1152,1]{2,1,0:T(8,128)}, bf16[4,2,768,512]{3,2,1,0:T(8,128)(2,1)}) custom-call(bf16[4,1152,1024]{2,1,0:T(8,128)(2,1)} %bitcast.78, bf16[4,1152,1024]{2,1,0:T(8,128)(2,1)} %bitcast.80, bf16[4,2,768,512]{3,2,1,0:T(8,128)(2,1)} %bitcast.137), custom_call_target="tpu_custom_call" | custom-call | flops 84934656 | bytes 122880 | tf_op jit(solution)/shard_map/experts/pallas_call | solution.py:391
  253.7 10.8 %dispatch.6 = (bf16[4,2,4,144,1024]{4,3,2,1,0:T(8,128)(2,1)}, bf16[4,2,4,144,1024]{4,3,2,1,0:T(8,128)(2,1)}) custom-call(bf16[8,32]{1,0:T(8,128)(2,1)} %fusion.1.sel_ref, bf16[4,544,1024]{2,1,0:T(8,128)(2,1)} %pad_maximum_fusion.1.pay_ref, bf16[4,512,1024]{2,1,0:T(8,128)(2,1)} %pad_maximum_fusion.3.grad_ref), custom_call_target="tpu_custom_call" | custom-call | flops 18874368 | bytes 81920 | tf_op jit(solution)/shard_map/dispatch/pallas_call | solution.py:250
  264.5 35.2 %experts.5 = (bf16[2,1152,1024]{2,1,0:T(8,128)(2,1)}, bf16[2,1152,1024]{2,1,0:T(8,128)(2,1)}, f32[2,1152,1]{2,1,0:T(8,128)}, bf16[4,2,768,512]{3,2,1,0:T(8,128)(2,1)}) custom-call(bf16[4,1152,1024]{2,1,0:T(8,128)(2,1)} %bitcast.79, bf16[4,1152,1024]{2,1,0:T(8,128)(2,1)} %bitcast.81, bf16[4,2,768,512]{3,2,1,0:T(8,128)(2,1)} %bitcast.135), custom_call_target="tpu_custom_call" | custom-call | flops 84934656 | bytes 122880 | tf_op jit(solution)/shard_map/experts/pallas_call | solution.py:391
  315.7 9.5 %combine.10 = (bf16[528,1024]{1,0:T(8,128)(2,1)}, bf16[528,1024]{1,0:T(8,128)(2,1)}, bf16[528,1024]{1,0:T(8,128)(2,1)}, bf16[528,1024]{1,0:T(8,128)(2,1)}) custom-call(bf16[8,32]{1,0:T(8,128)(2,1)} %fusion.1.sel_ref, bf16[4,544,1024]{2,1,0:T(8,128)(2,1)} %pad_maximum_fusion.pay_ref, bf16[2,8,144,1024]{3,2,1,0:T(8,128)(2,1)} %bitcast.92, ...), custom_call_target="tpu_custom_call" | custom-call | flops 2415919104 | bytes 20971520 | tf_op jit(solution)/shard_map/combine/pallas_call | solution.py:491
  326.8 9.4 %combine.11 = (bf16[528,1024]{1,0:T(8,128)(2,1)}, bf16[528,1024]{1,0:T(8,128)(2,1)}, bf16[528,1024]{1,0:T(8,128)(2,1)}, bf16[528,1024]{1,0:T(8,128)(2,1)}) custom-call(bf16[8,32]{1,0:T(8,128)(2,1)} %fusion.1.sel_ref, bf16[4,544,1024]{2,1,0:T(8,128)(2,1)} %pad_maximum_fusion.pay_ref, bf16[2,8,144,1024]{3,2,1,0:T(8,128)(2,1)} %bitcast.93, ...), custom_call_target="tpu_custom_call" | custom-call | flops 2415919104 | bytes 20971520 | tf_op jit(solution)/shard_map/combine/pallas_call | solution.py:491
  336.3 11.0 %dispatch.7 = (bf16[4,2,4,144,1024]{4,3,2,1,0:T(8,128)(2,1)}, bf16[4,2,4,144,1024]{4,3,2,1,0:T(8,128)(2,1)}) custom-call(bf16[8,32]{1,0:T(8,128)(2,1)} %fusion.1.sel_ref, bf16[4,544,1024]{2,1,0:T(8,128)(2,1)} %collective-permute-done.16.pay_ref, ...), custom_call_target="tpu_custom_call", output_to_operand_aliasing={{0}: (3, {}), {1}: (4, {})} | custom-call | flops 18874368 | bytes 81920 | tf_op jit(solution)/shard_map/dispatch/pallas_call | solution.py:250
  347.3 35.7 %experts.6 = (bf16[2,1152,1024]{2,1,0:T(8,128)(2,1)}, bf16[2,1152,1024]{2,1,0:T(8,128)(2,1)}, f32[2,1152,1]{2,1,0:T(8,128)}, bf16[4,2,768,512]{3,2,1,0:T(8,128)(2,1)}) custom-call(bf16[4,1152,1024]{2,1,0:T(8,128)(2,1)} %bitcast.130, bf16[4,1152,1024]{2,1,0:T(8,128)(2,1)} %bitcast.132, bf16[4,2,768,512]{3,2,1,0:T(8,128)(2,1)} %bitcast.138, ...), custom_call_target="tpu_custom_call" | custom-call | flops 21743271936 | bytes 31457280 | tf_op jit(solution)/shard_map/experts/pallas_call | solution.py:391
  392.8 35.7 %experts.7 = (bf16[2,1152,1024]{2,1,0:T(8,128)(2,1)}, bf16[2,1152,1024]{2,1,0:T(8,128)(2,1)}, f32[2,1152,1]{2,1,0:T(8,128)}, bf16[4,2,768,512]{3,2,1,0:T(8,128)(2,1)}) custom-call(bf16[4,1152,1024]{2,1,0:T(8,128)(2,1)} %bitcast.131, bf16[4,1152,1024]{2,1,0:T(8,128)(2,1)} %bitcast.133, bf16[4,2,768,512]{3,2,1,0:T(8,128)(2,1)} %bitcast.136, ...), custom_call_target="tpu_custom_call" | custom-call | flops 21743271936 | bytes 31457280 | tf_op jit(solution)/shard_map/experts/pallas_call | solution.py:391
  428.5 7.6 %combine.12 = bf16[2,1056,1024]{2,1,0:T(8,128)(2,1)} custom-call(bf16[8,32]{1,0:T(8,128)(2,1)} %fusion.1.sel_ref, bf16[4,544,1024]{2,1,0:T(8,128)(2,1)} %collective-permute-done.16.pay_ref, bf16[2,8,144,1024]{3,2,1,0:T(8,128)(2,1)} %bitcast.82, bf16[2,8,144,1024]{3,2,1,0:T(8,128)(2,1)} %bitcast.98, bf16[2,8,144,1024]{3,2,1,0:T(8,128)(2,1)} %bitcast.86, ...), custom_call_target="tpu_custom_call" | custom-call | flops 2415919104 | bytes 20971520 | tf_op jit(solution)/shard_map/combine/pallas_call | solution.py:491
  438.7 7.6 %combine.13 = bf16[2,1056,1024]{2,1,0:T(8,128)(2,1)} custom-call(bf16[8,32]{1,0:T(8,128)(2,1)} %fusion.1.sel_ref, bf16[4,544,1024]{2,1,0:T(8,128)(2,1)} %collective-permute-done.16.pay_ref, bf16[2,8,144,1024]{3,2,1,0:T(8,128)(2,1)} %bitcast.83, bf16[2,8,144,1024]{3,2,1,0:T(8,128)(2,1)} %bitcast.99, bf16[2,8,144,1024]{3,2,1,0:T(8,128)(2,1)} %bitcast.87, ...), custom_call_target="tpu_custom_call" | custom-call | flops 2415919104 | bytes 20971520 | tf_op jit(solution)/shard_map/combine/pallas_call | solution.py:491
  446.3 9.4 %combine.14 = (bf16[528,1024]{1,0:T(8,128)(2,1)}, bf16[528,1024]{1,0:T(8,128)(2,1)}, bf16[528,1024]{1,0:T(8,128)(2,1)}, bf16[528,1024]{1,0:T(8,128)(2,1)}) custom-call(bf16[8,32]{1,0:T(8,128)(2,1)} %fusion.1.sel_ref, bf16[4,544,1024]{2,1,0:T(8,128)(2,1)} %pad_maximum_fusion.1.pay_ref, bf16[2,8,144,1024]{3,2,1,0:T(8,128)(2,1)} %bitcast.84, ...), custom_call_target="tpu_custom_call" | custom-call | flops 2415919104 | bytes 20971520 | tf_op jit(solution)/shard_map/combine/pallas_call | solution.py:491
  458.7 9.6 %combine.15 = (bf16[528,1024]{1,0:T(8,128)(2,1)}, bf16[528,1024]{1,0:T(8,128)(2,1)}, bf16[528,1024]{1,0:T(8,128)(2,1)}, bf16[528,1024]{1,0:T(8,128)(2,1)}) custom-call(bf16[8,32]{1,0:T(8,128)(2,1)} %fusion.1.sel_ref, bf16[4,544,1024]{2,1,0:T(8,128)(2,1)} %pad_maximum_fusion.1.pay_ref, bf16[2,8,144,1024]{3,2,1,0:T(8,128)(2,1)} %bitcast.85, ...), custom_call_target="tpu_custom_call" | custom-call | flops 2415919104 | bytes 20971520 | tf_op jit(solution)/shard_map/combine/pallas_call | solution.py:491
  469.4 37.3 %attention_backward.2 = (bf16[2,512,1024]{2,1,0:T(8,128)(2,1)}, f32[2,512,1024]{2,1,0:T(8,128)}, bf16[1024,3200]{1,0:T(8,128)(2,1)}) custom-call(bf16[512,1024]{1,0:T(8,128)(2,1)} %get-tuple-element.263.x_ref.refs_0_, bf16[1024,3200]{1,0:T(8,128)(2,1)} %gather_layer.1.w_ref.refs_1_, f32[1,1024]{1,0:T(1,128)} %bitcast.154, f32[1,1024]{1,0:T(1,128)} %bitcast.150, ...), custom_call_target="tpu_custom_call" | custom-call | flops 17179869184 | bytes 41943040 | tf_op jit(solution)/shard_map/attention_backward/pallas_call | solution.py:643
  512.2 23.6 %collective-permute-done.33.refs_21_ = bf16[528,1024]{1,0:T(8,128)(2,1)S(1)} collective-permute-done((bf16[528,1024]{1,0:T(8,128)(2,1)S(1)}, bf16[528,1024]{1,0:T(8,128)(2,1)S(1)}, u32[]{:S(2)}, u32[]{:S(2)}) %collective-permute-start.33) | collective-permute-done | bytes 1081376 | tf_op jit(solution)/shard_map/ppermute | solution.py:880
  537.7 39.2 %attention_backward.3 = (bf16[2,512,1024]{2,1,0:T(8,128)(2,1)}, f32[2,512,1024]{2,1,0:T(8,128)}, bf16[1024,3200]{1,0:T(8,128)(2,1)}) custom-call(bf16[512,1024]{1,0:T(8,128)(2,1)} %get-tuple-element.116.x_ref.refs_0_, bf16[1024,3200]{1,0:T(8,128)(2,1)} %gather_layer.1.w_ref.refs_1_, ...), custom_call_target="tpu_custom_call", output_to_operand_aliasing={{0}: (24, {}), {1}: (25, {})} | custom-call | flops 17179869184 | bytes 41943040 | tf_op jit(solution)/shard_map/attention_backward/pallas_call | solution.py:643
  576.9 66.6 %reduce_layer.1 = f32[32,3200]{1,0:T(8,128)} custom-call(bf16[1024,3200]{1,0:T(8,128)(2,1)} %get-tuple-element.211.pack_ref), custom_call_target="tpu_custom_call" | custom-call | bytes 1073741824 | tf_op jit(solution)/shard_map/reduce_layer/pallas_call | solution.py:857
  (156 shorter events, 115.3 us)
Async XLA Ops:
  7.2 195.7 %all-gather.5.cloned.1.call-start = ((), (), s32[]{:S(2)}) async-start(), calls=%async_computation.4 | async-start | bytes 7864320 | tf_op jit(solution)/shard_map/all_gather | solution.py:959
  11.2 253.2 %all-gather.7.cloned.1.call-start = ((), (), s32[]{:S(2)}) async-start(), calls=%async_computation.5 | async-start | bytes 7864320 | tf_op jit(solution)/shard_map/all_gather | solution.py:959
  64.7 48.8 %collective-permute-start.1 = (bf16[512,1024]{1,0:T(8,128)(2,1)}, bf16[512,1024]{1,0:T(8,128)(2,1)}, u32[]{:S(2)}, u32[]{:S(2)}) collective-permute-start(bf16[512,1024]{1,0:T(8,128)(2,1)} %get-tuple-element.115.refs_8_), channel_id=1, source_target_pairs={{0,16},{4,20},{8,24},{12,28},{16,0},{20,4},{24,8},{28,12},{1,17},{... | collective-permute-start | bytes 3145736 | tf_op jit(solution)/shard_map/ppermute | solution.py:880
  64.7 48.8 %collective-permute-start.2 = (bf16[512,1024]{1,0:T(8,128)(2,1)}, bf16[512,1024]{1,0:T(8,128)(2,1)}, u32[]{:S(2)}, u32[]{:S(2)}) collective-permute-start(bf16[512,1024]{1,0:T(8,128)(2,1)} %get-tuple-element.115.refs_8_), channel_id=1, source_target_pairs={{0,24},{4,28},{8,16},{12,20},{16,8},{20,12},{24,0},{28,4},{1,25},{... | collective-permute-start | bytes 3145736 | tf_op jit(solution)/shard_map/ppermute | solution.py:880
  67.4 582.1 %reduce-scatter.3.cloned.1.call-start = ((), (), s32[]{:S(2)}) async-start(), calls=%async_computation.2 | async-start | bytes 7864320 | tf_op jit(solution)/shard_map/reduce_scatter | solution.py:1080
  95.3 40.6 %collective-permute-start.3 = (bf16[544,1024]{1,0:T(8,128)(2,1)}, bf16[544,1024]{1,0:T(8,128)(2,1)}, u32[]{:S(2)}, u32[]{:S(2)}) collective-permute-start(bf16[544,1024]{1,0:T(8,128)(2,1)} %get-tuple-element.126.refs_15_), channel_id=1, source_target_pairs={{0,8},{4,12},{8,0},{12,4},{16,24},{20,28},{24,16},{28,20},{1,9},{5... | collective-permute-start | bytes 3342344 | tf_op jit(solution)/shard_map/ppermute | solution.py:880
  96.2 40.9 %collective-permute-start.5 = (bf16[544,1024]{1,0:T(8,128)(2,1)}, bf16[544,1024]{1,0:T(8,128)(2,1)}, u32[]{:S(2)}, u32[]{:S(2)}) collective-permute-start(bf16[544,1024]{1,0:T(8,128)(2,1)} %get-tuple-element.126.refs_15_), channel_id=1, source_target_pairs={{0,16},{4,20},{8,24},{12,28},{16,0},{20,4},{24,8},{28,12},{1,17},{... | collective-permute-start | bytes 3342344 | tf_op jit(solution)/shard_map/ppermute | solution.py:880
  156.2 34.9 %collective-permute-start.10 = (bf16[4,544,1024]{2,1,0:T(8,128)(2,1)}, bf16[4,544,1024]{2,1,0:T(8,128)(2,1)}, u32[]{:S(2)}, u32[]{:S(2)}) collective-permute-start(bf16[4,544,1024]{2,1,0:T(8,128)(2,1)} %pad_maximum_fusion.pay_ref), channel_id=1, source_target_pairs={{0,4},{4,0},{8,12},{12,8},{16,20},{20,16},{24,28},{28,24},{1,5},{5... | collective-permute-start | bytes 13369352 | tf_op jit(solution)/shard_map/ppermute | solution.py:880
  183.5 66.4 %collective-permute-start.9 = (bf16[544,1024]{1,0:T(8,128)(2,1)}, bf16[544,1024]{1,0:T(8,128)(2,1)}, u32[]{:S(2)}, u32[]{:S(2)}) collective-permute-start(bf16[544,1024]{1,0:T(8,128)(2,1)} %get-tuple-element.137.refs_15_), channel_id=1, source_target_pairs={{0,8},{4,12},{8,0},{12,4},{16,24},{20,28},{24,16},{28,20},{1,9},{5... | collective-permute-start | bytes 3342344 | tf_op jit(solution)/shard_map/ppermute | solution.py:880
  184.4 65.5 %collective-permute-start.14 = (bf16[544,1024]{1,0:T(8,128)(2,1)}, bf16[544,1024]{1,0:T(8,128)(2,1)}, u32[]{:S(2)}, u32[]{:S(2)}) collective-permute-start(bf16[544,1024]{1,0:T(8,128)(2,1)} %get-tuple-element.137.refs_15_), channel_id=1, source_target_pairs={{0,16},{4,20},{8,24},{12,28},{16,0},{20,4},{24,8},{28,12},{1,17},{... | collective-permute-start | bytes 3342344 | tf_op jit(solution)/shard_map/ppermute | solution.py:880
  184.8 65.2 %collective-permute-start.15 = (bf16[544,1024]{1,0:T(8,128)(2,1)}, bf16[544,1024]{1,0:T(8,128)(2,1)}, u32[]{:S(2)}, u32[]{:S(2)}) collective-permute-start(bf16[544,1024]{1,0:T(8,128)(2,1)} %get-tuple-element.137.refs_15_), channel_id=1, source_target_pairs={{0,24},{4,28},{8,16},{12,20},{16,8},{20,12},{24,0},{28,4},{1,25},{... | collective-permute-start | bytes 3342344 | tf_op jit(solution)/shard_map/ppermute | solution.py:880
  188.9 56.0 %collective-permute-start.12 = (bf16[256,1024]{1,0:T(8,128)(2,1)}, bf16[256,1024]{1,0:T(8,128)(2,1)}, u32[]{:S(2)}, u32[]{:S(2)}) collective-permute-start(bf16[256,1024]{1,0:T(8,128)(2,1)} %slice.97), channel_id=1, source_target_pairs={{0,16},{4,20},{8,24},{12,28},{16,0},{20,4},{24,8},{28,12},{1,17},{... | collective-permute-start | bytes 1572872 | tf_op jit(solution)/shard_map/ppermute | solution.py:880
  191.0 53.9 %collective-permute-start.13 = (bf16[256,1024]{1,0:T(8,128)(2,1)}, bf16[256,1024]{1,0:T(8,128)(2,1)}, u32[]{:S(2)}, u32[]{:S(2)}) collective-permute-start(bf16[256,1024]{1,0:T(8,128)(2,1)} %slice.98), channel_id=1, source_target_pairs={{0,8},{4,12},{8,0},{12,4},{16,24},{20,28},{24,16},{28,20},{1,9},{5... | collective-permute-start | bytes 1572872 | tf_op jit(solution)/shard_map/ppermute | solution.py:880
  325.2 57.7 %collective-permute-start.21 = (bf16[528,1024]{1,0:T(8,128)(2,1)}, bf16[528,1024]{1,0:T(8,128)(2,1)}, u32[]{:S(2)}, u32[]{:S(2)}) collective-permute-start(bf16[528,1024]{1,0:T(8,128)(2,1)} %get-tuple-element.173), channel_id=1, source_target_pairs={{0,8},{4,12},{8,0},{12,4},{16,24},{20,28},{24,16},{28,20},{1,9},{5... | collective-permute-start | bytes 3244040 | tf_op jit(solution)/shard_map/ppermute | solution.py:880
  326.2 59.7 %collective-permute-start.20 = (bf16[528,1024]{1,0:T(8,128)(2,1)}, bf16[528,1024]{1,0:T(8,128)(2,1)}, u32[]{:S(2)}, u32[]{:S(2)}) collective-permute-start(bf16[528,1024]{1,0:T(8,128)(2,1)} %get-tuple-element.162), channel_id=1, source_target_pairs={{0,16},{4,20},{8,24},{12,28},{16,0},{20,4},{24,8},{28,12},{1,17},{... | collective-permute-start | bytes 3244040 | tf_op jit(solution)/shard_map/ppermute | solution.py:880
  388.6 260.8 %reduce-scatter.5.cloned.1.call-start = ((), (), s32[]{:S(2)}) async-start(), calls=%async_computation.3 | async-start | bytes 7864320 | tf_op jit(solution)/shard_map/reduce_scatter | solution.py:1080
  388.7 50.0 %collective-permute-start.23 = (bf16[528,1024]{1,0:T(8,128)(2,1)}, bf16[528,1024]{1,0:T(8,128)(2,1)}, u32[]{:S(2)}, u32[]{:S(2)}) collective-permute-start(bf16[528,1024]{1,0:T(8,128)(2,1)} %add_convert_fusion.2), channel_id=1, source_target_pairs={{0,16},{4,20},{8,24},{12,28},{16,0},{20,4},{24,8},{28,12},{1,17},{... | collective-permute-start | bytes 3244040 | tf_op jit(solution)/shard_map/ppermute | solution.py:880
  390.2 48.5 %collective-permute-start.22 = (bf16[528,1024]{1,0:T(8,128)(2,1)}, bf16[528,1024]{1,0:T(8,128)(2,1)}, u32[]{:S(2)}, u32[]{:S(2)}) collective-permute-start(bf16[528,1024]{1,0:T(8,128)(2,1)} %add_convert_fusion.3), channel_id=1, source_target_pairs={{0,8},{4,12},{8,0},{12,4},{16,24},{20,28},{24,16},{28,20},{1,9},{5... | collective-permute-start | bytes 3244040 | tf_op jit(solution)/shard_map/ppermute | solution.py:880
  391.2 46.4 %collective-permute-start.25 = (bf16[528,1024]{1,0:T(8,128)(2,1)}, bf16[528,1024]{1,0:T(8,128)(2,1)}, u32[]{:S(2)}, u32[]{:S(2)}) collective-permute-start(bf16[528,1024]{1,0:T(8,128)(2,1)} %get-tuple-element.184), channel_id=1, source_target_pairs={{0,16},{4,20},{8,24},{12,28},{16,0},{20,4},{24,8},{28,12},{1,17},{... | collective-permute-start | bytes 3244040 | tf_op jit(solution)/shard_map/ppermute | solution.py:880
  391.7 47.0 %collective-permute-start.24 = (bf16[528,1024]{1,0:T(8,128)(2,1)}, bf16[528,1024]{1,0:T(8,128)(2,1)}, u32[]{:S(2)}, u32[]{:S(2)}) collective-permute-start(bf16[528,1024]{1,0:T(8,128)(2,1)} %get-tuple-element.182), channel_id=1, source_target_pairs={{0,8},{4,12},{8,0},{12,4},{16,24},{20,28},{24,16},{28,20},{1,9},{5... | collective-permute-start | bytes 3244040 | tf_op jit(solution)/shard_map/ppermute | solution.py:880
  455.7 51.0 %collective-permute-start.31 = (bf16[528,1024]{1,0:T(8,128)(2,1)}, bf16[528,1024]{1,0:T(8,128)(2,1)}, u32[]{:S(2)}, u32[]{:S(2)}) collective-permute-start(bf16[528,1024]{1,0:T(8,128)(2,1)} %get-tuple-element.204), channel_id=1, source_target_pairs={{0,8},{4,12},{8,0},{12,4},{16,24},{20,28},{24,16},{28,20},{1,9},{5... | collective-permute-start | bytes 3244040 | tf_op jit(solution)/shard_map/ppermute | solution.py:880
  456.7 50.1 %collective-permute-start.32 = (bf16[528,1024]{1,0:T(8,128)(2,1)}, bf16[528,1024]{1,0:T(8,128)(2,1)}, u32[]{:S(2)}, u32[]{:S(2)}) collective-permute-start(bf16[528,1024]{1,0:T(8,128)(2,1)} %get-tuple-element.205), channel_id=1, source_target_pairs={{0,16},{4,20},{8,24},{12,28},{16,0},{20,4},{24,8},{28,12},{1,17},{... | collective-permute-start | bytes 3244040 | tf_op jit(solution)/shard_map/ppermute | solution.py:880
  457.3 51.6 %collective-permute-start.29 = (bf16[528,1024]{1,0:T(8,128)(2,1)}, bf16[528,1024]{1,0:T(8,128)(2,1)}, u32[]{:S(2)}, u32[]{:S(2)}) collective-permute-start(bf16[528,1024]{1,0:T(8,128)(2,1)} %get-tuple-element.193), channel_id=1, source_target_pairs={{0,16},{4,20},{8,24},{12,28},{16,0},{20,4},{24,8},{28,12},{1,17},{... | collective-permute-start | bytes 3244040 | tf_op jit(solution)/shard_map/ppermute | solution.py:880
  468.3 40.5 %collective-permute-start.28 = (bf16[528,1024]{1,0:T(8,128)(2,1)}, bf16[528,1024]{1,0:T(8,128)(2,1)}, u32[]{:S(2)}, u32[]{:S(2)}) collective-permute-start(bf16[528,1024]{1,0:T(8,128)(2,1)} %get-tuple-element.191), channel_id=1, source_target_pairs={{0,8},{4,12},{8,0},{12,4},{16,24},{20,28},{24,16},{28,20},{1,9},{5... | collective-permute-start | bytes 3244040 | tf_op jit(solution)/shard_map/ppermute | solution.py:880
  (33 other events, 389.5 us)
Sparse Core Ops, SparseCore 0:
  11.4 127.4 all-gather.4
  141.0 114.5 all-gather.6
  388.8 116.7 reduce-scatter.2
  510.7 126.5 reduce-scatter.4
